TPU v7x, 256 devices: a whole 4x4x8 slice. The times are simulated.
256 devices in a mesh: pts: 64 (over z, x, core), rhs: 4 (over y).
Axes of the slice: x: 4, y: 4, z: 8, core: 2. Of those that a mesh axis runs over, the one named last changes fastest.
Arguments:
- points: bfloat16 [131072, 32], P('pts'), may hold values from -0.5 to 0.5
- noise_var: float32 [131072], P('pts'), may hold values from 0.5 to 0.6
- right_side: float32 [64, 131072], P('rhs', 'pts'), may hold values from -12 to 12
- pattern: int32 [1024, 33], P('pts'), may hold values from 0 to 1, as said below
Outputs:
- solution: float32 [64, 131072], P('rhs', 'pts')
- residual: float32 [64, 131072], P('rhs', 'pts')
- res_image: float32 [64, 131072], P('rhs', 'pts')
Inputs may be any that keep to these rules, and one draw needn't show every extreme that they name: Symmetric: pattern[b, 16 + d] = pattern[b + d, 16 - d]; the centre column is 1; entries naming a block outside 0 to 1023 are 0.
All inputs are finite; a program needn't handle non-finite values.
Results may differ from a plain program's by a relative error of at most 0.0036.
Values may be sent and summed in bfloat16 or wider, within the bound.
A program may use at most 64 MiB of HBM per device.

v0:
```python
import jax
import jax.numpy as jnp
from jax import lax
from jax.sharding import PartitionSpec as P

F = 32
BLK = 128
REACH = 16
ITERS = 2
WIDE = 33
WEXP = 18


group_tiles = 64


def with_halo(cells, sides, width):
    for axis, dim in sides:
        count = lax.axis_size(axis)
        ends = count - 1
        head = lax.slice_in_dim(cells, 0, width, axis=dim)
        tail = lax.slice_in_dim(cells, cells.shape[dim] - width, cells.shape[dim], axis=dim)
        cells = jnp.concatenate(
            [
                lax.ppermute(tail, axis, [(i, (i + 1) % count) for i in range(ends)]),
                cells,
                lax.ppermute(head, axis, [((i + 1) % count, i) for i in range(ends)]),
            ],
            axis=dim,
        )
    return cells


def kernel_block(left_points, right_points, left_squares, right_squares):
    cross_terms = jnp.einsum(
        "gif,gjf->gij", left_points, right_points, preferred_element_type=jnp.float32
    )
    dist_squared = jnp.maximum(
        left_squares[:, :, None] + right_squares[:, None, :] - 2.0 * cross_terms, 0.0
    )
    radius = jnp.sqrt(dist_squared)
    return jnp.maximum(1.0 - radius, 0.0) ** WEXP * (WEXP * radius + 1.0)


def per_device(points, noise_var, right_side, pattern):
    local_rows = points.shape[0]
    block_count = local_rows // BLK
    rim_rows = REACH * BLK
    kernel_scale = 1.0 / (4 * BLK)
    wide_points = with_halo(points, (("pts", 0),), rim_rows)
    wide_squares = jnp.sum(jnp.square(wide_points.astype(jnp.float32)), axis=1)
    point_blocks = wide_points.reshape(-1, BLK, F)
    square_blocks = wide_squares.reshape(-1, BLK)
    flat_mask = pattern.reshape(-1)
    live_count = jnp.sum(flat_mask)
    slot_order = jnp.argsort(1 - flat_mask, stable=True)
    my_slots = slot_order
    slot_len = -(-my_slots.shape[0] // group_tiles) * group_tiles
    my_slots = jnp.pad(my_slots, (0, slot_len - my_slots.shape[0]))

    def accumulate(wide_vec):
        width = wide_vec.shape[0]
        vec_blocks = wide_vec.reshape(width, -1, BLK)

        def turn(turn_index, running):
            first_slot = turn_index * group_tiles
            slot_ids = lax.dynamic_slice_in_dim(my_slots, first_slot, group_tiles)
            valid_mask = first_slot + jnp.arange(group_tiles, dtype=jnp.int32) < live_count
            home_block = slot_ids // WIDE
            other_block = home_block + slot_ids % WIDE
            profile = kernel_block(
                point_blocks[home_block + REACH],
                point_blocks[other_block],
                square_blocks[home_block + REACH],
                square_blocks[other_block],
            )
            weights = (profile * valid_mask.astype(jnp.float32)[:, None, None]).astype(jnp.bfloat16)
            contribution = jnp.einsum(
                "gij,cgj->cgi",
                weights,
                vec_blocks[:, other_block],
                preferred_element_type=jnp.float32,
            )
            return running.at[:, home_block].add(contribution)

        turns = (live_count + group_tiles - 1) // group_tiles
        summed = lax.fori_loop(0, turns, turn, jnp.zeros((width, block_count, BLK), jnp.float32))
        return summed.reshape(width, local_rows)

    def apply_operator(vector):
        vec_low = vector.astype(jnp.bfloat16)
        wide_vec = with_halo(vec_low, (("pts", 1),), rim_rows)
        image_part = accumulate(wide_vec)
        return noise_var[None, :] * vector + kernel_scale * image_part

    solution = jnp.zeros_like(right_side)
    residual = right_side
    res_image = apply_operator(residual)
    direction = jnp.zeros_like(right_side)
    dir_image = jnp.zeros_like(right_side)
    dir_twice = jnp.zeros_like(right_side)
    norm_prev = None
    step_prev = None
    for iteration in range(ITERS):
        norm_flat, curv_flat = lax.psum(
            (jnp.sum(residual * residual, axis=1), jnp.sum(res_image * residual, axis=1)), "pts"
        )
        norm_now = norm_flat[:, None]
        curvature = curv_flat[:, None]
        square_image = apply_operator(res_image)
        if iteration == 0:
            step_len = norm_now / curvature
            direction = residual
            dir_image = res_image
            dir_twice = square_image
        else:
            mix_ratio = norm_now / norm_prev
            step_len = norm_now / (curvature - mix_ratio * norm_now / step_prev)
            direction = residual + mix_ratio * direction
            dir_image = res_image + mix_ratio * dir_image
            dir_twice = square_image + mix_ratio * dir_twice
        solution = solution + step_len * direction
        residual = residual - step_len * dir_image
        res_image = res_image - step_len * dir_twice
        norm_prev = norm_now
        step_prev = step_len
    return (solution, residual, res_image)


def solution(mesh):
    placed = (P("pts", None), P("pts"), P("rhs", "pts"), P("pts", None))
    return jax.shard_map(
        per_device,
        mesh=mesh,
        in_specs=placed,
        out_specs=(P("rhs", "pts"), P("rhs", "pts"), P("rhs", "pts")),
        check_vma=False,
    )
```

profile of v0, /device:TPU:232, one launch (start us, length us, event | category | flops | bytes accessed | tf_op | source)
XLA Modules:
  0.0 576.2 jit_solution(11921343937707853893)
XLA Ops:
  1.5 4.5 collective-permute-start.1
  9.9 5.8 collective-permute-start.3
  17.8 4.4 sort.17
  24.2 108.5 %while.36 = (s32[]{:T(128)}, f32[16,16,128]{2,0,1:T(8,128)S(1)}, s32[]{:T(128)}, s32[576]{0:T(1024)S(1)}, bf16[16,48,128]{2,0,1:T(8,128)(2,1)S(1)}, /*index=5*/f...) while((s32[]{:T(128)}, f32[16,16,128]{2,0,1:T(8,128)S(1)}, ...), condition=%wide.region_7.8_spmd, body=%wide.region_5.7_spmd.sunk | while | flops 117575240 | bytes 6238391 | solution.py:87
  24.4 2.2 gather_fusion
  31.1 5.6 fusion.47
  36.7 3.0 scatter_fusion
  39.9 2.2 gather_fusion
  46.6 5.6 fusion.47
  52.2 3.0 scatter_fusion
  62.1 5.6 fusion.47
  67.7 3.0 scatter_fusion
  70.9 2.2 gather_fusion
  77.6 5.6 fusion.47
  83.2 3.0 scatter_fusion
  86.4 2.2 gather_fusion
  93.2 5.6 fusion.47
  98.7 3.0 scatter_fusion
  101.9 2.2 gather_fusion
  108.7 5.6 fusion.47
  114.2 3.0 scatter_fusion
  124.2 5.6 fusion.47
  129.7 3.0 scatter_fusion
  134.7 2.4 collective-permute-start.4
  137.3 108.0 %all-reduce.2 = (f32[16]{0:T(128)S(1)}, f32[16]{0:T(128)S(1)}) all-reduce(f32[16]{0:T(128)S(1)} %get-tuple-element.375, f32[16]{0:T(128)S(1)} %get-tuple-element.374), channel_id=1, replica_groups=mesh['pts'=64,'rhs'=4] {'pts'}, use_global_device_ids=true, to_apply=%region_1.0 | all-reduce | flops 32 | bytes 256 | tf_op jit(solution)/shard_map/psum | solution.py:105
  245.4 108.5 %while.37 = (s32[]{:T(128)}, f32[16,16,128]{2,0,1:T(8,128)S(1)}, s32[]{:T(128)}, s32[576]{0:T(1024)S(1)}, bf16[16,48,128]{2,0,1:T(8,128)(2,1)S(1)}, /*index=5*/f...) while((s32[]{:T(128)}, f32[16,16,128]{2,0,1:T(8,128)S(1)}, ...), condition=%wide.region_14.15_spmd, body=%wide.region_12.14_spmd.sunk | while | flops 117575240 | bytes 6238391 | solution.py:87
  245.5 2.2 gather_fusion.5
  252.3 5.6 fusion.51
  257.9 3.0 scatter_fusion.1
  267.8 5.6 fusion.51
  273.4 3.0 scatter_fusion.1
  283.3 5.6 fusion.51
  288.9 3.0 scatter_fusion.1
  298.8 5.6 fusion.51
  304.4 3.0 scatter_fusion.1
  314.3 5.6 fusion.51
  319.9 3.0 scatter_fusion.1
  323.1 2.2 gather_fusion.5
  329.8 5.6 fusion.51
  335.4 3.0 scatter_fusion.1
  338.6 2.2 gather_fusion.5
  345.3 5.6 fusion.51
  350.9 3.0 scatter_fusion.1
  356.1 2.4 collective-permute-start.6
  358.5 108.0 %all-reduce.1 = (f32[16]{0:T(128)S(1)}, f32[16]{0:T(128)S(1)}) all-reduce(f32[16]{0:T(128)S(1)} %get-tuple-element.373, f32[16]{0:T(128)S(1)} %get-tuple-element.372), channel_id=1, replica_groups=mesh['pts'=64,'rhs'=4] {'pts'}, use_global_device_ids=true, to_apply=%region_11.12 | all-reduce | flops 32 | bytes 256 | tf_op jit(solution)/shard_map/psum | solution.py:105
  466.6 108.7 %while.38 = (s32[]{:T(128)}, f32[16,16,128]{2,0,1:T(8,128)S(1)}, s32[]{:T(128)}, s32[576]{0:T(1024)S(1)}, bf16[16,48,128]{2,0,1:T(8,128)(2,1)S(1)}, /*index=5*/f...) while((s32[]{:T(128)}, f32[16,16,128]{2,0,1:T(8,128)S(1)}, ...), condition=%wide.region_19.20_spmd, body=%wide.region_17.19_spmd.sunk | while | flops 117575240 | bytes 6238391 | solution.py:87
  466.9 2.2 gather_fusion.10
  473.7 5.6 fusion.55
  479.3 3.0 scatter_fusion.2
  482.4 2.2 gather_fusion.10
  489.2 5.6 fusion.55
  494.8 3.0 scatter_fusion.2
  498.0 2.2 gather_fusion.10
  504.7 5.6 fusion.55
  510.3 3.0 scatter_fusion.2
  513.5 2.2 gather_fusion.10
  520.2 5.6 fusion.55
  525.8 3.0 scatter_fusion.2
  535.7 5.6 fusion.55
  541.3 3.0 scatter_fusion.2
  551.2 5.6 fusion.55
  556.8 3.0 scatter_fusion.2
  566.7 5.6 fusion.55
  572.3 3.0 scatter_fusion.2
  (236 shorter events, 131.3 us)
Async XLA Ops:
  1.5 20.7 %collective-permute-start.1 = (bf16[16,2048]{1,0:T(8,128)(2,1)S(1)}, bf16[16,2048]{1,0:T(8,128)(2,1)S(1)}, u32[]{:S(2)}, u32[]{:S(2)}) collective-permute-start(bf16[16,2048]{1,0:T(8,128)(2,1)S(1)} %convert_element_type.60), channel_id=1, source_target_pairs={{4,0},{8,4},{12,8},{16,12},{20,16},{24,20},{28,24},{32,28},{36,32}... | collective-permute-start | bytes 196616 | tf_op jit(solution)/shard_map/ppermute | solution.py:27
  6.1 16.1 %collective-permute-start = (bf16[16,2048]{1,0:T(8,128)(2,1)S(1)}, bf16[16,2048]{1,0:T(8,128)(2,1)S(1)}, u32[]{:S(2)}, u32[]{:S(2)}) collective-permute-start(bf16[16,2048]{1,0:T(8,128)(2,1)S(1)} %convert_element_type.60), channel_id=1, source_target_pairs={{0,4},{4,8},{8,12},{12,16},{16,20},{20,24},{24,28},{28,32},{32,36}... | collective-permute-start | bytes 196616 | tf_op jit(solution)/shard_map/ppermute | solution.py:25
  8.0 14.2 %collective-permute-start.2 = (bf16[2048,32]{0,1:T(8,128)(2,1)}, bf16[2048,32]{0,1:T(8,128)(2,1)S(1)}, u32[]{:S(2)}, u32[]{:S(2)}) collective-permute-start(bf16[2048,32]{0,1:T(8,128)(2,1)} %param.10), channel_id=1, source_target_pairs={{0,4},{4,8},{8,12},{12,16},{16,20},{20,24},{24,28},{28,32},{32,36}... | collective-permute-start | bytes 393224 | tf_op jit(solution)/shard_map/ppermute | solution.py:25
  9.9 13.2 %collective-permute-start.3 = (bf16[2048,32]{0,1:T(8,128)(2,1)}, bf16[2048,32]{0,1:T(8,128)(2,1)S(1)}, u32[]{:S(2)}, u32[]{:S(2)}) collective-permute-start(bf16[2048,32]{0,1:T(8,128)(2,1)} %param.10), channel_id=1, source_target_pairs={{4,0},{8,4},{12,8},{16,12},{20,16},{24,20},{28,24},{32,28},{36,32}... | collective-permute-start | bytes 393224 | tf_op jit(solution)/shard_map/ppermute | solution.py:27
  24.2 108.6 %copy-start = (f32[16,2048]{1,0:T(8,128)S(1)}, f32[16,2048]{1,0:T(8,128)}, u32[]{:S(2)}) copy-start(f32[16,2048]{1,0:T(8,128)} %param.12) | copy-start | bytes 393220
  24.2 108.6 %copy-start.1 = (f32[2048]{0:T(1024)S(1)}, f32[2048]{0:T(1024)}, u32[]{:S(2)}) copy-start(f32[2048]{0:T(1024)} %param.11) | copy-start | bytes 24580
  132.8 112.5 %collective-permute-start.5 = (bf16[16,2048]{1,0:T(8,128)(2,1)S(1)}, bf16[16,2048]{1,0:T(8,128)(2,1)S(1)}, u32[]{:S(2)}, u32[]{:S(2)}) collective-permute-start(bf16[16,2048]{1,0:T(8,128)(2,1)S(1)} %get-tuple-element.436), channel_id=1, source_target_pairs={{4,0},{8,4},{12,8},{16,12},{20,16},{24,20},{28,24},{32,28},{36,32}... | collective-permute-start | bytes 196616 | tf_op jit(solution)/shard_map/ppermute | solution.py:27
  134.7 110.6 %collective-permute-start.4 = (bf16[16,2048]{1,0:T(8,128)(2,1)S(1)}, bf16[16,2048]{1,0:T(8,128)(2,1)S(1)}, u32[]{:S(2)}, u32[]{:S(2)}) collective-permute-start(bf16[16,2048]{1,0:T(8,128)(2,1)S(1)} %get-tuple-element.436), channel_id=1, source_target_pairs={{0,4},{4,8},{8,12},{12,16},{16,20},{20,24},{24,28},{28,32},{32,36}... | collective-permute-start | bytes 196616 | tf_op jit(solution)/shard_map/ppermute | solution.py:25
  354.2 112.4 %collective-permute-start.7 = (bf16[16,2048]{1,0:T(8,128)(2,1)S(1)}, bf16[16,2048]{1,0:T(8,128)(2,1)S(1)}, u32[]{:S(2)}, u32[]{:S(2)}) collective-permute-start(bf16[16,2048]{1,0:T(8,128)(2,1)S(1)} %get-tuple-element.446), channel_id=1, source_target_pairs={{4,0},{8,4},{12,8},{16,12},{20,16},{24,20},{28,24},{32,28},{36,32}... | collective-permute-start | bytes 196616 | tf_op jit(solution)/shard_map/ppermute | solution.py:27
  356.1 110.5 %collective-permute-start.6 = (bf16[16,2048]{1,0:T(8,128)(2,1)S(1)}, bf16[16,2048]{1,0:T(8,128)(2,1)S(1)}, u32[]{:S(2)}, u32[]{:S(2)}) collective-permute-start(bf16[16,2048]{1,0:T(8,128)(2,1)S(1)} %get-tuple-element.446), channel_id=1, source_target_pairs={{0,4},{4,8},{8,12},{12,16},{16,20},{20,24},{24,28},{28,32},{32,36}... | collective-permute-start | bytes 196616 | tf_op jit(solution)/shard_map/ppermute | solution.py:25
where the time goes:
time: 577 us; the launch traced here: 576 us
  blocking collectives  216 us (37%)
  local copies, waits for them, and re-layouts  130 us (23%)
  matrix products  117 us (20%)
  other arithmetic  87.8 us (15%)
  starting transfers between devices  22.8 us (4%)
    psum x2, blocking collectives, per_device(): lax.psum((jnp.sum(residual * residual, axis=1), jnp.sum(res_image * resid...  216 us
    dot_general x21, matrix products, turn(): jnp.einsum('gij,cgj->cgi', weights, vec_blocks[:, other_block], preferred...  117 us
    scatter-add x21, other arithmetic, turn(): return running.at[:, home_block].add(contribution)  63.8 us
    gather x21, local copies, waits for them, and re-layouts, turn(): point_blocks[home_block + REACH]  45.5 us
    gather x21, local copies, waits for them, and re-layouts, turn(): point_blocks[other_block]  44.3 us
    ppermute x4, starting transfers between devices, with_halo(): lax.ppermute(head, axis, [((i + 1) % count, i) for i in range(ends)])  14.1 us
    convert_element_type x21, other arithmetic, turn(): valid_mask.astype(jnp.float32)[:, None, None]  13.6 us
    gather x21, local copies, waits for them, and re-layouts, turn(): vec_blocks[:, other_block]  13.3 us
  transfers between devices with their start and end apart: 8, of which 0 were waited for; matrix products, arithmetic and copies ran while one was open for 1% of the time, Pallas kernels for 0%

commit v1 on v0

v1 whole, which is shorter than its diff:
```python
import functools

import jax
import jax.numpy as jnp
from jax import lax
from jax.experimental import pallas as pl
from jax.experimental.pallas import tpu as pltpu
from jax.sharding import PartitionSpec as P

F = 32
BLK = 128
REACH = 16
ITERS = 2
WIDE = 33
WEXP = 18


def with_halo(cells, axis, dim, width):
    count = lax.axis_size(axis)
    ends = count - 1
    head = lax.slice_in_dim(cells, 0, width, axis=dim)
    tail = lax.slice_in_dim(cells, cells.shape[dim] - width, cells.shape[dim], axis=dim)
    return jnp.concatenate(
        [
            lax.ppermute(tail, axis, [(i, (i + 1) % count) for i in range(ends)]),
            cells,
            lax.ppermute(head, axis, [((i + 1) % count, i) for i in range(ends)]),
        ],
        axis=dim,
    )


def profile_tile(left, right_t, pat):
    left_f = left.astype(jnp.float32)
    right_f = right_t.astype(jnp.float32)
    sq_left = jnp.sum(left_f * left_f, axis=1, keepdims=True)
    sq_right = jnp.sum(right_f * right_f, axis=0, keepdims=True)
    cross = jnp.dot(left, right_t, preferred_element_type=jnp.float32)
    dist = jnp.maximum(sq_left + sq_right - 2.0 * cross, 0.0)
    radius = jnp.sqrt(dist)
    base = jnp.maximum(1.0 - radius, 0.0)
    b2 = base * base
    b4 = b2 * b2
    b8 = b4 * b4
    b16 = b8 * b8
    value = (b16 * b2) * (WEXP * radius + 1.0)
    return (value * pat).astype(jnp.bfloat16)


def build_kernel(pat_ref, pw_ref, pwt_ref, k_ref):
    a = pl.program_id(0)
    start = pl.multiple_of((a + REACH) * BLK, BLK)
    left = pw_ref[pl.ds(start, BLK), :]

    def body(o, carry):
        col = pl.multiple_of((a + o) * BLK, BLK)
        right_t = pwt_ref[:, pl.ds(col, BLK)]
        pat = pat_ref[a * WIDE + o].astype(jnp.float32)
        k_ref[0, :, pl.ds(pl.multiple_of(o * BLK, BLK), BLK)] = profile_tile(left, right_t, pat)
        return carry

    lax.fori_loop(0, WIDE, body, 0)


def apply_kernel(v_ref, k_ref, out_ref):
    a = pl.program_id(0)
    start = pl.multiple_of(a * BLK, BLK)
    v_cat = v_ref[:, pl.ds(start, WIDE * BLK)]
    out_ref[...] = lax.dot_general(
        v_cat, k_ref[0], (((1,), (1,)), ((), ())), preferred_element_type=jnp.float32
    )


def build_k(pattern_flat, wide_points, wide_points_t, blocks):
    wide_rows = wide_points.shape[0]
    return pl.pallas_call(
        build_kernel,
        out_shape=jax.ShapeDtypeStruct((blocks, BLK, WIDE * BLK), jnp.bfloat16),
        grid_spec=pltpu.PrefetchScalarGridSpec(
            num_scalar_prefetch=1,
            grid=(blocks,),
            in_specs=[
                pl.BlockSpec((wide_rows, F), lambda a, p: (0, 0)),
                pl.BlockSpec((F, wide_rows), lambda a, p: (0, 0)),
            ],
            out_specs=pl.BlockSpec((1, BLK, WIDE * BLK), lambda a, p: (a, 0, 0)),
        ),
        compiler_params=pltpu.CompilerParams(dimension_semantics=("arbitrary",)),
    )(pattern_flat, wide_points, wide_points_t)


def apply_k(wide_vec, kmat):
    rows, wide_cols = wide_vec.shape
    blocks = kmat.shape[0]
    return pl.pallas_call(
        apply_kernel,
        out_shape=jax.ShapeDtypeStruct((rows, blocks * BLK), jnp.float32),
        grid=(blocks,),
        in_specs=[
            pl.BlockSpec((rows, wide_cols), lambda a: (0, 0)),
            pl.BlockSpec((1, BLK, WIDE * BLK), lambda a: (a, 0, 0)),
        ],
        out_specs=pl.BlockSpec((rows, BLK), lambda a: (0, a)),
        compiler_params=pltpu.CompilerParams(dimension_semantics=("arbitrary",)),
    )(wide_vec, kmat)


def per_device(points, noise_var, right_side, pattern):
    local_rows = points.shape[0]
    block_count = local_rows // BLK
    rim_rows = REACH * BLK
    kernel_scale = 1.0 / (4 * BLK)
    wide_points = with_halo(points, "pts", 0, rim_rows)
    kmat = build_k(pattern.reshape(-1), wide_points, wide_points.T, block_count)

    rhs_count = lax.axis_size("rhs")
    rhs_index = lax.axis_index("rhs")

    def total(parts):
        slots = jnp.zeros((rhs_count,) + parts.shape, parts.dtype)
        slots = lax.dynamic_update_index_in_dim(slots, parts, rhs_index, 0)
        summed = lax.psum(slots, ("pts", "rhs"))
        return lax.dynamic_index_in_dim(summed, rhs_index, 0, keepdims=False)

    def apply_operator(vector):
        vec_low = vector.astype(jnp.bfloat16)
        wide_vec = with_halo(vec_low, "pts", 1, rim_rows)
        image_part = apply_k(wide_vec, kmat)
        return noise_var[None, :] * vector + kernel_scale * image_part

    solution = jnp.zeros_like(right_side)
    residual = right_side
    res_image = apply_operator(residual)
    direction = jnp.zeros_like(right_side)
    dir_image = jnp.zeros_like(right_side)
    dir_twice = jnp.zeros_like(right_side)
    norm_prev = None
    step_prev = None
    for iteration in range(ITERS):
        sums = total(
            jnp.stack([jnp.sum(residual * residual, axis=1), jnp.sum(res_image * residual, axis=1)])
        )
        norm_now = sums[0][:, None]
        curvature = sums[1][:, None]
        square_image = apply_operator(res_image)
        if iteration == 0:
            step_len = norm_now / curvature
            direction = residual
            dir_image = res_image
            dir_twice = square_image
        else:
            mix_ratio = norm_now / norm_prev
            step_len = norm_now / (curvature - mix_ratio * norm_now / step_prev)
            direction = residual + mix_ratio * direction
            dir_image = res_image + mix_ratio * dir_image
            dir_twice = square_image + mix_ratio * dir_twice
        solution = solution + step_len * direction
        residual = residual - step_len * dir_image
        res_image = res_image - step_len * dir_twice
        norm_prev = norm_now
        step_prev = step_len
    return (solution, residual, res_image)


def solution(mesh):
    placed = (P("pts", None), P("pts"), P("rhs", "pts"), P("pts", None))
    return jax.shard_map(
        per_device,
        mesh=mesh,
        in_specs=placed,
        out_specs=(P("rhs", "pts"), P("rhs", "pts"), P("rhs", "pts")),
        check_vma=False,
    )
```

time: 577 us -> 341 us (0.59)
  the two profiles are of different devices: /device:TPU:232 before, /device:TPU:16 now
where the time goes in v1:
time: 341 us; the launch traced here: 336 us
  blocking collectives  163 us (48%)
  Pallas kernels  142 us (42%)
  starting transfers between devices  18.4 us (5%)
  other arithmetic  7.05 us (2%)
  local copies, waits for them, and re-layouts  3.9 us (1%)
    psum x2, blocking collectives, total(): summed = lax.psum(slots, ('pts', 'rhs'))  163 us
    pallas_call x1, Pallas kernels, build_k(): pl.pallas_call(build_kernel, out_shape=jax.ShapeDtypeStruct((blocks, BLK,...  96.7 us
    pallas_call x3, Pallas kernels, apply_k(): pl.pallas_call(apply_kernel, out_shape=jax.ShapeDtypeStruct((rows, blocks...  45.3 us
    ppermute x4, starting transfers between devices, with_halo(): lax.ppermute(tail, axis, [(i, (i + 1) % count) for i in range(ends)])  13.2 us
  transfers between devices with their start and end apart: 8, of which 1 were waited for; matrix products, arithmetic and copies ran while one was open for 1% of the time, Pallas kernels for 0%

profile of v1, /device:TPU:16, one launch (start us, length us, event | category | flops | bytes accessed | tf_op | source)
XLA Modules:
  0.0 336.0 jit_solution(14067712028772109730)
XLA Ops:
  0.6 0.9 convert_element_type.9
  1.5 1.7 collective-permute-start
  3.3 1.3 collective-permute-start.1
  4.6 4.3 %collective-permute-start.2 = (bf16[2048,32]{0,1:T(8,128)(2,1)}, bf16[2048,32]{0,1:T(8,128)(2,1)S(1)}, u32[]{:S(2)}, u32[]{:S(2)}) collective-permute-start(bf16[2048,32]{0,1:T(8,128)(2,1)} %param.4), channel_id=1, source_target_pairs={{0,4},{4,8},{8,12},{12,16},{16,20},{20,24},{24,28},{28,32},{32,36}... | collective-permute-start | bytes 393224 | tf_op jit(solution)/shard_map/ppermute | solution.py:25
  8.9 1.3 collective-permute-start.3
  10.2 1.4 reshape.83.pat_ref
  11.6 0.0 collective-permute-done
  11.6 0.0 collective-permute-done.1
  11.6 0.7 pad_maximum_fusion.v_ref
  12.3 0.0 collective-permute-done.2
  12.3 0.9 constant_dynamic-update-slice_fusion.1
  13.2 0.4 collective-permute-done.3
  13.6 0.0 copy-start.1
  13.6 1.6 copy.7.pw_ref
  15.2 0.0 copy-done.1
  15.2 0.0 copy-start
  15.2 0.0 copy-start.3
  15.2 96.7 %shard_map.67.k_ref = bf16[16,128,4224]{2,1,0:T(8,128)(2,1)} custom-call(s32[528]{0:T(1024)} %reshape.83.pat_ref, bf16[6144,32]{1,0:T(8,128)(2,1)} %copy.7.pw_ref, bf16[32,6144]{1,0:T(8,128)(2,1)} %bitcast.36), custom_call_target="tpu_custom_call" | custom-call | tf_op jit(solution)/shard_map/pallas_call | solution.py:76
  111.9 15.1 %shard_map.68 = f32[16,2048]{1,0:T(8,128)} custom-call(bf16[16,6144]{1,0:T(8,128)(2,1)} %pad_maximum_fusion.v_ref, bf16[16,128,4224]{2,1,0:T(8,128)(2,1)} %shard_map.67.k_ref), custom_call_target="tpu_custom_call" | custom-call | tf_op jit(solution)/shard_map/pallas_call | solution.py:95
  127.0 0.0 copy-done
  127.0 0.0 copy-done.3
  127.0 0.9 fusion.6
  127.9 5.5 %collective-permute-start.4 = (bf16[16,2048]{1,0:T(8,128)(2,1)S(1)}, bf16[16,2048]{1,0:T(8,128)(2,1)S(1)}, u32[]{:S(2)}, u32[]{:S(2)}) collective-permute-start(bf16[16,2048]{1,0:T(8,128)(2,1)S(1)} %get-tuple-element.9), channel_id=1, source_target_pairs={{0,4},{4,8},{8,12},{12,16},{16,20},{20,24},{24,28},{28,32},{32,36}... | collective-permute-start | bytes 196616 | tf_op jit(solution)/shard_map/ppermute | solution.py:25
  133.4 1.3 collective-permute-start.5
  134.7 0.1 multiply_reduce_fusion.3
  134.9 86.1 %psum.14 = f32[4,2,16]{2,1,0:T(2,128)S(1)} all-reduce(f32[4,2,16]{2,1,0:T(2,128)S(1)} %fusion), channel_id=1, replica_groups=mesh['pts'=64,'rhs'=4] {'pts','rhs'}, use_global_device_ids=true, to_apply=%region_2.3 | all-reduce | flops 128 | bytes 1024 | tf_op jit(solution)/shard_map/psum | solution.py:122
  221.0 0.0 collective-permute-done.4
  221.0 0.0 collective-permute-done.5
  221.0 0.7 pad_maximum_fusion.1.v_ref
  221.7 15.1 %shard_map.69 = f32[16,2048]{1,0:T(8,128)} custom-call(bf16[16,6144]{1,0:T(8,128)(2,1)} %pad_maximum_fusion.1.v_ref, bf16[16,128,4224]{2,1,0:T(8,128)(2,1)} %shard_map.67.k_ref), custom_call_target="tpu_custom_call" | custom-call | tf_op jit(solution)/shard_map/pallas_call | solution.py:95
  236.8 0.0 copy-start.2
  236.8 1.2 multiply_reduce_fusion.1
  238.0 1.7 collective-permute-start.6
  239.7 1.3 collective-permute-start.7
  241.1 77.4 %psum.15 = f32[4,2,16]{2,1,0:T(2,128)S(1)} all-reduce(f32[4,2,16]{2,1,0:T(2,128)S(1)} %fusion.1), channel_id=1, replica_groups=mesh['pts'=64,'rhs'=4] {'pts','rhs'}, use_global_device_ids=true, to_apply=%region_5.6 | all-reduce | flops 128 | bytes 1024 | tf_op jit(solution)/shard_map/psum | solution.py:122
  318.4 0.0 collective-permute-done.6
  318.4 0.0 collective-permute-done.7
  318.5 0.7 pad_maximum_fusion.2.v_ref
  319.1 15.1 %shard_map.70 = f32[16,2048]{1,0:T(8,128)} custom-call(bf16[16,6144]{1,0:T(8,128)(2,1)} %pad_maximum_fusion.2.v_ref, bf16[16,128,4224]{2,1,0:T(8,128)(2,1)} %shard_map.67.k_ref), custom_call_target="tpu_custom_call" | custom-call | tf_op jit(solution)/shard_map/pallas_call | solution.py:95
  334.2 0.0 copy-done.2
  334.2 1.8 multiply_subtract_fusion
  (10 shorter events, 0.1 us)
Async XLA Ops:
  1.5 10.0 %collective-permute-start = (bf16[16,2048]{1,0:T(8,128)(2,1)S(1)}, bf16[16,2048]{1,0:T(8,128)(2,1)S(1)}, u32[]{:S(2)}, u32[]{:S(2)}) collective-permute-start(bf16[16,2048]{1,0:T(8,128)(2,1)S(1)} %convert_element_type.9), channel_id=1, source_target_pairs={{0,4},{4,8},{8,12},{12,16},{16,20},{20,24},{24,28},{28,32},{32,36}... | collective-permute-start | bytes 196616 | tf_op jit(solution)/shard_map/ppermute | solution.py:25
  3.3 8.3 %collective-permute-start.1 = (bf16[16,2048]{1,0:T(8,128)(2,1)S(1)}, bf16[16,2048]{1,0:T(8,128)(2,1)S(1)}, u32[]{:S(2)}, u32[]{:S(2)}) collective-permute-start(bf16[16,2048]{1,0:T(8,128)(2,1)S(1)} %convert_element_type.9), channel_id=1, source_target_pairs={{4,0},{8,4},{12,8},{16,12},{20,16},{24,20},{28,24},{32,28},{36,32}... | collective-permute-start | bytes 196616 | tf_op jit(solution)/shard_map/ppermute | solution.py:27
  4.6 7.7 %collective-permute-start.2 = (bf16[2048,32]{0,1:T(8,128)(2,1)}, bf16[2048,32]{0,1:T(8,128)(2,1)S(1)}, u32[]{:S(2)}, u32[]{:S(2)}) collective-permute-start(bf16[2048,32]{0,1:T(8,128)(2,1)} %param.4), channel_id=1, source_target_pairs={{0,4},{4,8},{8,12},{12,16},{16,20},{20,24},{24,28},{28,32},{32,36}... | collective-permute-start | bytes 393224 | tf_op jit(solution)/shard_map/ppermute | solution.py:25
  8.9 4.7 %collective-permute-start.3 = (bf16[2048,32]{0,1:T(8,128)(2,1)}, bf16[2048,32]{0,1:T(8,128)(2,1)S(1)}, u32[]{:S(2)}, u32[]{:S(2)}) collective-permute-start(bf16[2048,32]{0,1:T(8,128)(2,1)} %param.4), channel_id=1, source_target_pairs={{4,0},{8,4},{12,8},{16,12},{20,16},{24,20},{28,24},{32,28},{36,32}... | collective-permute-start | bytes 393224 | tf_op jit(solution)/shard_map/ppermute | solution.py:27
  13.6 1.6 copy-start.1
  15.2 111.8 %copy-start = (f32[16,2048]{1,0:T(8,128)S(1)}, f32[16,2048]{1,0:T(8,128)}, u32[]{:S(2)}) copy-start(f32[16,2048]{1,0:T(8,128)} %param.6) | copy-start | bytes 393220
  15.2 111.8 %copy-start.3 = (f32[2048]{0:T(1024)S(1)}, f32[2048]{0:T(1024)}, u32[]{:S(2)}) copy-start(f32[2048]{0:T(1024)} %param.5) | copy-start | bytes 24580
  127.9 93.0 %collective-permute-start.4 = (bf16[16,2048]{1,0:T(8,128)(2,1)S(1)}, bf16[16,2048]{1,0:T(8,128)(2,1)S(1)}, u32[]{:S(2)}, u32[]{:S(2)}) collective-permute-start(bf16[16,2048]{1,0:T(8,128)(2,1)S(1)} %get-tuple-element.9), channel_id=1, source_target_pairs={{0,4},{4,8},{8,12},{12,16},{16,20},{20,24},{24,28},{28,32},{32,36}... | collective-permute-start | bytes 196616 | tf_op jit(solution)/shard_map/ppermute | solution.py:25
  133.4 87.6 %collective-permute-start.5 = (bf16[16,2048]{1,0:T(8,128)(2,1)S(1)}, bf16[16,2048]{1,0:T(8,128)(2,1)S(1)}, u32[]{:S(2)}, u32[]{:S(2)}) collective-permute-start(bf16[16,2048]{1,0:T(8,128)(2,1)S(1)} %get-tuple-element.9), channel_id=1, source_target_pairs={{4,0},{8,4},{12,8},{16,12},{20,16},{24,20},{28,24},{32,28},{36,32}... | collective-permute-start | bytes 196616 | tf_op jit(solution)/shard_map/ppermute | solution.py:27
  236.8 97.5 %copy-start.2 = (f32[16,2048]{1,0:T(8,128)S(1)}, f32[16,2048]{1,0:T(8,128)}, u32[]{:S(2)}) copy-start(f32[16,2048]{1,0:T(8,128)} %shard_map.69) | copy-start | bytes 393220
  238.0 80.5 %collective-permute-start.6 = (bf16[16,2048]{1,0:T(8,128)(2,1)S(1)}, bf16[16,2048]{1,0:T(8,128)(2,1)S(1)}, u32[]{:S(2)}, u32[]{:S(2)}) collective-permute-start(bf16[16,2048]{1,0:T(8,128)(2,1)S(1)} %get-tuple-element.13), channel_id=1, source_target_pairs={{0,4},{4,8},{8,12},{12,16},{16,20},{20,24},{24,28},{28,32},{32,36}... | collective-permute-start | bytes 196616 | tf_op jit(solution)/shard_map/ppermute | solution.py:25
  239.7 78.7 %collective-permute-start.7 = (bf16[16,2048]{1,0:T(8,128)(2,1)S(1)}, bf16[16,2048]{1,0:T(8,128)(2,1)S(1)}, u32[]{:S(2)}, u32[]{:S(2)}) collective-permute-start(bf16[16,2048]{1,0:T(8,128)(2,1)S(1)} %get-tuple-element.13), channel_id=1, source_target_pairs={{4,0},{8,4},{12,8},{16,12},{20,16},{24,20},{28,24},{32,28},{36,32}... | collective-permute-start | bytes 196616 | tf_op jit(solution)/shard_map/ppermute | solution.py:27

commit v2 on v1

--- a/solution.py
+++ b/solution.py
@@ -117,10 +117,10 @@
     rhs_index = lax.axis_index("rhs")
 
     def total(parts):
-        slots = jnp.zeros((rhs_count,) + parts.shape, parts.dtype)
-        slots = lax.dynamic_update_index_in_dim(slots, parts, rhs_index, 0)
-        summed = lax.psum(slots, ("pts", "rhs"))
-        return lax.dynamic_index_in_dim(summed, rhs_index, 0, keepdims=False)
+        slots = jnp.zeros((128, 128), parts.dtype)
+        slots = lax.dynamic_update_slice(slots, parts, (0, 0))
+        summed = lax.psum(slots, "pts")
+        return summed[:2, :16]
 
     def apply_operator(vector):
         vec_low = vector.astype(jnp.bfloat16)

time: 341 us -> 523 us (1.53)
  waiting for transfers between devices: 0.4 us -> 331 us
  blocking collectives: 163 us -> 0 us
  between operations: 0.77 us -> 14.2 us
    psum x0 -> x2, waiting for transfers between devices: none -> 331 us  [total(): summed = lax.psum(slots, 'pts')]
    psum x2 -> x0, blocking collectives: 163 us -> none  [total(): summed = lax.psum(slots, ('pts', 'rhs'))]
  transfers between devices with their start and end apart: 8 -> 10, of which waited for: 1 -> 2; matrix products, arithmetic and copies ran while one was open for 1% -> 1% of each run, Pallas kernels for 0% -> 0%
where the time goes in v2:
time: 523 us; the launch traced here: 520 us
  waiting for transfers between devices  331 us (63%)
  Pallas kernels  142 us (27%)
  starting transfers between devices  19.5 us (4%)
  between operations  14.2 us (3%)
  other arithmetic  9.8 us (2%)
    psum x2, waiting for transfers between devices, total(): summed = lax.psum(slots, 'pts')  331 us
    pallas_call x1, Pallas kernels, build_k(): pl.pallas_call(build_kernel, out_shape=jax.ShapeDtypeStruct((blocks, BLK,...  96.7 us
    pallas_call x3, Pallas kernels, apply_k(): pl.pallas_call(apply_kernel, out_shape=jax.ShapeDtypeStruct((rows, blocks...  45.3 us
    ppermute x4, starting transfers between devices, with_halo(): lax.ppermute(tail, axis, [(i, (i + 1) % count) for i in range(ends)])  14.3 us
  transfers between devices with their start and end apart: 10, of which 2 were waited for; matrix products, arithmetic and copies ran while one was open for 1% of the time, Pallas kernels for 0%

profile of v2, /device:TPU:16, one launch (start us, length us, event | category | flops | bytes accessed | tf_op | source)
XLA Modules:
  0.0 520.2 jit_solution(2988545772322954116)
XLA Ops:
  7.2 0.0 all-reduce.5.cloned.1.call-start
  7.2 0.9 convert_element_type.9
  8.1 1.3 collective-permute-start.1
  9.4 3.0 collective-permute-start
  12.5 3.0 collective-permute-start.2
  15.5 1.3 collective-permute-start.3
  16.8 1.4 reshape.75.pat_ref
  18.2 0.0 collective-permute-done.1
  18.2 0.0 collective-permute-done
  18.2 0.7 pad_maximum_fusion.v_ref
  18.8 0.0 collective-permute-done.2
  18.9 0.9 constant_dynamic-update-slice_fusion.1
  19.8 0.0 collective-permute-done.3
  19.8 0.0 copy-start.1
  19.8 1.5 copy.7.pw_ref
  21.4 0.0 copy-done.1
  21.4 0.0 copy-start
  21.4 0.0 copy-start.3
  21.4 96.7 %shard_map.67.k_ref = bf16[16,128,4224]{2,1,0:T(8,128)(2,1)} custom-call(s32[528]{0:T(1024)} %reshape.75.pat_ref, bf16[6144,32]{1,0:T(8,128)(2,1)} %copy.7.pw_ref, bf16[32,6144]{1,0:T(8,128)(2,1)} %bitcast.33), custom_call_target="tpu_custom_call" | custom-call | tf_op jit(solution)/shard_map/pallas_call | solution.py:76
  118.1 15.1 %shard_map.68 = f32[16,2048]{1,0:T(8,128)} custom-call(bf16[16,6144]{1,0:T(8,128)(2,1)} %pad_maximum_fusion.v_ref, bf16[16,128,4224]{2,1,0:T(8,128)(2,1)} %shard_map.67.k_ref), custom_call_target="tpu_custom_call" | custom-call | tf_op jit(solution)/shard_map/pallas_call | solution.py:95
  133.2 0.0 copy-done
  133.2 0.0 copy-done.3
  133.2 0.9 fusion.7
  134.1 0.1 multiply_reduce_fusion.3
  134.2 0.6 select_maximum_fusion.1
  134.9 0.0 all-reduce.5.cloned.1.call-update
  134.9 0.0 all-reduce.7.cloned.1.call-start
  135.0 1.3 collective-permute-start.5
  136.3 5.2 %collective-permute-start.4 = (bf16[16,2048]{1,0:T(8,128)(2,1)S(1)}, bf16[16,2048]{1,0:T(8,128)(2,1)S(1)}, u32[]{:S(2)}, u32[]{:S(2)}) collective-permute-start(bf16[16,2048]{1,0:T(8,128)(2,1)S(1)} %get-tuple-element.9), channel_id=1, source_target_pairs={{0,4},{4,8},{8,12},{12,16},{16,20},{20,24},{24,28},{28,32},{32,36}... | collective-permute-start | bytes 196616 | tf_op jit(solution)/shard_map/ppermute | solution.py:25
  141.5 169.8 %all-reduce.5.cloned.1.call-done = f32[128,128]{1,0:T(8,128)} async-done(((f32[128,128]{1,0:T(8,128)}), f32[128,128]{1,0:T(8,128)}) %all-reduce.5.cloned.1.call-update) | async-done | bytes 65552 | tf_op jit(solution)/shard_map/psum | solution.py:122
  311.3 0.8 fusion.3
  312.1 0.0 collective-permute-done.5
  312.1 0.0 collective-permute-done.4
  312.1 0.7 pad_maximum_fusion.1.v_ref
  312.8 15.1 %shard_map.69 = f32[16,2048]{1,0:T(8,128)} custom-call(bf16[16,6144]{1,0:T(8,128)(2,1)} %pad_maximum_fusion.1.v_ref, bf16[16,128,4224]{2,1,0:T(8,128)(2,1)} %shard_map.67.k_ref), custom_call_target="tpu_custom_call" | custom-call | tf_op jit(solution)/shard_map/pallas_call | solution.py:95
  327.9 0.0 copy-start.2
  327.9 1.2 multiply_reduce_fusion.1
  329.0 0.6 select_maximum_fusion
  329.7 0.0 all-reduce.7.cloned.1.call-update
  329.7 1.3 collective-permute-start.7
  331.0 3.0 collective-permute-start.6
  334.1 160.9 %all-reduce.7.cloned.1.call-done = f32[128,128]{1,0:T(8,128)} async-done(((f32[128,128]{1,0:T(8,128)}), f32[128,128]{1,0:T(8,128)}) %all-reduce.7.cloned.1.call-update) | async-done | bytes 65552 | tf_op jit(solution)/shard_map/psum | solution.py:122
  495.0 0.8 fusion.2
  495.8 0.0 collective-permute-done.7
  495.8 0.0 collective-permute-done.6
  495.8 0.7 pad_maximum_fusion.2.v_ref
  496.5 15.1 %shard_map.70 = f32[16,2048]{1,0:T(8,128)} custom-call(bf16[16,6144]{1,0:T(8,128)(2,1)} %pad_maximum_fusion.2.v_ref, bf16[16,128,4224]{2,1,0:T(8,128)(2,1)} %shard_map.67.k_ref), custom_call_target="tpu_custom_call" | custom-call | tf_op jit(solution)/shard_map/pallas_call | solution.py:95
  511.6 0.0 copy-done.2
  511.6 1.8 multiply_subtract_fusion
  (2 shorter events, 0.0 us)
Async XLA Ops:
  7.2 304.1 %all-reduce.5.cloned.1.call-start = ((), (), s32[]{:S(2)}) async-start(), calls=%async_computation | async-start | bytes 131072 | tf_op jit(solution)/shard_map/psum | solution.py:122
  8.1 10.0 %collective-permute-start.1 = (bf16[16,2048]{1,0:T(8,128)(2,1)S(1)}, bf16[16,2048]{1,0:T(8,128)(2,1)S(1)}, u32[]{:S(2)}, u32[]{:S(2)}) collective-permute-start(bf16[16,2048]{1,0:T(8,128)(2,1)S(1)} %convert_element_type.9), channel_id=1, source_target_pairs={{4,0},{8,4},{12,8},{16,12},{20,16},{24,20},{28,24},{32,28},{36,32}... | collective-permute-start | bytes 196616 | tf_op jit(solution)/shard_map/ppermute | solution.py:27
  9.4 8.8 %collective-permute-start = (bf16[16,2048]{1,0:T(8,128)(2,1)S(1)}, bf16[16,2048]{1,0:T(8,128)(2,1)S(1)}, u32[]{:S(2)}, u32[]{:S(2)}) collective-permute-start(bf16[16,2048]{1,0:T(8,128)(2,1)S(1)} %convert_element_type.9), channel_id=1, source_target_pairs={{0,4},{4,8},{8,12},{12,16},{16,20},{20,24},{24,28},{28,32},{32,36}... | collective-permute-start | bytes 196616 | tf_op jit(solution)/shard_map/ppermute | solution.py:25
  12.5 6.4 %collective-permute-start.2 = (bf16[2048,32]{0,1:T(8,128)(2,1)}, bf16[2048,32]{0,1:T(8,128)(2,1)S(1)}, u32[]{:S(2)}, u32[]{:S(2)}) collective-permute-start(bf16[2048,32]{0,1:T(8,128)(2,1)} %param.4), channel_id=1, source_target_pairs={{0,4},{4,8},{8,12},{12,16},{16,20},{20,24},{24,28},{28,32},{32,36}... | collective-permute-start | bytes 393224 | tf_op jit(solution)/shard_map/ppermute | solution.py:25
  15.5 4.3 collective-permute-start.3
  19.8 1.5 copy-start.1
  21.4 111.8 %copy-start = (f32[16,2048]{1,0:T(8,128)S(1)}, f32[16,2048]{1,0:T(8,128)}, u32[]{:S(2)}) copy-start(f32[16,2048]{1,0:T(8,128)} %param.6) | copy-start | bytes 393220
  21.4 111.8 %copy-start.3 = (f32[2048]{0:T(1024)S(1)}, f32[2048]{0:T(1024)}, u32[]{:S(2)}) copy-start(f32[2048]{0:T(1024)} %param.5) | copy-start | bytes 24580
  134.9 360.1 %all-reduce.7.cloned.1.call-start = ((), (), s32[]{:S(2)}) async-start(), calls=%async_computation.1 | async-start | bytes 131072 | tf_op jit(solution)/shard_map/psum | solution.py:122
  135.0 177.1 %collective-permute-start.5 = (bf16[16,2048]{1,0:T(8,128)(2,1)S(1)}, bf16[16,2048]{1,0:T(8,128)(2,1)S(1)}, u32[]{:S(2)}, u32[]{:S(2)}) collective-permute-start(bf16[16,2048]{1,0:T(8,128)(2,1)S(1)} %get-tuple-element.9), channel_id=1, source_target_pairs={{4,0},{8,4},{12,8},{16,12},{20,16},{24,20},{28,24},{32,28},{36,32}... | collective-permute-start | bytes 196616 | tf_op jit(solution)/shard_map/ppermute | solution.py:27
  136.3 175.8 %collective-permute-start.4 = (bf16[16,2048]{1,0:T(8,128)(2,1)S(1)}, bf16[16,2048]{1,0:T(8,128)(2,1)S(1)}, u32[]{:S(2)}, u32[]{:S(2)}) collective-permute-start(bf16[16,2048]{1,0:T(8,128)(2,1)S(1)} %get-tuple-element.9), channel_id=1, source_target_pairs={{0,4},{4,8},{8,12},{12,16},{16,20},{20,24},{24,28},{28,32},{32,36}... | collective-permute-start | bytes 196616 | tf_op jit(solution)/shard_map/ppermute | solution.py:25
  327.9 183.7 %copy-start.2 = (f32[16,2048]{1,0:T(8,128)S(1)}, f32[16,2048]{1,0:T(8,128)}, u32[]{:S(2)}) copy-start(f32[16,2048]{1,0:T(8,128)} %shard_map.69) | copy-start | bytes 393220
  329.7 166.1 %collective-permute-start.7 = (bf16[16,2048]{1,0:T(8,128)(2,1)S(1)}, bf16[16,2048]{1,0:T(8,128)(2,1)S(1)}, u32[]{:S(2)}, u32[]{:S(2)}) collective-permute-start(bf16[16,2048]{1,0:T(8,128)(2,1)S(1)} %get-tuple-element.13), channel_id=1, source_target_pairs={{4,0},{8,4},{12,8},{16,12},{20,16},{24,20},{28,24},{32,28},{36,32}... | collective-permute-start | bytes 196616 | tf_op jit(solution)/shard_map/ppermute | solution.py:27
  331.0 164.8 %collective-permute-start.6 = (bf16[16,2048]{1,0:T(8,128)(2,1)S(1)}, bf16[16,2048]{1,0:T(8,128)(2,1)S(1)}, u32[]{:S(2)}, u32[]{:S(2)}) collective-permute-start(bf16[16,2048]{1,0:T(8,128)(2,1)S(1)} %get-tuple-element.13), channel_id=1, source_target_pairs={{0,4},{4,8},{8,12},{12,16},{16,20},{20,24},{24,28},{28,32},{32,36}... | collective-permute-start | bytes 196616 | tf_op jit(solution)/shard_map/ppermute | solution.py:25
Sparse Core Ops, SparseCore 0:
  135.0 176.2 all-reduce.4
  329.8 165.1 all-reduce.6

commit v3 on v2

--- a/solution.py
+++ b/solution.py
@@ -13,6 +13,7 @@
 ITERS = 2
 WIDE = 33
 WEXP = 18
+MESH = pl.DeviceIdType.MESH
 
 
 def with_halo(cells, axis, dim, width):
@@ -105,6 +106,73 @@
     )(wide_vec, kmat)
 
 
+def sum_kernel(count, part_ref, out_ref, recv, send_sem, recv_sem):
+    me = lax.axis_index("pts")
+    row = lax.axis_index("rhs")
+
+    barrier = pltpu.get_barrier_semaphore()
+
+    def greet(k, carry):
+        peer = lax.rem(me + k, count)
+        pl.semaphore_signal(barrier, inc=1, device_id=(peer, row), device_id_type=MESH)
+        return carry
+
+    lax.fori_loop(1, count, greet, 0)
+    pl.semaphore_wait(barrier, count - 1)
+
+    def outgoing(peer):
+        return pltpu.make_async_remote_copy(
+            src_ref=part_ref,
+            dst_ref=recv.at[me],
+            send_sem=send_sem.at[peer],
+            recv_sem=recv_sem.at[me],
+            device_id=(peer, row),
+            device_id_type=MESH,
+        )
+
+    def incoming(peer):
+        return pltpu.make_async_remote_copy(
+            src_ref=part_ref,
+            dst_ref=recv.at[peer],
+            send_sem=send_sem.at[peer],
+            recv_sem=recv_sem.at[peer],
+            device_id=(peer, row),
+            device_id_type=MESH,
+        )
+
+    def send(k, carry):
+        outgoing(lax.rem(me + k, count)).start()
+        return carry
+
+    lax.fori_loop(1, count, send, 0)
+    recv[me] = part_ref[...]
+
+    def finish(k, carry):
+        peer = lax.rem(me + k, count)
+        outgoing(peer).wait_send()
+        incoming(peer).wait_recv()
+        return carry
+
+    lax.fori_loop(1, count, finish, 0)
+    out_ref[...] = jnp.sum(recv[...], axis=0)
+
+
+def all_sum(tile):
+    count = lax.axis_size("pts")
+    return pl.pallas_call(
+        functools.partial(sum_kernel, count),
+        out_shape=jax.ShapeDtypeStruct(tile.shape, jnp.float32),
+        in_specs=[pl.BlockSpec(memory_space=pltpu.VMEM)],
+        out_specs=pl.BlockSpec(memory_space=pltpu.VMEM),
+        scratch_shapes=[
+            pltpu.VMEM((count,) + tile.shape, jnp.float32),
+            pltpu.SemaphoreType.DMA((count,)),
+            pltpu.SemaphoreType.DMA((count,)),
+        ],
+        compiler_params=pltpu.CompilerParams(collective_id=0, has_side_effects=True),
+    )(tile)
+
+
 def per_device(points, noise_var, right_side, pattern):
     local_rows = points.shape[0]
     block_count = local_rows // BLK
@@ -117,10 +185,10 @@
     rhs_index = lax.axis_index("rhs")
 
     def total(parts):
-        slots = jnp.zeros((128, 128), parts.dtype)
-        slots = lax.dynamic_update_slice(slots, parts, (0, 0))
-        summed = lax.psum(slots, "pts")
-        return summed[:2, :16]
+        tile = jnp.zeros((8, 128), jnp.float32)
+        tile = lax.dynamic_update_slice(tile, parts, (0, 0))
+        summed = all_sum(tile)
+        return summed[: parts.shape[0], : parts.shape[1]]
 
     def apply_operator(vector):
         vec_low = vector.astype(jnp.bfloat16)

time: 523 us -> 229 us (0.44)
  waiting for transfers between devices: 331 us -> 0.02 us
  Pallas kernels: 142 us -> 192 us
  between operations: 14.2 us -> 0.77 us
    psum x2 -> x0, waiting for transfers between devices: 331 us -> none  [total(): summed = lax.psum(slots, 'pts')]
    pallas_call x0 -> x2, Pallas kernels: none -> 50.3 us  [all_sum(): pl.pallas_call(functools.partial(sum_kernel, count), out_shape=jax.ShapeD...]
  transfers between devices with their start and end apart: 10 -> 8, of which waited for: 2 -> 0; matrix products, arithmetic and copies ran while one was open for 1% -> 3% of each run, Pallas kernels for 0% -> 22%
where the time goes in v3:
time: 229 us; the launch traced here: 226 us
  Pallas kernels  192 us (84%)
  starting transfers between devices  19.5 us (9%)
  other arithmetic  9.72 us (4%)
  local copies, waits for them, and re-layouts  3.86 us (2%)
    pallas_call x1, Pallas kernels, build_k(): pl.pallas_call(build_kernel, out_shape=jax.ShapeDtypeStruct((blocks, BLK,...  96.7 us
    pallas_call x2, Pallas kernels, all_sum(): pl.pallas_call(functools.partial(sum_kernel, count), out_shape=jax.ShapeD...  50.3 us
    pallas_call x3, Pallas kernels, apply_k(): pl.pallas_call(apply_kernel, out_shape=jax.ShapeDtypeStruct((rows, blocks...  45.3 us
    ppermute x4, starting transfers between devices, with_halo(): lax.ppermute(tail, axis, [(i, (i + 1) % count) for i in range(ends)])  14.3 us
    ppermute x4, starting transfers between devices, with_halo(): lax.ppermute(head, axis, [((i + 1) % count, i) for i in range(ends)])  5.15 us
  transfers between devices with their start and end apart: 8, of which 0 were waited for; matrix products, arithmetic and copies ran while one was open for 3% of the time, Pallas kernels for 22%

profile of v3, /device:TPU:16, one launch (start us, length us, event | category | flops | bytes accessed | tf_op | source)
XLA Modules:
  0.0 226.2 jit_solution(15695506666722486114)
XLA Ops:
  0.6 0.9 convert_element_type.9
  1.5 1.3 collective-permute-start.1
  2.8 3.0 %collective-permute-start = (bf16[16,2048]{1,0:T(8,128)(2,1)S(1)}, bf16[16,2048]{1,0:T(8,128)(2,1)S(1)}, u32[]{:S(2)}, u32[]{:S(2)}) collective-permute-start(bf16[16,2048]{1,0:T(8,128)(2,1)S(1)} %convert_element_type.9), channel_id=1, source_target_pairs={{0,4},{4,8},{8,12},{12,16},{16,20},{20,24},{24,28},{28,32},{32,36}... | collective-permute-start | bytes 196616 | tf_op jit(solution)/shard_map/ppermute | solution.py:26
  5.9 3.0 %collective-permute-start.2 = (bf16[2048,32]{0,1:T(8,128)(2,1)}, bf16[2048,32]{0,1:T(8,128)(2,1)S(1)}, u32[]{:S(2)}, u32[]{:S(2)}) collective-permute-start(bf16[2048,32]{0,1:T(8,128)(2,1)} %param.4), channel_id=1, source_target_pairs={{0,4},{4,8},{8,12},{12,16},{16,20},{20,24},{24,28},{28,32},{32,36}... | collective-permute-start | bytes 393224 | tf_op jit(solution)/shard_map/ppermute | solution.py:26
  8.9 1.3 collective-permute-start.3
  10.2 1.4 reshape.75.pat_ref
  11.6 0.0 collective-permute-done.1
  11.6 0.0 collective-permute-done
  11.6 0.7 pad_maximum_fusion.v_ref
  12.3 0.0 collective-permute-done.2
  12.3 0.9 constant_dynamic-update-slice_fusion.1
  13.2 0.0 collective-permute-done.3
  13.2 0.0 copy-start.1
  13.2 1.5 copy.7.pw_ref
  14.8 0.0 copy-done.1
  14.8 0.0 copy-start
  14.8 0.0 copy-start.3
  14.8 96.7 %shard_map.67.k_ref = bf16[16,128,4224]{2,1,0:T(8,128)(2,1)} custom-call(s32[528]{0:T(1024)} %reshape.75.pat_ref, bf16[6144,32]{1,0:T(8,128)(2,1)} %copy.7.pw_ref, bf16[32,6144]{1,0:T(8,128)(2,1)} %bitcast.28), custom_call_target="tpu_custom_call" | custom-call | tf_op jit(solution)/shard_map/pallas_call | solution.py:77
  111.5 15.1 %shard_map.68 = f32[16,2048]{1,0:T(8,128)} custom-call(bf16[16,6144]{1,0:T(8,128)(2,1)} %pad_maximum_fusion.v_ref, bf16[16,128,4224]{2,1,0:T(8,128)(2,1)} %shard_map.67.k_ref), custom_call_target="tpu_custom_call" | custom-call | tf_op jit(solution)/shard_map/pallas_call | solution.py:96
  126.6 0.0 copy-done
  126.6 0.0 copy-done.3
  126.6 0.9 fusion.5
  127.5 1.3 collective-permute-start.5
  128.8 5.2 %collective-permute-start.4 = (bf16[16,2048]{1,0:T(8,128)(2,1)S(1)}, bf16[16,2048]{1,0:T(8,128)(2,1)S(1)}, u32[]{:S(2)}, u32[]{:S(2)}) collective-permute-start(bf16[16,2048]{1,0:T(8,128)(2,1)S(1)} %get-tuple-element.9), channel_id=1, source_target_pairs={{0,4},{4,8},{8,12},{12,16},{16,20},{20,24},{24,28},{28,32},{32,36}... | collective-permute-start | bytes 196616 | tf_op jit(solution)/shard_map/ppermute | solution.py:26
  134.0 0.1 multiply_reduce_fusion.3
  134.2 0.6 select_maximum_fusion.1.part_ref
  134.8 29.4 %shard_map.69 = f32[8,128]{1,0:T(8,128)} custom-call(f32[8,128]{1,0:T(8,128)} %select_maximum_fusion.1.part_ref), custom_call_target="tpu_custom_call" | custom-call | tf_op jit(solution)/shard_map/pallas_call | solution.py:162
  164.2 0.8 bitcast_divide_fusion.1
  164.9 0.0 collective-permute-done.5
  164.9 0.0 collective-permute-done.4
  164.9 0.7 pad_maximum_fusion.1.v_ref
  165.6 15.1 %shard_map.70 = f32[16,2048]{1,0:T(8,128)} custom-call(bf16[16,6144]{1,0:T(8,128)(2,1)} %pad_maximum_fusion.1.v_ref, bf16[16,128,4224]{2,1,0:T(8,128)(2,1)} %shard_map.67.k_ref), custom_call_target="tpu_custom_call" | custom-call | tf_op jit(solution)/shard_map/pallas_call | solution.py:96
  180.7 0.0 copy-start.2
  180.7 1.2 multiply_reduce_fusion.1
  181.9 1.3 collective-permute-start.7
  183.2 3.0 %collective-permute-start.6 = (bf16[16,2048]{1,0:T(8,128)(2,1)S(1)}, bf16[16,2048]{1,0:T(8,128)(2,1)S(1)}, u32[]{:S(2)}, u32[]{:S(2)}) collective-permute-start(bf16[16,2048]{1,0:T(8,128)(2,1)S(1)} %get-tuple-element.13), channel_id=1, source_target_pairs={{0,4},{4,8},{8,12},{12,16},{16,20},{20,24},{24,28},{28,32},{32,36}... | collective-permute-start | bytes 196616 | tf_op jit(solution)/shard_map/ppermute | solution.py:26
  186.3 0.6 select_maximum_fusion.part_ref
  186.9 21.0 %shard_map.71 = f32[8,128]{1,0:T(8,128)} custom-call(f32[8,128]{1,0:T(8,128)} %select_maximum_fusion.part_ref), custom_call_target="tpu_custom_call" | custom-call | tf_op jit(solution)/shard_map/pallas_call | solution.py:162
  207.8 0.8 fusion.1
  208.6 0.0 collective-permute-done.7
  208.6 0.0 collective-permute-done.6
  208.6 0.7 pad_maximum_fusion.2.v_ref
  209.3 15.1 %shard_map.72 = f32[16,2048]{1,0:T(8,128)} custom-call(bf16[16,6144]{1,0:T(8,128)(2,1)} %pad_maximum_fusion.2.v_ref, bf16[16,128,4224]{2,1,0:T(8,128)(2,1)} %shard_map.67.k_ref), custom_call_target="tpu_custom_call" | custom-call | tf_op jit(solution)/shard_map/pallas_call | solution.py:96
  224.4 0.0 copy-done.2
  224.4 1.8 multiply_subtract_fusion
  (2 shorter events, 0.0 us)
Async XLA Ops:
  1.5 10.0 %collective-permute-start.1 = (bf16[16,2048]{1,0:T(8,128)(2,1)S(1)}, bf16[16,2048]{1,0:T(8,128)(2,1)S(1)}, u32[]{:S(2)}, u32[]{:S(2)}) collective-permute-start(bf16[16,2048]{1,0:T(8,128)(2,1)S(1)} %convert_element_type.9), channel_id=1, source_target_pairs={{4,0},{8,4},{12,8},{16,12},{20,16},{24,20},{28,24},{32,28},{36,32}... | collective-permute-start | bytes 196616 | tf_op jit(solution)/shard_map/ppermute | solution.py:28
  2.8 8.8 %collective-permute-start = (bf16[16,2048]{1,0:T(8,128)(2,1)S(1)}, bf16[16,2048]{1,0:T(8,128)(2,1)S(1)}, u32[]{:S(2)}, u32[]{:S(2)}) collective-permute-start(bf16[16,2048]{1,0:T(8,128)(2,1)S(1)} %convert_element_type.9), channel_id=1, source_target_pairs={{0,4},{4,8},{8,12},{12,16},{16,20},{20,24},{24,28},{28,32},{32,36}... | collective-permute-start | bytes 196616 | tf_op jit(solution)/shard_map/ppermute | solution.py:26
  5.9 6.4 %collective-permute-start.2 = (bf16[2048,32]{0,1:T(8,128)(2,1)}, bf16[2048,32]{0,1:T(8,128)(2,1)S(1)}, u32[]{:S(2)}, u32[]{:S(2)}) collective-permute-start(bf16[2048,32]{0,1:T(8,128)(2,1)} %param.4), channel_id=1, source_target_pairs={{0,4},{4,8},{8,12},{12,16},{16,20},{20,24},{24,28},{28,32},{32,36}... | collective-permute-start | bytes 393224 | tf_op jit(solution)/shard_map/ppermute | solution.py:26
  8.9 4.3 %collective-permute-start.3 = (bf16[2048,32]{0,1:T(8,128)(2,1)}, bf16[2048,32]{0,1:T(8,128)(2,1)S(1)}, u32[]{:S(2)}, u32[]{:S(2)}) collective-permute-start(bf16[2048,32]{0,1:T(8,128)(2,1)} %param.4), channel_id=1, source_target_pairs={{4,0},{8,4},{12,8},{16,12},{20,16},{24,20},{28,24},{32,28},{36,32}... | collective-permute-start | bytes 393224 | tf_op jit(solution)/shard_map/ppermute | solution.py:28
  13.2 1.5 copy-start.1
  14.8 111.8 %copy-start = (f32[16,2048]{1,0:T(8,128)S(1)}, f32[16,2048]{1,0:T(8,128)}, u32[]{:S(2)}) copy-start(f32[16,2048]{1,0:T(8,128)} %param.6) | copy-start | bytes 393220
  14.8 111.8 %copy-start.3 = (f32[2048]{0:T(1024)S(1)}, f32[2048]{0:T(1024)}, u32[]{:S(2)}) copy-start(f32[2048]{0:T(1024)} %param.5) | copy-start | bytes 24580
  127.5 37.4 %collective-permute-start.5 = (bf16[16,2048]{1,0:T(8,128)(2,1)S(1)}, bf16[16,2048]{1,0:T(8,128)(2,1)S(1)}, u32[]{:S(2)}, u32[]{:S(2)}) collective-permute-start(bf16[16,2048]{1,0:T(8,128)(2,1)S(1)} %get-tuple-element.9), channel_id=1, source_target_pairs={{4,0},{8,4},{12,8},{16,12},{20,16},{24,20},{28,24},{32,28},{36,32}... | collective-permute-start | bytes 196616 | tf_op jit(solution)/shard_map/ppermute | solution.py:28
  128.8 36.1 %collective-permute-start.4 = (bf16[16,2048]{1,0:T(8,128)(2,1)S(1)}, bf16[16,2048]{1,0:T(8,128)(2,1)S(1)}, u32[]{:S(2)}, u32[]{:S(2)}) collective-permute-start(bf16[16,2048]{1,0:T(8,128)(2,1)S(1)} %get-tuple-element.9), channel_id=1, source_target_pairs={{0,4},{4,8},{8,12},{12,16},{16,20},{20,24},{24,28},{28,32},{32,36}... | collective-permute-start | bytes 196616 | tf_op jit(solution)/shard_map/ppermute | solution.py:26
  180.7 43.7 %copy-start.2 = (f32[16,2048]{1,0:T(8,128)S(1)}, f32[16,2048]{1,0:T(8,128)}, u32[]{:S(2)}) copy-start(f32[16,2048]{1,0:T(8,128)} %shard_map.70) | copy-start | bytes 393220
  181.9 26.7 %collective-permute-start.7 = (bf16[16,2048]{1,0:T(8,128)(2,1)S(1)}, bf16[16,2048]{1,0:T(8,128)(2,1)S(1)}, u32[]{:S(2)}, u32[]{:S(2)}) collective-permute-start(bf16[16,2048]{1,0:T(8,128)(2,1)S(1)} %get-tuple-element.13), channel_id=1, source_target_pairs={{4,0},{8,4},{12,8},{16,12},{20,16},{24,20},{28,24},{32,28},{36,32}... | collective-permute-start | bytes 196616 | tf_op jit(solution)/shard_map/ppermute | solution.py:28
  183.2 25.4 %collective-permute-start.6 = (bf16[16,2048]{1,0:T(8,128)(2,1)S(1)}, bf16[16,2048]{1,0:T(8,128)(2,1)S(1)}, u32[]{:S(2)}, u32[]{:S(2)}) collective-permute-start(bf16[16,2048]{1,0:T(8,128)(2,1)S(1)} %get-tuple-element.13), channel_id=1, source_target_pairs={{0,4},{4,8},{8,12},{12,16},{16,20},{20,24},{24,28},{28,32},{32,36}... | collective-permute-start | bytes 196616 | tf_op jit(solution)/shard_map/ppermute | solution.py:26

commit v4 on v3

--- a/solution.py
+++ b/solution.py
@@ -31,13 +31,9 @@
     )
 
 
-def profile_tile(left, right_t, pat):
-    left_f = left.astype(jnp.float32)
-    right_f = right_t.astype(jnp.float32)
-    sq_left = jnp.sum(left_f * left_f, axis=1, keepdims=True)
-    sq_right = jnp.sum(right_f * right_f, axis=0, keepdims=True)
-    cross = jnp.dot(left, right_t, preferred_element_type=jnp.float32)
-    dist = jnp.maximum(sq_left + sq_right - 2.0 * cross, 0.0)
+def profile_tile(left_m2, sq_left, right_t, sq_right):
+    cross = jnp.dot(left_m2, right_t, preferred_element_type=jnp.float32)
+    dist = jnp.maximum((sq_left + sq_right) + cross, 0.0)
     radius = jnp.sqrt(dist)
     base = jnp.maximum(1.0 - radius, 0.0)
     b2 = base * base
@@ -45,19 +41,32 @@
     b8 = b4 * b4
     b16 = b8 * b8
     value = (b16 * b2) * (WEXP * radius + 1.0)
-    return (value * pat).astype(jnp.bfloat16)
-
-
-def build_kernel(pat_ref, pw_ref, pwt_ref, k_ref):
+    return value.astype(jnp.bfloat16)
+
+
+def build_kernel(pat_ref, pw_ref, pwt_ref, sqr_ref, k_ref):
     a = pl.program_id(0)
     start = pl.multiple_of((a + REACH) * BLK, BLK)
     left = pw_ref[pl.ds(start, BLK), :]
+    left_f = left.astype(jnp.float32)
+    sq_left = jnp.sum(left_f * left_f, axis=1, keepdims=True)
+    left_m2 = left * jnp.asarray(-2.0, jnp.bfloat16)
 
     def body(o, carry):
         col = pl.multiple_of((a + o) * BLK, BLK)
-        right_t = pwt_ref[:, pl.ds(col, BLK)]
-        pat = pat_ref[a * WIDE + o].astype(jnp.float32)
-        k_ref[0, :, pl.ds(pl.multiple_of(o * BLK, BLK), BLK)] = profile_tile(left, right_t, pat)
+        dst = pl.ds(pl.multiple_of(o * BLK, BLK), BLK)
+        live = pat_ref[a * WIDE + o] != 0
+
+        @pl.when(live)
+        def _():
+            right_t = pwt_ref[:, pl.ds(col, BLK)]
+            sq_right = sqr_ref[:, pl.ds(col, BLK)]
+            k_ref[0, :, dst] = profile_tile(left_m2, sq_left, right_t, sq_right)
+
+        @pl.when(jnp.logical_not(live))
+        def _():
+            k_ref[0, :, dst] = jnp.zeros((BLK, BLK), jnp.bfloat16)
+
         return carry
 
     lax.fori_loop(0, WIDE, body, 0)
@@ -72,8 +81,11 @@
     )
 
 
-def build_k(pattern_flat, wide_points, wide_points_t, blocks):
+def build_k(pattern_flat, wide_points, blocks):
     wide_rows = wide_points.shape[0]
+    wide_points_t = wide_points.T
+    wide_f = wide_points_t.astype(jnp.float32)
+    sq_row = jnp.sum(wide_f * wide_f, axis=0, keepdims=True)
     return pl.pallas_call(
         build_kernel,
         out_shape=jax.ShapeDtypeStruct((blocks, BLK, WIDE * BLK), jnp.bfloat16),
@@ -83,11 +95,12 @@
             in_specs=[
                 pl.BlockSpec((wide_rows, F), lambda a, p: (0, 0)),
                 pl.BlockSpec((F, wide_rows), lambda a, p: (0, 0)),
+                pl.BlockSpec((1, wide_rows), lambda a, p: (0, 0)),
             ],
             out_specs=pl.BlockSpec((1, BLK, WIDE * BLK), lambda a, p: (a, 0, 0)),
         ),
         compiler_params=pltpu.CompilerParams(dimension_semantics=("arbitrary",)),
-    )(pattern_flat, wide_points, wide_points_t)
+    )(pattern_flat, wide_points, wide_points_t, sq_row)
 
 
 def apply_k(wide_vec, kmat):
@@ -179,7 +192,7 @@
     rim_rows = REACH * BLK
     kernel_scale = 1.0 / (4 * BLK)
     wide_points = with_halo(points, "pts", 0, rim_rows)
-    kmat = build_k(pattern.reshape(-1), wide_points, wide_points.T, block_count)
+    kmat = build_k(pattern.reshape(-1), wide_points, block_count)
 
     rhs_count = lax.axis_size("rhs")
     rhs_index = lax.axis_index("rhs")

time: 229 us -> 207 us (0.904)
  Pallas kernels: 192 us -> 135 us
  starting transfers between devices: 19.5 us -> 53 us
    pallas_call x1, Pallas kernels: 96.7 us -> 36.7 us  [build_k(): pl.pallas_call(build_kernel, out_shape=jax.ShapeDtypeStruct((blocks, BLK,...]
    ppermute x4, starting transfers between devices: 14.3 us -> 47.9 us  [with_halo(): lax.ppermute(tail, axis, [(i, (i + 1) % count) for i in range(ends)])]
    pallas_call x2, Pallas kernels: 50.3 us -> 53.6 us  [all_sum(): pl.pallas_call(functools.partial(sum_kernel, count), out_shape=jax.ShapeD...]
  transfers between devices with their start and end apart: 8 -> 8, of which waited for: 0 -> 1; matrix products, arithmetic and copies ran while one was open for 3% -> 3% of each run, Pallas kernels for 22% -> 26%
where the time goes in v4:
time: 207 us; the launch traced here: 204 us
  Pallas kernels  135 us (65%)
  starting transfers between devices  53 us (26%)
  other arithmetic  10.5 us (5%)
  local copies, waits for them, and re-layouts  3.87 us (2%)
    pallas_call x2, Pallas kernels, all_sum(): pl.pallas_call(functools.partial(sum_kernel, count), out_shape=jax.ShapeD...  53.6 us
    ppermute x4, starting transfers between devices, with_halo(): lax.ppermute(tail, axis, [(i, (i + 1) % count) for i in range(ends)])  47.9 us
    pallas_call x3, Pallas kernels, apply_k(): pl.pallas_call(apply_kernel, out_shape=jax.ShapeDtypeStruct((rows, blocks...  45.3 us
    pallas_call x1, Pallas kernels, build_k(): pl.pallas_call(build_kernel, out_shape=jax.ShapeDtypeStruct((blocks, BLK,...  36.7 us
    ppermute x4, starting transfers between devices, with_halo(): lax.ppermute(head, axis, [((i + 1) % count, i) for i in range(ends)])  5.17 us
  transfers between devices with their start and end apart: 8, of which 1 were waited for; matrix products, arithmetic and copies ran while one was open for 3% of the time, Pallas kernels for 26%

profile of v4, /device:TPU:16, one launch (start us, length us, event | category | flops | bytes accessed | tf_op | source)
XLA Modules:
  0.0 204.0 jit_solution(16034298316251141999)
XLA Ops:
  0.6 0.9 convert_element_type.12
  1.5 1.7 collective-permute-start
  3.3 1.3 collective-permute-start.1
  4.6 4.3 %collective-permute-start.2 = (bf16[2048,32]{0,1:T(8,128)(2,1)}, bf16[2048,32]{0,1:T(8,128)(2,1)S(1)}, u32[]{:S(2)}, u32[]{:S(2)}) collective-permute-start(bf16[2048,32]{0,1:T(8,128)(2,1)} %param.4), channel_id=1, source_target_pairs={{0,4},{4,8},{8,12},{12,16},{16,20},{20,24},{24,28},{28,32},{32,36}... | collective-permute-start | bytes 393224 | tf_op jit(solution)/shard_map/ppermute | solution.py:26
  8.9 1.3 collective-permute-start.3
  10.2 1.4 reshape.75.pat_ref
  11.6 0.0 collective-permute-done
  11.6 0.0 collective-permute-done.1
  11.6 0.7 pad_maximum_fusion.v_ref
  12.3 0.0 collective-permute-done.2
  12.3 0.9 constant_dynamic-update-slice_fusion.1
  13.2 0.4 collective-permute-done.3
  13.6 0.0 copy-start
  13.6 1.5 copy.7.pw_ref
  15.2 0.7 multiply_reduce_fusion
  15.9 0.0 copy-done
  15.9 0.0 copy-start.1
  15.9 0.0 copy-start.3
  15.9 36.7 %shard_map.67.k_ref = bf16[16,128,4224]{2,1,0:T(8,128)(2,1)} custom-call(s32[528]{0:T(1024)} %reshape.75.pat_ref, bf16[6144,32]{1,0:T(8,128)(2,1)} %copy.7.pw_ref, bf16[32,6144]{1,0:T(8,128)(2,1)} %bitcast.30, f32[1,6144]{1,0:T(1,128)} %bitcast.31), custom_call_target="tpu_custom_call" | custom-call | tf_op jit(solution)/shard_map/pallas_call | solution.py:89
  52.6 15.1 %shard_map.68 = f32[16,2048]{1,0:T(8,128)} custom-call(bf16[16,6144]{1,0:T(8,128)(2,1)} %pad_maximum_fusion.v_ref, bf16[16,128,4224]{2,1,0:T(8,128)(2,1)} %shard_map.67.k_ref), custom_call_target="tpu_custom_call" | custom-call | tf_op jit(solution)/shard_map/pallas_call | solution.py:109
  67.6 0.0 copy-done.1
  67.7 0.0 copy-done.3
  67.7 0.9 fusion.5
  68.6 39.8 %collective-permute-start.4 = (bf16[16,2048]{1,0:T(8,128)(2,1)S(1)}, bf16[16,2048]{1,0:T(8,128)(2,1)S(1)}, u32[]{:S(2)}, u32[]{:S(2)}) collective-permute-start(bf16[16,2048]{1,0:T(8,128)(2,1)S(1)} %get-tuple-element.9), channel_id=1, source_target_pairs={{0,4},{4,8},{8,12},{12,16},{16,20},{20,24},{24,28},{28,32},{32,36}... | collective-permute-start | bytes 196616 | tf_op jit(solution)/shard_map/ppermute | solution.py:26
  108.4 1.3 collective-permute-start.5
  109.7 0.1 multiply_reduce_fusion.4
  109.8 0.6 select_maximum_fusion.1.part_ref
  110.4 31.8 %shard_map.69 = f32[8,128]{1,0:T(8,128)} custom-call(f32[8,128]{1,0:T(8,128)} %select_maximum_fusion.1.part_ref), custom_call_target="tpu_custom_call" | custom-call | tf_op jit(solution)/shard_map/pallas_call | solution.py:175
  142.3 0.7 bitcast_divide_fusion.1
  143.0 0.0 collective-permute-done.4
  143.0 0.0 collective-permute-done.5
  143.0 0.7 pad_maximum_fusion.1.v_ref
  143.7 15.1 %shard_map.70 = f32[16,2048]{1,0:T(8,128)} custom-call(bf16[16,6144]{1,0:T(8,128)(2,1)} %pad_maximum_fusion.1.v_ref, bf16[16,128,4224]{2,1,0:T(8,128)(2,1)} %shard_map.67.k_ref), custom_call_target="tpu_custom_call" | custom-call | tf_op jit(solution)/shard_map/pallas_call | solution.py:109
  158.8 0.0 copy-start.2
  158.8 1.2 multiply_reduce_fusion.2
  160.0 2.0 collective-permute-start.6
  162.0 1.3 collective-permute-start.7
  163.3 0.6 select_maximum_fusion.part_ref
  163.9 21.7 %shard_map.71 = f32[8,128]{1,0:T(8,128)} custom-call(f32[8,128]{1,0:T(8,128)} %select_maximum_fusion.part_ref), custom_call_target="tpu_custom_call" | custom-call | tf_op jit(solution)/shard_map/pallas_call | solution.py:175
  185.7 0.8 fusion.1
  186.4 0.0 collective-permute-done.6
  186.4 0.0 collective-permute-done.7
  186.5 0.7 pad_maximum_fusion.2.v_ref
  187.1 15.1 %shard_map.72 = f32[16,2048]{1,0:T(8,128)} custom-call(bf16[16,6144]{1,0:T(8,128)(2,1)} %pad_maximum_fusion.2.v_ref, bf16[16,128,4224]{2,1,0:T(8,128)(2,1)} %shard_map.67.k_ref), custom_call_target="tpu_custom_call" | custom-call | tf_op jit(solution)/shard_map/pallas_call | solution.py:109
  202.2 0.0 copy-done.2
  202.2 1.8 multiply_subtract_fusion
  (2 shorter events, 0.0 us)
Async XLA Ops:
  1.5 10.0 %collective-permute-start = (bf16[16,2048]{1,0:T(8,128)(2,1)S(1)}, bf16[16,2048]{1,0:T(8,128)(2,1)S(1)}, u32[]{:S(2)}, u32[]{:S(2)}) collective-permute-start(bf16[16,2048]{1,0:T(8,128)(2,1)S(1)} %convert_element_type.12), channel_id=1, source_target_pairs={{0,4},{4,8},{8,12},{12,16},{16,20},{20,24},{24,28},{28,32},{32,36}... | collective-permute-start | bytes 196616 | tf_op jit(solution)/shard_map/ppermute | solution.py:26
  3.3 8.3 %collective-permute-start.1 = (bf16[16,2048]{1,0:T(8,128)(2,1)S(1)}, bf16[16,2048]{1,0:T(8,128)(2,1)S(1)}, u32[]{:S(2)}, u32[]{:S(2)}) collective-permute-start(bf16[16,2048]{1,0:T(8,128)(2,1)S(1)} %convert_element_type.12), channel_id=1, source_target_pairs={{4,0},{8,4},{12,8},{16,12},{20,16},{24,20},{28,24},{32,28},{36,32}... | collective-permute-start | bytes 196616 | tf_op jit(solution)/shard_map/ppermute | solution.py:28
  4.6 7.7 %collective-permute-start.2 = (bf16[2048,32]{0,1:T(8,128)(2,1)}, bf16[2048,32]{0,1:T(8,128)(2,1)S(1)}, u32[]{:S(2)}, u32[]{:S(2)}) collective-permute-start(bf16[2048,32]{0,1:T(8,128)(2,1)} %param.4), channel_id=1, source_target_pairs={{0,4},{4,8},{8,12},{12,16},{16,20},{20,24},{24,28},{28,32},{32,36}... | collective-permute-start | bytes 393224 | tf_op jit(solution)/shard_map/ppermute | solution.py:26
  8.9 4.7 %collective-permute-start.3 = (bf16[2048,32]{0,1:T(8,128)(2,1)}, bf16[2048,32]{0,1:T(8,128)(2,1)S(1)}, u32[]{:S(2)}, u32[]{:S(2)}) collective-permute-start(bf16[2048,32]{0,1:T(8,128)(2,1)} %param.4), channel_id=1, source_target_pairs={{4,0},{8,4},{12,8},{16,12},{20,16},{24,20},{28,24},{32,28},{36,32}... | collective-permute-start | bytes 393224 | tf_op jit(solution)/shard_map/ppermute | solution.py:28
  13.6 2.3 %copy-start = (bf16[6144,32]{0,1:T(8,128)(2,1)}, bf16[6144,32]{0,1:T(8,128)(2,1)S(1)}, u32[]{:S(2)}) copy-start(bf16[6144,32]{0,1:T(8,128)(2,1)S(1)} %constant_dynamic-update-slice_fusion) | copy-start | bytes 1179652
  15.9 51.8 %copy-start.1 = (f32[16,2048]{1,0:T(8,128)S(1)}, f32[16,2048]{1,0:T(8,128)}, u32[]{:S(2)}) copy-start(f32[16,2048]{1,0:T(8,128)} %param.6) | copy-start | bytes 393220
  15.9 51.8 %copy-start.3 = (f32[2048]{0:T(1024)S(1)}, f32[2048]{0:T(1024)}, u32[]{:S(2)}) copy-start(f32[2048]{0:T(1024)} %param.5) | copy-start | bytes 24580
  68.6 74.4 %collective-permute-start.4 = (bf16[16,2048]{1,0:T(8,128)(2,1)S(1)}, bf16[16,2048]{1,0:T(8,128)(2,1)S(1)}, u32[]{:S(2)}, u32[]{:S(2)}) collective-permute-start(bf16[16,2048]{1,0:T(8,128)(2,1)S(1)} %get-tuple-element.9), channel_id=1, source_target_pairs={{0,4},{4,8},{8,12},{12,16},{16,20},{20,24},{24,28},{28,32},{32,36}... | collective-permute-start | bytes 196616 | tf_op jit(solution)/shard_map/ppermute | solution.py:26
  108.4 34.6 %collective-permute-start.5 = (bf16[16,2048]{1,0:T(8,128)(2,1)S(1)}, bf16[16,2048]{1,0:T(8,128)(2,1)S(1)}, u32[]{:S(2)}, u32[]{:S(2)}) collective-permute-start(bf16[16,2048]{1,0:T(8,128)(2,1)S(1)} %get-tuple-element.9), channel_id=1, source_target_pairs={{4,0},{8,4},{12,8},{16,12},{20,16},{24,20},{28,24},{32,28},{36,32}... | collective-permute-start | bytes 196616 | tf_op jit(solution)/shard_map/ppermute | solution.py:28
  158.8 43.4 %copy-start.2 = (f32[16,2048]{1,0:T(8,128)S(1)}, f32[16,2048]{1,0:T(8,128)}, u32[]{:S(2)}) copy-start(f32[16,2048]{1,0:T(8,128)} %shard_map.70) | copy-start | bytes 393220
  160.0 26.4 %collective-permute-start.6 = (bf16[16,2048]{1,0:T(8,128)(2,1)S(1)}, bf16[16,2048]{1,0:T(8,128)(2,1)S(1)}, u32[]{:S(2)}, u32[]{:S(2)}) collective-permute-start(bf16[16,2048]{1,0:T(8,128)(2,1)S(1)} %get-tuple-element.13), channel_id=1, source_target_pairs={{0,4},{4,8},{8,12},{12,16},{16,20},{20,24},{24,28},{28,32},{32,36}... | collective-permute-start | bytes 196616 | tf_op jit(solution)/shard_map/ppermute | solution.py:26
  162.0 24.4 %collective-permute-start.7 = (bf16[16,2048]{1,0:T(8,128)(2,1)S(1)}, bf16[16,2048]{1,0:T(8,128)(2,1)S(1)}, u32[]{:S(2)}, u32[]{:S(2)}) collective-permute-start(bf16[16,2048]{1,0:T(8,128)(2,1)S(1)} %get-tuple-element.13), channel_id=1, source_target_pairs={{4,0},{8,4},{12,8},{16,12},{20,16},{24,20},{28,24},{32,28},{36,32}... | collective-permute-start | bytes 196616 | tf_op jit(solution)/shard_map/ppermute | solution.py:28

commit v5 on v4

--- a/solution.py
+++ b/solution.py
@@ -119,68 +119,103 @@
     )(wide_vec, kmat)
 
 
-def sum_kernel(count, part_ref, out_ref, recv, send_sem, recv_sem):
+def sum_kernel(inner, outer, part_ref, out_ref, stage1, stage2, local_sem, send1, recv1, send2, recv2):
     me = lax.axis_index("pts")
     row = lax.axis_index("rhs")
+    zc = me // inner
+    rc = me % inner
 
     barrier = pltpu.get_barrier_semaphore()
 
-    def greet(k, carry):
-        peer = lax.rem(me + k, count)
+    def greet_inner(k, carry):
+        peer = zc * inner + lax.rem(rc + k, inner)
         pl.semaphore_signal(barrier, inc=1, device_id=(peer, row), device_id_type=MESH)
         return carry
 
-    lax.fori_loop(1, count, greet, 0)
-    pl.semaphore_wait(barrier, count - 1)
-
-    def outgoing(peer):
+    def greet_outer(k, carry):
+        peer = lax.rem(zc + k, outer) * inner + rc
+        pl.semaphore_signal(barrier, inc=1, device_id=(peer, row), device_id_type=MESH)
+        return carry
+
+    lax.fori_loop(1, inner, greet_inner, 0)
+    lax.fori_loop(1, outer, greet_outer, 0)
+    pl.semaphore_wait(barrier, (inner - 1) + (outer - 1))
+
+    def first(slot, other):
         return pltpu.make_async_remote_copy(
             src_ref=part_ref,
-            dst_ref=recv.at[me],
-            send_sem=send_sem.at[peer],
-            recv_sem=recv_sem.at[me],
-            device_id=(peer, row),
+            dst_ref=stage1.at[slot],
+            send_sem=send1.at[other],
+            recv_sem=recv1.at[slot],
+            device_id=(zc * inner + other, row),
             device_id_type=MESH,
         )
 
-    def incoming(peer):
+    own1 = pltpu.make_async_copy(part_ref, stage1.at[rc], local_sem.at[0])
+    own1.start()
+
+    def send_first(k, carry):
+        first(rc, lax.rem(rc + k, inner)).start()
+        return carry
+
+    lax.fori_loop(1, inner, send_first, 0)
+
+    def finish_first(k, carry):
+        other = lax.rem(rc + k, inner)
+        first(rc, other).wait_send()
+        first(other, other).wait_recv()
+        return carry
+
+    lax.fori_loop(1, inner, finish_first, 0)
+    own1.wait()
+
+    def second(slot, other):
         return pltpu.make_async_remote_copy(
-            src_ref=part_ref,
-            dst_ref=recv.at[peer],
-            send_sem=send_sem.at[peer],
-            recv_sem=recv_sem.at[peer],
-            device_id=(peer, row),
+            src_ref=stage1,
+            dst_ref=stage2.at[slot],
+            send_sem=send2.at[other],
+            recv_sem=recv2.at[slot],
+            device_id=(other * inner + rc, row),
             device_id_type=MESH,
         )
 
-    def send(k, carry):
-        outgoing(lax.rem(me + k, count)).start()
-        return carry
-
-    lax.fori_loop(1, count, send, 0)
-    recv[me] = part_ref[...]
-
-    def finish(k, carry):
-        peer = lax.rem(me + k, count)
-        outgoing(peer).wait_send()
-        incoming(peer).wait_recv()
-        return carry
-
-    lax.fori_loop(1, count, finish, 0)
-    out_ref[...] = jnp.sum(recv[...], axis=0)
+    own2 = pltpu.make_async_copy(stage1, stage2.at[zc], local_sem.at[1])
+    own2.start()
+
+    def send_second(k, carry):
+        second(zc, lax.rem(zc + k, outer)).start()
+        return carry
+
+    lax.fori_loop(1, outer, send_second, 0)
+
+    def finish_second(k, carry):
+        other = lax.rem(zc + k, outer)
+        second(zc, other).wait_send()
+        second(other, other).wait_recv()
+        return carry
+
+    lax.fori_loop(1, outer, finish_second, 0)
+    own2.wait()
+    out_ref[...] = jnp.sum(jnp.sum(stage2[...], axis=0), axis=0)
 
 
 def all_sum(tile):
     count = lax.axis_size("pts")
+    inner = 8 if count % 8 == 0 else count
+    outer = count // inner
     return pl.pallas_call(
-        functools.partial(sum_kernel, count),
+        functools.partial(sum_kernel, inner, outer),
         out_shape=jax.ShapeDtypeStruct(tile.shape, jnp.float32),
         in_specs=[pl.BlockSpec(memory_space=pltpu.VMEM)],
         out_specs=pl.BlockSpec(memory_space=pltpu.VMEM),
         scratch_shapes=[
-            pltpu.VMEM((count,) + tile.shape, jnp.float32),
-            pltpu.SemaphoreType.DMA((count,)),
-            pltpu.SemaphoreType.DMA((count,)),
+            pltpu.VMEM((inner,) + tile.shape, jnp.float32),
+            pltpu.VMEM((outer, inner) + tile.shape, jnp.float32),
+            pltpu.SemaphoreType.DMA((2,)),
+            pltpu.SemaphoreType.DMA((inner,)),
+            pltpu.SemaphoreType.DMA((inner,)),
+            pltpu.SemaphoreType.DMA((outer,)),
+            pltpu.SemaphoreType.DMA((outer,)),
         ],
         compiler_params=pltpu.CompilerParams(collective_id=0, has_side_effects=True),
     )(tile)

time: 207 us -> 205 us (level)
  starting transfers between devices: 53 us -> 26 us
  Pallas kernels: 135 us -> 161 us
    ppermute x4, starting transfers between devices: 47.9 us -> 20.8 us  [with_halo(): lax.ppermute(tail, axis, [(i, (i + 1) % count) for i in range(ends)])]
    pallas_call x1, Pallas kernels: 36.7 us -> 55 us  [build_k(): pl.pallas_call(build_kernel, out_shape=jax.ShapeDtypeStruct((blocks, BLK,...]
    pallas_call x2, Pallas kernels: 53.6 us -> 60.2 us  [all_sum(): pl.pallas_call(functools.partial(sum_kernel, inner, outer), out_shape=jax...]
  transfers between devices with their start and end apart: 8 -> 8, of which waited for: 1 -> 1; matrix products, arithmetic and copies ran while one was open for 3% -> 3% of each run, Pallas kernels for 26% -> 30%
where the time goes in v5:
time: 205 us; the launch traced here: 202 us
  Pallas kernels  161 us (79%)
  starting transfers between devices  26 us (13%)
  other arithmetic  10.5 us (5%)
  local copies, waits for them, and re-layouts  3.87 us (2%)
    pallas_call x2, Pallas kernels, all_sum(): pl.pallas_call(functools.partial(sum_kernel, inner, outer), out_shape=jax...  60.2 us
    pallas_call x1, Pallas kernels, build_k(): pl.pallas_call(build_kernel, out_shape=jax.ShapeDtypeStruct((blocks, BLK,...  55 us
    pallas_call x3, Pallas kernels, apply_k(): pl.pallas_call(apply_kernel, out_shape=jax.ShapeDtypeStruct((rows, blocks...  45.3 us
    ppermute x4, starting transfers between devices, with_halo(): lax.ppermute(tail, axis, [(i, (i + 1) % count) for i in range(ends)])  20.8 us
    ppermute x4, starting transfers between devices, with_halo(): lax.ppermute(head, axis, [((i + 1) % count, i) for i in range(ends)])  5.17 us
  transfers between devices with their start and end apart: 8, of which 1 were waited for; matrix products, arithmetic and copies ran while one was open for 3% of the time, Pallas kernels for 30%

profile of v5, /device:TPU:16, one launch (start us, length us, event | category | flops | bytes accessed | tf_op | source)
XLA Modules:
  0.0 202.0 jit_solution(13801184010994813988)
XLA Ops:
  0.6 0.9 convert_element_type.12
  1.5 1.7 collective-permute-start
  3.3 1.3 collective-permute-start.1
  4.6 4.3 %collective-permute-start.2 = (bf16[2048,32]{0,1:T(8,128)(2,1)}, bf16[2048,32]{0,1:T(8,128)(2,1)S(1)}, u32[]{:S(2)}, u32[]{:S(2)}) collective-permute-start(bf16[2048,32]{0,1:T(8,128)(2,1)} %param.4), channel_id=1, source_target_pairs={{0,4},{4,8},{8,12},{12,16},{16,20},{20,24},{24,28},{28,32},{32,36}... | collective-permute-start | bytes 393224 | tf_op jit(solution)/shard_map/ppermute | solution.py:26
  8.9 1.3 collective-permute-start.3
  10.2 1.4 reshape.75.pat_ref
  11.6 0.0 collective-permute-done
  11.6 0.0 collective-permute-done.1
  11.6 0.7 pad_maximum_fusion.v_ref
  12.3 0.0 collective-permute-done.2
  12.3 0.9 constant_dynamic-update-slice_fusion.1
  13.2 0.4 collective-permute-done.3
  13.6 0.0 copy-start
  13.6 1.5 copy.7.pw_ref
  15.2 0.7 multiply_reduce_fusion
  15.9 0.0 copy-done
  15.9 0.0 copy-start.1
  15.9 0.0 copy-start.3
  15.9 55.0 %shard_map.67.k_ref = bf16[16,128,4224]{2,1,0:T(8,128)(2,1)} custom-call(s32[528]{0:T(1024)} %reshape.75.pat_ref, bf16[6144,32]{1,0:T(8,128)(2,1)} %copy.7.pw_ref, bf16[32,6144]{1,0:T(8,128)(2,1)} %bitcast.30, f32[1,6144]{1,0:T(1,128)} %bitcast.31), custom_call_target="tpu_custom_call" | custom-call | tf_op jit(solution)/shard_map/pallas_call | solution.py:89
  70.9 15.1 %shard_map.68 = f32[16,2048]{1,0:T(8,128)} custom-call(bf16[16,6144]{1,0:T(8,128)(2,1)} %pad_maximum_fusion.v_ref, bf16[16,128,4224]{2,1,0:T(8,128)(2,1)} %shard_map.67.k_ref), custom_call_target="tpu_custom_call" | custom-call | tf_op jit(solution)/shard_map/pallas_call | solution.py:109
  86.0 0.0 copy-done.1
  86.0 0.0 copy-done.3
  86.0 0.9 fusion.5
  86.9 13.4 %collective-permute-start.4 = (bf16[16,2048]{1,0:T(8,128)(2,1)S(1)}, bf16[16,2048]{1,0:T(8,128)(2,1)S(1)}, u32[]{:S(2)}, u32[]{:S(2)}) collective-permute-start(bf16[16,2048]{1,0:T(8,128)(2,1)S(1)} %get-tuple-element.9), channel_id=1, source_target_pairs={{0,4},{4,8},{8,12},{12,16},{16,20},{20,24},{24,28},{28,32},{32,36}... | collective-permute-start | bytes 196616 | tf_op jit(solution)/shard_map/ppermute | solution.py:26
  100.3 1.3 collective-permute-start.5
  101.6 0.1 multiply_reduce_fusion.4
  101.8 0.6 select_maximum_fusion.1.part_ref
  102.4 37.7 %shard_map.69 = f32[8,128]{1,0:T(8,128)} custom-call(f32[8,128]{1,0:T(8,128)} %select_maximum_fusion.1.part_ref), custom_call_target="tpu_custom_call" | custom-call | tf_op jit(solution)/shard_map/pallas_call | solution.py:206
  140.1 0.7 bitcast_divide_fusion.1
  140.8 0.0 collective-permute-done.4
  140.8 0.0 collective-permute-done.5
  140.8 0.7 pad_maximum_fusion.1.v_ref
  141.5 15.1 %shard_map.70 = f32[16,2048]{1,0:T(8,128)} custom-call(bf16[16,6144]{1,0:T(8,128)(2,1)} %pad_maximum_fusion.1.v_ref, bf16[16,128,4224]{2,1,0:T(8,128)(2,1)} %shard_map.67.k_ref), custom_call_target="tpu_custom_call" | custom-call | tf_op jit(solution)/shard_map/pallas_call | solution.py:109
  156.6 0.0 copy-start.2
  156.6 1.2 multiply_reduce_fusion.2
  157.8 1.4 collective-permute-start.6
  159.2 1.3 collective-permute-start.7
  160.5 0.6 select_maximum_fusion.part_ref
  161.1 22.6 %shard_map.71 = f32[8,128]{1,0:T(8,128)} custom-call(f32[8,128]{1,0:T(8,128)} %select_maximum_fusion.part_ref), custom_call_target="tpu_custom_call" | custom-call | tf_op jit(solution)/shard_map/pallas_call | solution.py:206
  183.7 0.8 fusion.1
  184.4 0.0 collective-permute-done.6
  184.5 0.0 collective-permute-done.7
  184.5 0.7 pad_maximum_fusion.2.v_ref
  185.2 15.1 %shard_map.72 = f32[16,2048]{1,0:T(8,128)} custom-call(bf16[16,6144]{1,0:T(8,128)(2,1)} %pad_maximum_fusion.2.v_ref, bf16[16,128,4224]{2,1,0:T(8,128)(2,1)} %shard_map.67.k_ref), custom_call_target="tpu_custom_call" | custom-call | tf_op jit(solution)/shard_map/pallas_call | solution.py:109
  200.2 0.0 copy-done.2
  200.2 1.8 multiply_subtract_fusion
  (2 shorter events, 0.0 us)
Async XLA Ops:
  1.5 10.0 %collective-permute-start = (bf16[16,2048]{1,0:T(8,128)(2,1)S(1)}, bf16[16,2048]{1,0:T(8,128)(2,1)S(1)}, u32[]{:S(2)}, u32[]{:S(2)}) collective-permute-start(bf16[16,2048]{1,0:T(8,128)(2,1)S(1)} %convert_element_type.12), channel_id=1, source_target_pairs={{0,4},{4,8},{8,12},{12,16},{16,20},{20,24},{24,28},{28,32},{32,36}... | collective-permute-start | bytes 196616 | tf_op jit(solution)/shard_map/ppermute | solution.py:26
  3.3 8.3 %collective-permute-start.1 = (bf16[16,2048]{1,0:T(8,128)(2,1)S(1)}, bf16[16,2048]{1,0:T(8,128)(2,1)S(1)}, u32[]{:S(2)}, u32[]{:S(2)}) collective-permute-start(bf16[16,2048]{1,0:T(8,128)(2,1)S(1)} %convert_element_type.12), channel_id=1, source_target_pairs={{4,0},{8,4},{12,8},{16,12},{20,16},{24,20},{28,24},{32,28},{36,32}... | collective-permute-start | bytes 196616 | tf_op jit(solution)/shard_map/ppermute | solution.py:28
  4.6 7.7 %collective-permute-start.2 = (bf16[2048,32]{0,1:T(8,128)(2,1)}, bf16[2048,32]{0,1:T(8,128)(2,1)S(1)}, u32[]{:S(2)}, u32[]{:S(2)}) collective-permute-start(bf16[2048,32]{0,1:T(8,128)(2,1)} %param.4), channel_id=1, source_target_pairs={{0,4},{4,8},{8,12},{12,16},{16,20},{20,24},{24,28},{28,32},{32,36}... | collective-permute-start | bytes 393224 | tf_op jit(solution)/shard_map/ppermute | solution.py:26
  8.9 4.7 %collective-permute-start.3 = (bf16[2048,32]{0,1:T(8,128)(2,1)}, bf16[2048,32]{0,1:T(8,128)(2,1)S(1)}, u32[]{:S(2)}, u32[]{:S(2)}) collective-permute-start(bf16[2048,32]{0,1:T(8,128)(2,1)} %param.4), channel_id=1, source_target_pairs={{4,0},{8,4},{12,8},{16,12},{20,16},{24,20},{28,24},{32,28},{36,32}... | collective-permute-start | bytes 393224 | tf_op jit(solution)/shard_map/ppermute | solution.py:28
  13.6 2.3 %copy-start = (bf16[6144,32]{0,1:T(8,128)(2,1)}, bf16[6144,32]{0,1:T(8,128)(2,1)S(1)}, u32[]{:S(2)}) copy-start(bf16[6144,32]{0,1:T(8,128)(2,1)S(1)} %constant_dynamic-update-slice_fusion) | copy-start | bytes 1179652
  15.9 70.1 %copy-start.1 = (f32[16,2048]{1,0:T(8,128)S(1)}, f32[16,2048]{1,0:T(8,128)}, u32[]{:S(2)}) copy-start(f32[16,2048]{1,0:T(8,128)} %param.6) | copy-start | bytes 393220
  15.9 70.1 %copy-start.3 = (f32[2048]{0:T(1024)S(1)}, f32[2048]{0:T(1024)}, u32[]{:S(2)}) copy-start(f32[2048]{0:T(1024)} %param.5) | copy-start | bytes 24580
  86.9 53.9 %collective-permute-start.4 = (bf16[16,2048]{1,0:T(8,128)(2,1)S(1)}, bf16[16,2048]{1,0:T(8,128)(2,1)S(1)}, u32[]{:S(2)}, u32[]{:S(2)}) collective-permute-start(bf16[16,2048]{1,0:T(8,128)(2,1)S(1)} %get-tuple-element.9), channel_id=1, source_target_pairs={{0,4},{4,8},{8,12},{12,16},{16,20},{20,24},{24,28},{28,32},{32,36}... | collective-permute-start | bytes 196616 | tf_op jit(solution)/shard_map/ppermute | solution.py:26
  100.3 40.5 %collective-permute-start.5 = (bf16[16,2048]{1,0:T(8,128)(2,1)S(1)}, bf16[16,2048]{1,0:T(8,128)(2,1)S(1)}, u32[]{:S(2)}, u32[]{:S(2)}) collective-permute-start(bf16[16,2048]{1,0:T(8,128)(2,1)S(1)} %get-tuple-element.9), channel_id=1, source_target_pairs={{4,0},{8,4},{12,8},{16,12},{20,16},{24,20},{28,24},{32,28},{36,32}... | collective-permute-start | bytes 196616 | tf_op jit(solution)/shard_map/ppermute | solution.py:28
  156.6 43.6 %copy-start.2 = (f32[16,2048]{1,0:T(8,128)S(1)}, f32[16,2048]{1,0:T(8,128)}, u32[]{:S(2)}) copy-start(f32[16,2048]{1,0:T(8,128)} %shard_map.70) | copy-start | bytes 393220
  157.8 26.7 %collective-permute-start.6 = (bf16[16,2048]{1,0:T(8,128)(2,1)S(1)}, bf16[16,2048]{1,0:T(8,128)(2,1)S(1)}, u32[]{:S(2)}, u32[]{:S(2)}) collective-permute-start(bf16[16,2048]{1,0:T(8,128)(2,1)S(1)} %get-tuple-element.13), channel_id=1, source_target_pairs={{0,4},{4,8},{8,12},{12,16},{16,20},{20,24},{24,28},{28,32},{32,36}... | collective-permute-start | bytes 196616 | tf_op jit(solution)/shard_map/ppermute | solution.py:26
  159.2 25.3 %collective-permute-start.7 = (bf16[16,2048]{1,0:T(8,128)(2,1)S(1)}, bf16[16,2048]{1,0:T(8,128)(2,1)S(1)}, u32[]{:S(2)}, u32[]{:S(2)}) collective-permute-start(bf16[16,2048]{1,0:T(8,128)(2,1)S(1)} %get-tuple-element.13), channel_id=1, source_target_pairs={{4,0},{8,4},{12,8},{16,12},{20,16},{24,20},{28,24},{32,28},{36,32}... | collective-permute-start | bytes 196616 | tf_op jit(solution)/shard_map/ppermute | solution.py:28

commit v6 on v5

--- a/solution.py
+++ b/solution.py
@@ -119,27 +119,27 @@
     )(wide_vec, kmat)
 
 
-def sum_kernel(inner, outer, part_ref, out_ref, stage1, stage2, local_sem, send1, recv1, send2, recv2):
+def reduction_steps(inner, outer, part_ref, stage1, stage2, local_sem, send1, recv1, send2, recv2):
     me = lax.axis_index("pts")
     row = lax.axis_index("rhs")
     zc = me // inner
     rc = me % inner
 
-    barrier = pltpu.get_barrier_semaphore()
-
-    def greet_inner(k, carry):
-        peer = zc * inner + lax.rem(rc + k, inner)
-        pl.semaphore_signal(barrier, inc=1, device_id=(peer, row), device_id_type=MESH)
-        return carry
-
-    def greet_outer(k, carry):
-        peer = lax.rem(zc + k, outer) * inner + rc
-        pl.semaphore_signal(barrier, inc=1, device_id=(peer, row), device_id_type=MESH)
-        return carry
-
-    lax.fori_loop(1, inner, greet_inner, 0)
-    lax.fori_loop(1, outer, greet_outer, 0)
-    pl.semaphore_wait(barrier, (inner - 1) + (outer - 1))
+    def greet():
+        barrier = pltpu.get_barrier_semaphore()
+
+        def greet_inner(k, carry):
+            peer = zc * inner + lax.rem(rc + k, inner)
+            pl.semaphore_signal(barrier, inc=1, device_id=(peer, row), device_id_type=MESH)
+            return carry
+
+        def greet_outer(k, carry):
+            peer = lax.rem(zc + k, outer) * inner + rc
+            pl.semaphore_signal(barrier, inc=1, device_id=(peer, row), device_id_type=MESH)
+            return carry
+
+        lax.fori_loop(1, inner, greet_inner, 0)
+        lax.fori_loop(1, outer, greet_outer, 0)
 
     def first(slot, other):
         return pltpu.make_async_remote_copy(
@@ -151,24 +151,6 @@
             device_id_type=MESH,
         )
 
-    own1 = pltpu.make_async_copy(part_ref, stage1.at[rc], local_sem.at[0])
-    own1.start()
-
-    def send_first(k, carry):
-        first(rc, lax.rem(rc + k, inner)).start()
-        return carry
-
-    lax.fori_loop(1, inner, send_first, 0)
-
-    def finish_first(k, carry):
-        other = lax.rem(rc + k, inner)
-        first(rc, other).wait_send()
-        first(other, other).wait_recv()
-        return carry
-
-    lax.fori_loop(1, inner, finish_first, 0)
-    own1.wait()
-
     def second(slot, other):
         return pltpu.make_async_remote_copy(
             src_ref=stage1,
@@ -179,35 +161,102 @@
             device_id_type=MESH,
         )
 
+    own1 = pltpu.make_async_copy(part_ref, stage1.at[rc], local_sem.at[0])
     own2 = pltpu.make_async_copy(stage1, stage2.at[zc], local_sem.at[1])
-    own2.start()
-
-    def send_second(k, carry):
-        second(zc, lax.rem(zc + k, outer)).start()
-        return carry
-
-    lax.fori_loop(1, outer, send_second, 0)
-
-    def finish_second(k, carry):
-        other = lax.rem(zc + k, outer)
-        second(zc, other).wait_send()
-        second(other, other).wait_recv()
-        return carry
-
-    lax.fori_loop(1, outer, finish_second, 0)
-    own2.wait()
-    out_ref[...] = jnp.sum(jnp.sum(stage2[...], axis=0), axis=0)
-
-
-def all_sum(tile):
+
+    def start_first():
+        pl.semaphore_wait(pltpu.get_barrier_semaphore(), (inner - 1) + (outer - 1))
+        own1.start()
+
+        def send_first(k, carry):
+            first(rc, lax.rem(rc + k, inner)).start()
+            return carry
+
+        lax.fori_loop(1, inner, send_first, 0)
+
+    def start_second():
+        def finish_first(k, carry):
+            other = lax.rem(rc + k, inner)
+            first(rc, other).wait_send()
+            first(other, other).wait_recv()
+            return carry
+
+        lax.fori_loop(1, inner, finish_first, 0)
+        own1.wait()
+        own2.start()
+
+        def send_second(k, carry):
+            second(zc, lax.rem(zc + k, outer)).start()
+            return carry
+
+        lax.fori_loop(1, outer, send_second, 0)
+
+    def finish():
+        def finish_second(k, carry):
+            other = lax.rem(zc + k, outer)
+            second(zc, other).wait_send()
+            second(other, other).wait_recv()
+            return carry
+
+        lax.fori_loop(1, outer, finish_second, 0)
+        own2.wait()
+        return jnp.sum(jnp.sum(stage2[...], axis=0), axis=0)
+
+    return greet, start_first, start_second, finish
+
+
+def apply_sum_kernel(inner, outer, v_ref, k_ref, part_ref, out_ref, sum_ref, *scratch):
+    a = pl.program_id(0)
+    last = pl.num_programs(0) - 1
+    greet, start_first, start_second, finish = reduction_steps(inner, outer, part_ref, *scratch)
+
+    @pl.when(a == 0)
+    def _():
+        greet()
+
+    blocks = v_ref.shape[1] // BLK - 2 * REACH
+
+    @pl.when(a == min(2, blocks - 1))
+    def _():
+        start_first()
+
+    @pl.when(a == min(blocks // 2, blocks - 1))
+    def _():
+        start_second()
+
+    start = pl.multiple_of(a * BLK, BLK)
+    v_cat = v_ref[:, pl.ds(start, WIDE * BLK)]
+    out_ref[...] = lax.dot_general(
+        v_cat, k_ref[0], (((1,), (1,)), ((), ())), preferred_element_type=jnp.float32
+    )
+
+    @pl.when(a == last)
+    def _():
+        sum_ref[...] = finish()
+
+
+def apply_sum(wide_vec, kmat, tile):
+    rows, wide_cols = wide_vec.shape
+    blocks = kmat.shape[0]
     count = lax.axis_size("pts")
     inner = 8 if count % 8 == 0 else count
     outer = count // inner
     return pl.pallas_call(
-        functools.partial(sum_kernel, inner, outer),
-        out_shape=jax.ShapeDtypeStruct(tile.shape, jnp.float32),
-        in_specs=[pl.BlockSpec(memory_space=pltpu.VMEM)],
-        out_specs=pl.BlockSpec(memory_space=pltpu.VMEM),
+        functools.partial(apply_sum_kernel, inner, outer),
+        out_shape=(
+            jax.ShapeDtypeStruct((rows, blocks * BLK), jnp.float32),
+            jax.ShapeDtypeStruct(tile.shape, jnp.float32),
+        ),
+        grid=(blocks,),
+        in_specs=[
+            pl.BlockSpec((rows, wide_cols), lambda a: (0, 0)),
+            pl.BlockSpec((1, BLK, WIDE * BLK), lambda a: (a, 0, 0)),
+            pl.BlockSpec(tile.shape, lambda a: (0, 0)),
+        ],
+        out_specs=(
+            pl.BlockSpec((rows, BLK), lambda a: (0, a)),
+            pl.BlockSpec(tile.shape, lambda a: (0, 0)),
+        ),
         scratch_shapes=[
             pltpu.VMEM((inner,) + tile.shape, jnp.float32),
             pltpu.VMEM((outer, inner) + tile.shape, jnp.float32),
@@ -217,8 +266,10 @@
             pltpu.SemaphoreType.DMA((outer,)),
             pltpu.SemaphoreType.DMA((outer,)),
         ],
-        compiler_params=pltpu.CompilerParams(collective_id=0, has_side_effects=True),
-    )(tile)
+        compiler_params=pltpu.CompilerParams(
+            dimension_semantics=("arbitrary",), collective_id=0, has_side_effects=True
+        ),
+    )(wide_vec, kmat, tile)
 
 
 def per_device(points, noise_var, right_side, pattern):
@@ -232,17 +283,20 @@
     rhs_count = lax.axis_size("rhs")
     rhs_index = lax.axis_index("rhs")
 
-    def total(parts):
-        tile = jnp.zeros((8, 128), jnp.float32)
-        tile = lax.dynamic_update_slice(tile, parts, (0, 0))
-        summed = all_sum(tile)
-        return summed[: parts.shape[0], : parts.shape[1]]
-
     def apply_operator(vector):
         vec_low = vector.astype(jnp.bfloat16)
         wide_vec = with_halo(vec_low, "pts", 1, rim_rows)
         image_part = apply_k(wide_vec, kmat)
         return noise_var[None, :] * vector + kernel_scale * image_part
+
+    def apply_and_total(vector, parts):
+        tile = jnp.zeros((8, 128), jnp.float32)
+        tile = lax.dynamic_update_slice(tile, parts, (0, 0))
+        vec_low = vector.astype(jnp.bfloat16)
+        wide_vec = with_halo(vec_low, "pts", 1, rim_rows)
+        image_part, summed = apply_sum(wide_vec, kmat, tile)
+        image = noise_var[None, :] * vector + kernel_scale * image_part
+        return image, summed[: parts.shape[0], : parts.shape[1]]
 
     solution = jnp.zeros_like(right_side)
     residual = right_side
@@ -253,12 +307,12 @@
     norm_prev = None
     step_prev = None
     for iteration in range(ITERS):
-        sums = total(
-            jnp.stack([jnp.sum(residual * residual, axis=1), jnp.sum(res_image * residual, axis=1)])
+        square_image, sums = apply_and_total(
+            res_image,
+            jnp.stack([jnp.sum(residual * residual, axis=1), jnp.sum(res_image * residual, axis=1)]),
         )
         norm_now = sums[0][:, None]
         curvature = sums[1][:, None]
-        square_image = apply_operator(res_image)
         if iteration == 0:
             step_len = norm_now / curvature
             direction = residual

time: 205 us -> 183 us (0.89)
  Pallas kernels: 161 us -> 139 us
  waiting for transfers between devices: 0.38 us -> 10.1 us
  starting transfers between devices: 26 us -> 17 us
    pallas_call x3 -> x1, Pallas kernels: 45.3 us -> 15.1 us  [apply_k(): pl.pallas_call(apply_kernel, out_shape=jax.ShapeDtypeStruct((rows, blocks...]
    ppermute x4, waiting for transfers between devices: 0.37 us -> 10.1 us  [with_halo(): lax.ppermute(head, axis, [((i + 1) % count, i) for i in range(ends)])]
    pallas_call x2, Pallas kernels: 60.2 us -> 69.7 us  [apply_sum(): pl.pallas_call(functools.partial(apply_sum_kernel, inner, outer), out_sha...]
    ppermute x4, starting transfers between devices: 20.8 us -> 11.8 us  [with_halo(): lax.ppermute(tail, axis, [(i, (i + 1) % count) for i in range(ends)])]
  transfers between devices with their start and end apart: 8 -> 8, of which waited for: 1 -> 3; matrix products, arithmetic and copies ran while one was open for 3% -> 2% of each run, Pallas kernels for 30% -> 0%
where the time goes in v6:
time: 183 us; the launch traced here: 182 us
  Pallas kernels  139 us (76%)
  starting transfers between devices  17 us (9%)
  other arithmetic  10.4 us (6%)
  waiting for transfers between devices  10.1 us (6%)
  local copies, waits for them, and re-layouts  3.85 us (2%)
    pallas_call x2, Pallas kernels, apply_sum(): pl.pallas_call(functools.partial(apply_sum_kernel, inner, outer), out_sha...  69.7 us
    pallas_call x1, Pallas kernels, build_k(): pl.pallas_call(build_kernel, out_shape=jax.ShapeDtypeStruct((blocks, BLK,...  54.7 us
    pallas_call x1, Pallas kernels, apply_k(): pl.pallas_call(apply_kernel, out_shape=jax.ShapeDtypeStruct((rows, blocks...  15.1 us
    ppermute x4, starting transfers between devices, with_halo(): lax.ppermute(tail, axis, [(i, (i + 1) % count) for i in range(ends)])  11.8 us
    ppermute x4, waiting for transfers between devices, with_halo(): lax.ppermute(head, axis, [((i + 1) % count, i) for i in range(ends)])  10.1 us
    ppermute x4, starting transfers between devices, with_halo(): lax.ppermute(head, axis, [((i + 1) % count, i) for i in range(ends)])  5.17 us
  transfers between devices with their start and end apart: 8, of which 3 were waited for; matrix products, arithmetic and copies ran while one was open for 2% of the time, Pallas kernels for 0%

profile of v6, /device:TPU:16, one launch (start us, length us, event | category | flops | bytes accessed | tf_op | source)
XLA Modules:
  0.0 181.5 jit_solution(1103699298673520496)
XLA Ops:
  0.6 0.9 convert_element_type.12
  1.5 1.7 collective-permute-start
  3.3 1.3 collective-permute-start.1
  4.6 4.3 %collective-permute-start.2 = (bf16[2048,32]{0,1:T(8,128)(2,1)}, bf16[2048,32]{0,1:T(8,128)(2,1)S(1)}, u32[]{:S(2)}, u32[]{:S(2)}) collective-permute-start(bf16[2048,32]{0,1:T(8,128)(2,1)} %param.4), channel_id=1, source_target_pairs={{0,4},{4,8},{8,12},{12,16},{16,20},{20,24},{24,28},{28,32},{32,36}... | collective-permute-start | bytes 393224 | tf_op jit(solution)/shard_map/ppermute | solution.py:26
  8.9 1.3 collective-permute-start.3
  10.2 1.4 reshape.75.pat_ref
  11.6 0.0 collective-permute-done
  11.6 0.0 collective-permute-done.1
  11.6 0.7 pad_maximum_fusion.v_ref
  12.3 0.0 collective-permute-done.2
  12.3 0.9 constant_dynamic-update-slice_fusion.1
  13.2 0.4 collective-permute-done.3
  13.6 0.0 copy-start
  13.6 1.5 copy.7.pw_ref
  15.1 0.7 multiply_reduce_fusion
  15.9 0.0 copy-done
  15.9 0.0 copy-start.1
  15.9 0.0 copy-start.3
  15.9 54.7 %shard_map.67.k_ref = bf16[16,128,4224]{2,1,0:T(8,128)(2,1)} custom-call(s32[528]{0:T(1024)} %reshape.75.pat_ref, bf16[6144,32]{1,0:T(8,128)(2,1)} %copy.7.pw_ref, bf16[32,6144]{1,0:T(8,128)(2,1)} %bitcast.30, f32[1,6144]{1,0:T(1,128)} %bitcast.31), custom_call_target="tpu_custom_call" | custom-call | tf_op jit(solution)/shard_map/pallas_call | solution.py:89
  70.5 15.1 %shard_map.68 = f32[16,2048]{1,0:T(8,128)} custom-call(bf16[16,6144]{1,0:T(8,128)(2,1)} %pad_maximum_fusion.v_ref, bf16[16,128,4224]{2,1,0:T(8,128)(2,1)} %shard_map.67.k_ref), custom_call_target="tpu_custom_call" | custom-call | tf_op jit(solution)/shard_map/pallas_call | solution.py:109
  85.6 0.0 copy-done.1
  85.6 0.0 copy-done.3
  85.6 1.0 multiply_reduce_fusion.4
  86.7 4.5 %collective-permute-start.4 = (bf16[16,2048]{1,0:T(8,128)(2,1)S(1)}, bf16[16,2048]{1,0:T(8,128)(2,1)S(1)}, u32[]{:S(2)}, u32[]{:S(2)}) collective-permute-start(bf16[16,2048]{1,0:T(8,128)(2,1)S(1)} %convert_element_type.14), channel_id=1, source_target_pairs={{0,4},{4,8},{8,12},{12,16},{16,20},{20,24},{24,28},{28,32},{32,36}... | collective-permute-start | bytes 196616 | tf_op jit(solution)/shard_map/ppermute | solution.py:26
  91.2 1.3 collective-permute-start.5
  92.5 0.6 select_maximum_fusion.1.part_ref
  93.1 0.0 collective-permute-done.4
  93.1 7.3 %collective-permute-done.5 = bf16[16,2048]{1,0:T(8,128)(2,1)S(1)} collective-permute-done((bf16[16,2048]{1,0:T(8,128)(2,1)S(1)}, bf16[16,2048]{1,0:T(8,128)(2,1)S(1)}, u32[]{:S(2)}, u32[]{:S(2)}) %collective-permute-start.5) | collective-permute-done | bytes 65568 | tf_op jit(solution)/shard_map/ppermute | solution.py:28
  100.4 0.7 pad_maximum_fusion.1.v_ref
  101.1 44.2 %shard_map.69 = (f32[16,2048]{1,0:T(8,128)}, f32[8,128]{1,0:T(8,128)}) custom-call(bf16[16,6144]{1,0:T(8,128)(2,1)} %pad_maximum_fusion.1.v_ref, bf16[16,128,4224]{2,1,0:T(8,128)(2,1)} %shard_map.67.k_ref, f32[8,128]{1,0:T(8,128)} %select_maximum_fusion.1.part_ref), custom_call_target="tpu_custom_call" | custom-call | tf_op jit(solution)/shard_map/pallas_call | solution.py:244
  145.3 0.0 copy-start.2
  145.3 0.8 bitcast_divide_fusion.1
  146.1 1.1 multiply_reduce_fusion.2
  147.2 1.3 collective-permute-start.6
  148.5 1.3 collective-permute-start.7
  149.8 0.6 select_maximum_fusion.part_ref
  150.4 0.0 collective-permute-done.6
  150.4 2.3 %collective-permute-done.7 = bf16[16,2048]{1,0:T(8,128)(2,1)S(1)} collective-permute-done((bf16[16,2048]{1,0:T(8,128)(2,1)S(1)}, bf16[16,2048]{1,0:T(8,128)(2,1)S(1)}, u32[]{:S(2)}, u32[]{:S(2)}) %collective-permute-start.7) | collective-permute-done | bytes 65568 | tf_op jit(solution)/shard_map/ppermute | solution.py:28
  152.8 0.7 pad_maximum_fusion.2.v_ref
  153.4 25.5 %shard_map.70 = (f32[16,2048]{1,0:T(8,128)}, f32[8,128]{1,0:T(8,128)}) custom-call(bf16[16,6144]{1,0:T(8,128)(2,1)} %pad_maximum_fusion.2.v_ref, bf16[16,128,4224]{2,1,0:T(8,128)(2,1)} %shard_map.67.k_ref, f32[8,128]{1,0:T(8,128)} %select_maximum_fusion.part_ref), custom_call_target="tpu_custom_call" | custom-call | tf_op jit(solution)/shard_map/pallas_call | solution.py:244
  179.0 0.8 fusion.1
  179.8 0.0 copy-done.2
  179.8 1.8 multiply_subtract_fusion
  (3 shorter events, 0.0 us)
Async XLA Ops:
  1.5 10.0 %collective-permute-start = (bf16[16,2048]{1,0:T(8,128)(2,1)S(1)}, bf16[16,2048]{1,0:T(8,128)(2,1)S(1)}, u32[]{:S(2)}, u32[]{:S(2)}) collective-permute-start(bf16[16,2048]{1,0:T(8,128)(2,1)S(1)} %convert_element_type.12), channel_id=1, source_target_pairs={{0,4},{4,8},{8,12},{12,16},{16,20},{20,24},{24,28},{28,32},{32,36}... | collective-permute-start | bytes 196616 | tf_op jit(solution)/shard_map/ppermute | solution.py:26
  3.3 8.3 %collective-permute-start.1 = (bf16[16,2048]{1,0:T(8,128)(2,1)S(1)}, bf16[16,2048]{1,0:T(8,128)(2,1)S(1)}, u32[]{:S(2)}, u32[]{:S(2)}) collective-permute-start(bf16[16,2048]{1,0:T(8,128)(2,1)S(1)} %convert_element_type.12), channel_id=1, source_target_pairs={{4,0},{8,4},{12,8},{16,12},{20,16},{24,20},{28,24},{32,28},{36,32}... | collective-permute-start | bytes 196616 | tf_op jit(solution)/shard_map/ppermute | solution.py:28
  4.6 7.7 %collective-permute-start.2 = (bf16[2048,32]{0,1:T(8,128)(2,1)}, bf16[2048,32]{0,1:T(8,128)(2,1)S(1)}, u32[]{:S(2)}, u32[]{:S(2)}) collective-permute-start(bf16[2048,32]{0,1:T(8,128)(2,1)} %param.4), channel_id=1, source_target_pairs={{0,4},{4,8},{8,12},{12,16},{16,20},{20,24},{24,28},{28,32},{32,36}... | collective-permute-start | bytes 393224 | tf_op jit(solution)/shard_map/ppermute | solution.py:26
  8.9 4.7 %collective-permute-start.3 = (bf16[2048,32]{0,1:T(8,128)(2,1)}, bf16[2048,32]{0,1:T(8,128)(2,1)S(1)}, u32[]{:S(2)}, u32[]{:S(2)}) collective-permute-start(bf16[2048,32]{0,1:T(8,128)(2,1)} %param.4), channel_id=1, source_target_pairs={{4,0},{8,4},{12,8},{16,12},{20,16},{24,20},{28,24},{32,28},{36,32}... | collective-permute-start | bytes 393224 | tf_op jit(solution)/shard_map/ppermute | solution.py:28
  13.6 2.3 %copy-start = (bf16[6144,32]{0,1:T(8,128)(2,1)}, bf16[6144,32]{0,1:T(8,128)(2,1)S(1)}, u32[]{:S(2)}) copy-start(bf16[6144,32]{0,1:T(8,128)(2,1)S(1)} %constant_dynamic-update-slice_fusion) | copy-start | bytes 1179652
  15.9 69.8 %copy-start.1 = (f32[16,2048]{1,0:T(8,128)S(1)}, f32[16,2048]{1,0:T(8,128)}, u32[]{:S(2)}) copy-start(f32[16,2048]{1,0:T(8,128)} %param.6) | copy-start | bytes 393220
  15.9 69.8 %copy-start.3 = (f32[2048]{0:T(1024)S(1)}, f32[2048]{0:T(1024)}, u32[]{:S(2)}) copy-start(f32[2048]{0:T(1024)} %param.5) | copy-start | bytes 24580
  86.7 6.4 %collective-permute-start.4 = (bf16[16,2048]{1,0:T(8,128)(2,1)S(1)}, bf16[16,2048]{1,0:T(8,128)(2,1)S(1)}, u32[]{:S(2)}, u32[]{:S(2)}) collective-permute-start(bf16[16,2048]{1,0:T(8,128)(2,1)S(1)} %convert_element_type.14), channel_id=1, source_target_pairs={{0,4},{4,8},{8,12},{12,16},{16,20},{20,24},{24,28},{28,32},{32,36}... | collective-permute-start | bytes 196616 | tf_op jit(solution)/shard_map/ppermute | solution.py:26
  91.2 9.2 %collective-permute-start.5 = (bf16[16,2048]{1,0:T(8,128)(2,1)S(1)}, bf16[16,2048]{1,0:T(8,128)(2,1)S(1)}, u32[]{:S(2)}, u32[]{:S(2)}) collective-permute-start(bf16[16,2048]{1,0:T(8,128)(2,1)S(1)} %convert_element_type.14), channel_id=1, source_target_pairs={{4,0},{8,4},{12,8},{16,12},{20,16},{24,20},{28,24},{32,28},{36,32}... | collective-permute-start | bytes 196616 | tf_op jit(solution)/shard_map/ppermute | solution.py:28
  145.3 34.5 %copy-start.2 = (f32[16,2048]{1,0:T(8,128)S(1)}, f32[16,2048]{1,0:T(8,128)}, u32[]{:S(2)}) copy-start(f32[16,2048]{1,0:T(8,128)} %get-tuple-element.8) | copy-start | bytes 393220
  147.2 3.2 %collective-permute-start.6 = (bf16[16,2048]{1,0:T(8,128)(2,1)S(1)}, bf16[16,2048]{1,0:T(8,128)(2,1)S(1)}, u32[]{:S(2)}, u32[]{:S(2)}) collective-permute-start(bf16[16,2048]{1,0:T(8,128)(2,1)S(1)} %get-tuple-element.20), channel_id=1, source_target_pairs={{0,4},{4,8},{8,12},{12,16},{16,20},{20,24},{24,28},{28,32},{32,36}... | collective-permute-start | bytes 196616 | tf_op jit(solution)/shard_map/ppermute | solution.py:26
  148.5 4.3 %collective-permute-start.7 = (bf16[16,2048]{1,0:T(8,128)(2,1)S(1)}, bf16[16,2048]{1,0:T(8,128)(2,1)S(1)}, u32[]{:S(2)}, u32[]{:S(2)}) collective-permute-start(bf16[16,2048]{1,0:T(8,128)(2,1)S(1)} %get-tuple-element.20), channel_id=1, source_target_pairs={{4,0},{8,4},{12,8},{16,12},{20,16},{24,20},{28,24},{32,28},{36,32}... | collective-permute-start | bytes 196616 | tf_op jit(solution)/shard_map/ppermute | solution.py:28

commit v7 on v6

--- a/solution.py
+++ b/solution.py
@@ -40,12 +40,12 @@
     b4 = b2 * b2
     b8 = b4 * b4
     b16 = b8 * b8
-    value = (b16 * b2) * (WEXP * radius + 1.0)
-    return value.astype(jnp.bfloat16)
-
-
-def build_kernel(pat_ref, pw_ref, pwt_ref, sqr_ref, k_ref):
+    return (b16 * b2) * (WEXP * radius + 1.0)
+
+
+def build_kernel(pat_ref, pw_ref, pwt_ref, sqr_ref, k_ref, mirror):
     a = pl.program_id(0)
+    blocks = pl.num_programs(0)
     start = pl.multiple_of((a + REACH) * BLK, BLK)
     left = pw_ref[pl.ds(start, BLK), :]
     left_f = left.astype(jnp.float32)
@@ -56,12 +56,24 @@
         col = pl.multiple_of((a + o) * BLK, BLK)
         dst = pl.ds(pl.multiple_of(o * BLK, BLK), BLK)
         live = pat_ref[a * WIDE + o] != 0
-
-        @pl.when(live)
+        other = a + o - REACH
+        lower = jnp.logical_and(other >= 0, other < a)
+        upper = jnp.logical_and(other > a, other < blocks)
+
+        @pl.when(jnp.logical_and(live, lower))
+        def _():
+            k_ref[0, :, dst] = mirror[a, other]
+
+        @pl.when(jnp.logical_and(live, jnp.logical_not(lower)))
         def _():
             right_t = pwt_ref[:, pl.ds(col, BLK)]
             sq_right = sqr_ref[:, pl.ds(col, BLK)]
-            k_ref[0, :, dst] = profile_tile(left_m2, sq_left, right_t, sq_right)
+            value = profile_tile(left_m2, sq_left, right_t, sq_right)
+            k_ref[0, :, dst] = value.astype(jnp.bfloat16)
+
+            @pl.when(upper)
+            def _():
+                mirror[other, a] = value.T.astype(jnp.bfloat16)
 
         @pl.when(jnp.logical_not(live))
         def _():
@@ -98,6 +110,7 @@
                 pl.BlockSpec((1, wide_rows), lambda a, p: (0, 0)),
             ],
             out_specs=pl.BlockSpec((1, BLK, WIDE * BLK), lambda a, p: (a, 0, 0)),
+            scratch_shapes=[pltpu.VMEM((blocks, blocks, BLK, BLK), jnp.bfloat16)],
         ),
         compiler_params=pltpu.CompilerParams(dimension_semantics=("arbitrary",)),
     )(pattern_flat, wide_points, wide_points_t, sq_row)

time: 183 us -> 179 us (0.978)
  starting transfers between devices: 17 us -> 34.7 us
  Pallas kernels: 139 us -> 123 us
  waiting for transfers between devices: 10.1 us -> 4 us
    ppermute x4, starting transfers between devices: 11.8 us -> 29.5 us  [with_halo(): lax.ppermute(tail, axis, [(i, (i + 1) % count) for i in range(ends)])]
    pallas_call x2, Pallas kernels: 69.7 us -> 52.1 us  [apply_sum(): pl.pallas_call(functools.partial(apply_sum_kernel, inner, outer), out_sha...]
    ppermute x4, waiting for transfers between devices: 10.1 us -> 3.99 us  [with_halo(): lax.ppermute(head, axis, [((i + 1) % count, i) for i in range(ends)])]
where the time goes in v7:
time: 179 us; the launch traced here: 177 us
  Pallas kernels  123 us (69%)
  starting transfers between devices  34.7 us (19%)
  other arithmetic  10.4 us (6%)
  waiting for transfers between devices  4 us (2%)
  local copies, waits for them, and re-layouts  3.85 us (2%)
    pallas_call x1, Pallas kernels, build_k(): pl.pallas_call(build_kernel, out_shape=jax.ShapeDtypeStruct((blocks, BLK,...  56.2 us
    pallas_call x2, Pallas kernels, apply_sum(): pl.pallas_call(functools.partial(apply_sum_kernel, inner, outer), out_sha...  52.1 us
    ppermute x4, starting transfers between devices, with_halo(): lax.ppermute(tail, axis, [(i, (i + 1) % count) for i in range(ends)])  29.5 us
    pallas_call x1, Pallas kernels, apply_k(): pl.pallas_call(apply_kernel, out_shape=jax.ShapeDtypeStruct((rows, blocks...  15.1 us
    ppermute x4, starting transfers between devices, with_halo(): lax.ppermute(head, axis, [((i + 1) % count, i) for i in range(ends)])  5.17 us
    ppermute x4, waiting for transfers between devices, with_halo(): lax.ppermute(head, axis, [((i + 1) % count, i) for i in range(ends)])  3.99 us
  transfers between devices with their start and end apart: 8, of which 3 were waited for; matrix products, arithmetic and copies ran while one was open for 2% of the time, Pallas kernels for 0%

profile of v7, /device:TPU:16, one launch (start us, length us, event | category | flops | bytes accessed | tf_op | source)
XLA Modules:
  0.0 177.0 jit_solution(10493849189729605061)
XLA Ops:
  0.6 0.9 convert_element_type.12
  1.5 1.7 collective-permute-start
  3.3 1.3 collective-permute-start.1
  4.6 4.3 %collective-permute-start.2 = (bf16[2048,32]{0,1:T(8,128)(2,1)}, bf16[2048,32]{0,1:T(8,128)(2,1)S(1)}, u32[]{:S(2)}, u32[]{:S(2)}) collective-permute-start(bf16[2048,32]{0,1:T(8,128)(2,1)} %param.4), channel_id=1, source_target_pairs={{0,4},{4,8},{8,12},{12,16},{16,20},{20,24},{24,28},{28,32},{32,36}... | collective-permute-start | bytes 393224 | tf_op jit(solution)/shard_map/ppermute | solution.py:26
  8.9 1.3 collective-permute-start.3
  10.2 1.4 reshape.75.pat_ref
  11.6 0.0 collective-permute-done
  11.6 0.0 collective-permute-done.1
  11.6 0.7 pad_maximum_fusion.v_ref
  12.3 0.0 collective-permute-done.2
  12.3 0.9 constant_dynamic-update-slice_fusion.1
  13.2 0.4 collective-permute-done.3
  13.6 0.0 copy-start
  13.6 1.5 copy.7.pw_ref
  15.1 0.7 multiply_reduce_fusion
  15.9 0.0 copy-done
  15.9 0.0 copy-start.1
  15.9 0.0 copy-start.3
  15.9 56.2 %shard_map.67.k_ref = bf16[16,128,4224]{2,1,0:T(8,128)(2,1)} custom-call(s32[528]{0:T(1024)} %reshape.75.pat_ref, bf16[6144,32]{1,0:T(8,128)(2,1)} %copy.7.pw_ref, bf16[32,6144]{1,0:T(8,128)(2,1)} %bitcast.30, f32[1,6144]{1,0:T(1,128)} %bitcast.31), custom_call_target="tpu_custom_call" | custom-call | tf_op jit(solution)/shard_map/pallas_call | solution.py:101
  72.1 15.1 %shard_map.68 = f32[16,2048]{1,0:T(8,128)} custom-call(bf16[16,6144]{1,0:T(8,128)(2,1)} %pad_maximum_fusion.v_ref, bf16[16,128,4224]{2,1,0:T(8,128)(2,1)} %shard_map.67.k_ref), custom_call_target="tpu_custom_call" | custom-call | tf_op jit(solution)/shard_map/pallas_call | solution.py:122
  87.2 0.0 copy-done.1
  87.2 0.0 copy-done.3
  87.2 1.0 multiply_reduce_fusion.4
  88.2 22.2 %collective-permute-start.4 = (bf16[16,2048]{1,0:T(8,128)(2,1)S(1)}, bf16[16,2048]{1,0:T(8,128)(2,1)S(1)}, u32[]{:S(2)}, u32[]{:S(2)}) collective-permute-start(bf16[16,2048]{1,0:T(8,128)(2,1)S(1)} %convert_element_type.14), channel_id=1, source_target_pairs={{0,4},{4,8},{8,12},{12,16},{16,20},{20,24},{24,28},{28,32},{32,36}... | collective-permute-start | bytes 196616 | tf_op jit(solution)/shard_map/ppermute | solution.py:26
  110.4 1.3 collective-permute-start.5
  111.7 0.6 select_maximum_fusion.1.part_ref
  112.3 0.0 collective-permute-done.4
  112.3 1.2 collective-permute-done.5
  113.5 0.7 pad_maximum_fusion.1.v_ref
  114.2 29.5 %shard_map.69 = (f32[16,2048]{1,0:T(8,128)}, f32[8,128]{1,0:T(8,128)}) custom-call(bf16[16,6144]{1,0:T(8,128)(2,1)} %pad_maximum_fusion.1.v_ref, bf16[16,128,4224]{2,1,0:T(8,128)(2,1)} %shard_map.67.k_ref, f32[8,128]{1,0:T(8,128)} %select_maximum_fusion.1.part_ref), custom_call_target="tpu_custom_call" | custom-call | tf_op jit(solution)/shard_map/pallas_call | solution.py:257
  143.7 0.0 copy-start.2
  143.7 0.8 bitcast_divide_fusion.1
  144.5 1.1 multiply_reduce_fusion.2
  145.6 1.3 collective-permute-start.6
  146.9 1.3 collective-permute-start.7
  148.2 0.6 select_maximum_fusion.part_ref
  148.8 0.0 collective-permute-done.6
  148.8 2.4 %collective-permute-done.7 = bf16[16,2048]{1,0:T(8,128)(2,1)S(1)} collective-permute-done((bf16[16,2048]{1,0:T(8,128)(2,1)S(1)}, bf16[16,2048]{1,0:T(8,128)(2,1)S(1)}, u32[]{:S(2)}, u32[]{:S(2)}) %collective-permute-start.7) | collective-permute-done | bytes 65568 | tf_op jit(solution)/shard_map/ppermute | solution.py:28
  151.2 0.7 pad_maximum_fusion.2.v_ref
  151.8 22.6 %shard_map.70 = (f32[16,2048]{1,0:T(8,128)}, f32[8,128]{1,0:T(8,128)}) custom-call(bf16[16,6144]{1,0:T(8,128)(2,1)} %pad_maximum_fusion.2.v_ref, bf16[16,128,4224]{2,1,0:T(8,128)(2,1)} %shard_map.67.k_ref, f32[8,128]{1,0:T(8,128)} %select_maximum_fusion.part_ref), custom_call_target="tpu_custom_call" | custom-call | tf_op jit(solution)/shard_map/pallas_call | solution.py:257
  174.4 0.8 fusion.1
  175.2 0.0 copy-done.2
  175.2 1.8 %multiply_subtract_fusion = (f32[16,2048]{1,0:T(8,128)}, f32[16,2048]{1,0:T(8,128)}, f32[16,2048]{1,0:T(8,128)}) fusion(f32[16,2048]{1,0:T(8,128)} %get-tuple-element.10, f32[16,2048]{1,0:T(8,128)S(1)} %copy-done.2, f32[16,2048]{1,0:T(8,128)S(1)} %get-tuple-element.17, f32[16]{0:T(128)S(1)} %get-tuple-element.16, f32[16]{0:T(128)S(1)} %get-tuple-element.15, ...), kind=kLoop, calls=%fused_computation.4 | loop fusion | flops 753664 | bytes 925888 | tf_op jit(solution)/shard_map/sub | solution.py:342
  (3 shorter events, 0.0 us)
Async XLA Ops:
  1.5 10.0 %collective-permute-start = (bf16[16,2048]{1,0:T(8,128)(2,1)S(1)}, bf16[16,2048]{1,0:T(8,128)(2,1)S(1)}, u32[]{:S(2)}, u32[]{:S(2)}) collective-permute-start(bf16[16,2048]{1,0:T(8,128)(2,1)S(1)} %convert_element_type.12), channel_id=1, source_target_pairs={{0,4},{4,8},{8,12},{12,16},{16,20},{20,24},{24,28},{28,32},{32,36}... | collective-permute-start | bytes 196616 | tf_op jit(solution)/shard_map/ppermute | solution.py:26
  3.3 8.3 %collective-permute-start.1 = (bf16[16,2048]{1,0:T(8,128)(2,1)S(1)}, bf16[16,2048]{1,0:T(8,128)(2,1)S(1)}, u32[]{:S(2)}, u32[]{:S(2)}) collective-permute-start(bf16[16,2048]{1,0:T(8,128)(2,1)S(1)} %convert_element_type.12), channel_id=1, source_target_pairs={{4,0},{8,4},{12,8},{16,12},{20,16},{24,20},{28,24},{32,28},{36,32}... | collective-permute-start | bytes 196616 | tf_op jit(solution)/shard_map/ppermute | solution.py:28
  4.6 7.7 %collective-permute-start.2 = (bf16[2048,32]{0,1:T(8,128)(2,1)}, bf16[2048,32]{0,1:T(8,128)(2,1)S(1)}, u32[]{:S(2)}, u32[]{:S(2)}) collective-permute-start(bf16[2048,32]{0,1:T(8,128)(2,1)} %param.4), channel_id=1, source_target_pairs={{0,4},{4,8},{8,12},{12,16},{16,20},{20,24},{24,28},{28,32},{32,36}... | collective-permute-start | bytes 393224 | tf_op jit(solution)/shard_map/ppermute | solution.py:26
  8.9 4.7 %collective-permute-start.3 = (bf16[2048,32]{0,1:T(8,128)(2,1)}, bf16[2048,32]{0,1:T(8,128)(2,1)S(1)}, u32[]{:S(2)}, u32[]{:S(2)}) collective-permute-start(bf16[2048,32]{0,1:T(8,128)(2,1)} %param.4), channel_id=1, source_target_pairs={{4,0},{8,4},{12,8},{16,12},{20,16},{24,20},{28,24},{32,28},{36,32}... | collective-permute-start | bytes 393224 | tf_op jit(solution)/shard_map/ppermute | solution.py:28
  13.6 2.3 %copy-start = (bf16[6144,32]{0,1:T(8,128)(2,1)}, bf16[6144,32]{0,1:T(8,128)(2,1)S(1)}, u32[]{:S(2)}) copy-start(bf16[6144,32]{0,1:T(8,128)(2,1)S(1)} %constant_dynamic-update-slice_fusion) | copy-start | bytes 1179652
  15.9 71.3 %copy-start.1 = (f32[16,2048]{1,0:T(8,128)S(1)}, f32[16,2048]{1,0:T(8,128)}, u32[]{:S(2)}) copy-start(f32[16,2048]{1,0:T(8,128)} %param.6) | copy-start | bytes 393220
  15.9 71.3 %copy-start.3 = (f32[2048]{0:T(1024)S(1)}, f32[2048]{0:T(1024)}, u32[]{:S(2)}) copy-start(f32[2048]{0:T(1024)} %param.5) | copy-start | bytes 24580
  88.2 24.1 %collective-permute-start.4 = (bf16[16,2048]{1,0:T(8,128)(2,1)S(1)}, bf16[16,2048]{1,0:T(8,128)(2,1)S(1)}, u32[]{:S(2)}, u32[]{:S(2)}) collective-permute-start(bf16[16,2048]{1,0:T(8,128)(2,1)S(1)} %convert_element_type.14), channel_id=1, source_target_pairs={{0,4},{4,8},{8,12},{12,16},{16,20},{20,24},{24,28},{28,32},{32,36}... | collective-permute-start | bytes 196616 | tf_op jit(solution)/shard_map/ppermute | solution.py:26
  110.4 3.1 %collective-permute-start.5 = (bf16[16,2048]{1,0:T(8,128)(2,1)S(1)}, bf16[16,2048]{1,0:T(8,128)(2,1)S(1)}, u32[]{:S(2)}, u32[]{:S(2)}) collective-permute-start(bf16[16,2048]{1,0:T(8,128)(2,1)S(1)} %convert_element_type.14), channel_id=1, source_target_pairs={{4,0},{8,4},{12,8},{16,12},{20,16},{24,20},{28,24},{32,28},{36,32}... | collective-permute-start | bytes 196616 | tf_op jit(solution)/shard_map/ppermute | solution.py:28
  143.7 31.5 %copy-start.2 = (f32[16,2048]{1,0:T(8,128)S(1)}, f32[16,2048]{1,0:T(8,128)}, u32[]{:S(2)}) copy-start(f32[16,2048]{1,0:T(8,128)} %get-tuple-element.8) | copy-start | bytes 393220
  145.6 3.2 %collective-permute-start.6 = (bf16[16,2048]{1,0:T(8,128)(2,1)S(1)}, bf16[16,2048]{1,0:T(8,128)(2,1)S(1)}, u32[]{:S(2)}, u32[]{:S(2)}) collective-permute-start(bf16[16,2048]{1,0:T(8,128)(2,1)S(1)} %get-tuple-element.20), channel_id=1, source_target_pairs={{0,4},{4,8},{8,12},{12,16},{16,20},{20,24},{24,28},{28,32},{32,36}... | collective-permute-start | bytes 196616 | tf_op jit(solution)/shard_map/ppermute | solution.py:26
  146.9 4.3 %collective-permute-start.7 = (bf16[16,2048]{1,0:T(8,128)(2,1)S(1)}, bf16[16,2048]{1,0:T(8,128)(2,1)S(1)}, u32[]{:S(2)}, u32[]{:S(2)}) collective-permute-start(bf16[16,2048]{1,0:T(8,128)(2,1)S(1)} %get-tuple-element.20), channel_id=1, source_target_pairs={{4,0},{8,4},{12,8},{16,12},{20,16},{24,20},{28,24},{32,28},{36,32}... | collective-permute-start | bytes 196616 | tf_op jit(solution)/shard_map/ppermute | solution.py:28

commit v8 on v7

--- a/solution.py
+++ b/solution.py
@@ -31,8 +31,7 @@
     )
 
 
-def profile_tile(left_m2, sq_left, right_t, sq_right):
-    cross = jnp.dot(left_m2, right_t, preferred_element_type=jnp.float32)
+def profile_tile(sq_left, sq_right, cross):
     dist = jnp.maximum((sq_left + sq_right) + cross, 0.0)
     radius = jnp.sqrt(dist)
     base = jnp.maximum(1.0 - radius, 0.0)
@@ -43,7 +42,7 @@
     return (b16 * b2) * (WEXP * radius + 1.0)
 
 
-def build_kernel(pat_ref, pw_ref, pwt_ref, sqr_ref, k_ref, mirror):
+def build_kernel(pat_ref, pw_ref, pwt_ref, sqr_ref, k_ref, mirror, cross_ref):
     a = pl.program_id(0)
     blocks = pl.num_programs(0)
     start = pl.multiple_of((a + REACH) * BLK, BLK)
@@ -51,6 +50,8 @@
     left_f = left.astype(jnp.float32)
     sq_left = jnp.sum(left_f * left_f, axis=1, keepdims=True)
     left_m2 = left * jnp.asarray(-2.0, jnp.bfloat16)
+    window = pwt_ref[:, pl.ds(pl.multiple_of(a * BLK, BLK), WIDE * BLK)]
+    cross_ref[...] = jnp.dot(left_m2, window, preferred_element_type=jnp.float32)
 
     def body(o, carry):
         col = pl.multiple_of((a + o) * BLK, BLK)
@@ -66,9 +67,8 @@
 
         @pl.when(jnp.logical_and(live, jnp.logical_not(lower)))
         def _():
-            right_t = pwt_ref[:, pl.ds(col, BLK)]
             sq_right = sqr_ref[:, pl.ds(col, BLK)]
-            value = profile_tile(left_m2, sq_left, right_t, sq_right)
+            value = profile_tile(sq_left, sq_right, cross_ref[:, dst])
             k_ref[0, :, dst] = value.astype(jnp.bfloat16)
 
             @pl.when(upper)
@@ -110,7 +110,10 @@
                 pl.BlockSpec((1, wide_rows), lambda a, p: (0, 0)),
             ],
             out_specs=pl.BlockSpec((1, BLK, WIDE * BLK), lambda a, p: (a, 0, 0)),
-            scratch_shapes=[pltpu.VMEM((blocks, blocks, BLK, BLK), jnp.bfloat16)],
+            scratch_shapes=[
+                pltpu.VMEM((blocks, blocks, BLK, BLK), jnp.bfloat16),
+                pltpu.VMEM((BLK, WIDE * BLK), jnp.float32),
+            ],
         ),
         compiler_params=pltpu.CompilerParams(dimension_semantics=("arbitrary",)),
     )(pattern_flat, wide_points, wide_points_t, sq_row)

time: 179 us -> 152 us (0.85)
  Pallas kernels: 123 us -> 107 us
  starting transfers between devices: 34.7 us -> 22.5 us
    pallas_call x1, Pallas kernels: 56.2 us -> 33.9 us  [build_k(): pl.pallas_call(build_kernel, out_shape=jax.ShapeDtypeStruct((blocks, BLK,...]
    ppermute x4, starting transfers between devices: 29.5 us -> 17.4 us  [with_halo(): lax.ppermute(tail, axis, [(i, (i + 1) % count) for i in range(ends)])]
    pallas_call x2, Pallas kernels: 52.1 us -> 57.9 us  [apply_sum(): pl.pallas_call(functools.partial(apply_sum_kernel, inner, outer), out_sha...]
  transfers between devices with their start and end apart: 8 -> 8, of which waited for: 3 -> 3; matrix products, arithmetic and copies ran while one was open for 2% -> 3% of each run, Pallas kernels for 0% -> 0%
where the time goes in v8:
time: 152 us; the launch traced here: 150 us
  Pallas kernels  107 us (70%)
  starting transfers between devices  22.5 us (15%)
  other arithmetic  10.4 us (7%)
  waiting for transfers between devices  5.28 us (3%)
  local copies, waits for them, and re-layouts  3.85 us (3%)
    pallas_call x2, Pallas kernels, apply_sum(): pl.pallas_call(functools.partial(apply_sum_kernel, inner, outer), out_sha...  57.9 us
    pallas_call x1, Pallas kernels, build_k(): pl.pallas_call(build_kernel, out_shape=jax.ShapeDtypeStruct((blocks, BLK,...  33.9 us
    ppermute x4, starting transfers between devices, with_halo(): lax.ppermute(tail, axis, [(i, (i + 1) % count) for i in range(ends)])  17.4 us
    pallas_call x1, Pallas kernels, apply_k(): pl.pallas_call(apply_kernel, out_shape=jax.ShapeDtypeStruct((rows, blocks...  15.1 us
    ppermute x4, waiting for transfers between devices, with_halo(): lax.ppermute(head, axis, [((i + 1) % count, i) for i in range(ends)])  5.27 us
    ppermute x4, starting transfers between devices, with_halo(): lax.ppermute(head, axis, [((i + 1) % count, i) for i in range(ends)])  5.17 us
  transfers between devices with their start and end apart: 8, of which 3 were waited for; matrix products, arithmetic and copies ran while one was open for 3% of the time, Pallas kernels for 0%

profile of v8, /device:TPU:16, one launch (start us, length us, event | category | flops | bytes accessed | tf_op | source)
XLA Modules:
  0.0 149.7 jit_solution(221307508450496447)
XLA Ops:
  0.6 0.9 convert_element_type.12
  1.5 1.7 %collective-permute-start = (bf16[16,2048]{1,0:T(8,128)(2,1)S(1)}, bf16[16,2048]{1,0:T(8,128)(2,1)S(1)}, u32[]{:S(2)}, u32[]{:S(2)}) collective-permute-start(bf16[16,2048]{1,0:T(8,128)(2,1)S(1)} %convert_element_type.12), channel_id=1, source_target_pairs={{0,4},{4,8},{8,12},{12,16},{16,20},{20,24},{24,28},{28,32},{32,36}... | collective-permute-start | bytes 196616 | tf_op jit(solution)/shard_map/ppermute | solution.py:26
  3.3 1.3 collective-permute-start.1
  4.6 4.3 %collective-permute-start.2 = (bf16[2048,32]{0,1:T(8,128)(2,1)}, bf16[2048,32]{0,1:T(8,128)(2,1)S(1)}, u32[]{:S(2)}, u32[]{:S(2)}) collective-permute-start(bf16[2048,32]{0,1:T(8,128)(2,1)} %param.4), channel_id=1, source_target_pairs={{0,4},{4,8},{8,12},{12,16},{16,20},{20,24},{24,28},{28,32},{32,36}... | collective-permute-start | bytes 393224 | tf_op jit(solution)/shard_map/ppermute | solution.py:26
  8.9 1.3 collective-permute-start.3
  10.2 1.4 reshape.75.pat_ref
  11.6 0.0 collective-permute-done
  11.6 0.0 collective-permute-done.1
  11.6 0.7 pad_maximum_fusion.v_ref
  12.3 0.0 collective-permute-done.2
  12.3 0.9 constant_dynamic-update-slice_fusion.1
  13.2 0.4 collective-permute-done.3
  13.6 0.0 copy-start
  13.6 1.5 %copy.7.pw_ref = bf16[6144,32]{1,0:T(8,128)(2,1)} copy(bf16[6144,32]{0,1:T(8,128)(2,1)S(1)} %constant_dynamic-update-slice_fusion) | data formatting | bytes 786432 | tf_op jit(solution)/shard_map/concatenate | solution.py:24
  15.1 0.7 multiply_reduce_fusion
  15.9 0.0 copy-done
  15.9 0.0 copy-start.1
  15.9 0.0 copy-start.3
  15.9 33.9 %shard_map.67.k_ref = bf16[16,128,4224]{2,1,0:T(8,128)(2,1)} custom-call(s32[528]{0:T(1024)} %reshape.75.pat_ref, bf16[6144,32]{1,0:T(8,128)(2,1)} %copy.7.pw_ref, bf16[32,6144]{1,0:T(8,128)(2,1)} %bitcast.30, f32[1,6144]{1,0:T(1,128)} %bitcast.31), custom_call_target="tpu_custom_call" | custom-call | tf_op jit(solution)/shard_map/pallas_call | solution.py:101
  49.7 15.1 %shard_map.68 = f32[16,2048]{1,0:T(8,128)} custom-call(bf16[16,6144]{1,0:T(8,128)(2,1)} %pad_maximum_fusion.v_ref, bf16[16,128,4224]{2,1,0:T(8,128)(2,1)} %shard_map.67.k_ref), custom_call_target="tpu_custom_call" | custom-call | tf_op jit(solution)/shard_map/pallas_call | solution.py:125
  64.8 0.0 copy-done.1
  64.8 0.0 copy-done.3
  64.8 1.0 multiply_reduce_fusion.4
  65.9 10.0 %collective-permute-start.4 = (bf16[16,2048]{1,0:T(8,128)(2,1)S(1)}, bf16[16,2048]{1,0:T(8,128)(2,1)S(1)}, u32[]{:S(2)}, u32[]{:S(2)}) collective-permute-start(bf16[16,2048]{1,0:T(8,128)(2,1)S(1)} %convert_element_type.14), channel_id=1, source_target_pairs={{0,4},{4,8},{8,12},{12,16},{16,20},{20,24},{24,28},{28,32},{32,36}... | collective-permute-start | bytes 196616 | tf_op jit(solution)/shard_map/ppermute | solution.py:26
  76.0 1.3 collective-permute-start.5
  77.3 0.6 select_maximum_fusion.1.part_ref
  77.9 0.0 collective-permute-done.4
  77.9 2.3 %collective-permute-done.5 = bf16[16,2048]{1,0:T(8,128)(2,1)S(1)} collective-permute-done((bf16[16,2048]{1,0:T(8,128)(2,1)S(1)}, bf16[16,2048]{1,0:T(8,128)(2,1)S(1)}, u32[]{:S(2)}, u32[]{:S(2)}) %collective-permute-start.5) | collective-permute-done | bytes 65568 | tf_op jit(solution)/shard_map/ppermute | solution.py:28
  80.1 0.7 pad_maximum_fusion.1.v_ref
  80.8 32.3 %shard_map.69 = (f32[16,2048]{1,0:T(8,128)}, f32[8,128]{1,0:T(8,128)}) custom-call(bf16[16,6144]{1,0:T(8,128)(2,1)} %pad_maximum_fusion.1.v_ref, bf16[16,128,4224]{2,1,0:T(8,128)(2,1)} %shard_map.67.k_ref, f32[8,128]{1,0:T(8,128)} %select_maximum_fusion.1.part_ref), custom_call_target="tpu_custom_call" | custom-call | tf_op jit(solution)/shard_map/pallas_call | solution.py:260
  113.1 0.0 copy-start.2
  113.1 0.8 bitcast_divide_fusion.1
  113.9 1.1 multiply_reduce_fusion.2
  115.0 1.3 collective-permute-start.6
  116.3 1.3 collective-permute-start.7
  117.6 0.6 select_maximum_fusion.part_ref
  118.2 0.0 collective-permute-done.6
  118.2 2.6 %collective-permute-done.7 = bf16[16,2048]{1,0:T(8,128)(2,1)S(1)} collective-permute-done((bf16[16,2048]{1,0:T(8,128)(2,1)S(1)}, bf16[16,2048]{1,0:T(8,128)(2,1)S(1)}, u32[]{:S(2)}, u32[]{:S(2)}) %collective-permute-start.7) | collective-permute-done | bytes 65568 | tf_op jit(solution)/shard_map/ppermute | solution.py:28
  120.8 0.7 pad_maximum_fusion.2.v_ref
  121.5 25.6 %shard_map.70 = (f32[16,2048]{1,0:T(8,128)}, f32[8,128]{1,0:T(8,128)}) custom-call(bf16[16,6144]{1,0:T(8,128)(2,1)} %pad_maximum_fusion.2.v_ref, bf16[16,128,4224]{2,1,0:T(8,128)(2,1)} %shard_map.67.k_ref, f32[8,128]{1,0:T(8,128)} %select_maximum_fusion.part_ref), custom_call_target="tpu_custom_call" | custom-call | tf_op jit(solution)/shard_map/pallas_call | solution.py:260
  147.1 0.8 fusion.1
  147.9 0.0 copy-done.2
  147.9 1.8 %multiply_subtract_fusion = (f32[16,2048]{1,0:T(8,128)}, f32[16,2048]{1,0:T(8,128)}, f32[16,2048]{1,0:T(8,128)}) fusion(f32[16,2048]{1,0:T(8,128)} %get-tuple-element.10, f32[16,2048]{1,0:T(8,128)S(1)} %copy-done.2, f32[16,2048]{1,0:T(8,128)S(1)} %get-tuple-element.17, f32[16]{0:T(128)S(1)} %get-tuple-element.16, f32[16]{0:T(128)S(1)} %get-tuple-element.15, ...), kind=kLoop, calls=%fused_computation.4 | loop fusion | flops 753664 | bytes 925888 | tf_op jit(solution)/shard_map/sub | solution.py:345
  (3 shorter events, 0.0 us)
Async XLA Ops:
  1.5 10.0 %collective-permute-start = (bf16[16,2048]{1,0:T(8,128)(2,1)S(1)}, bf16[16,2048]{1,0:T(8,128)(2,1)S(1)}, u32[]{:S(2)}, u32[]{:S(2)}) collective-permute-start(bf16[16,2048]{1,0:T(8,128)(2,1)S(1)} %convert_element_type.12), channel_id=1, source_target_pairs={{0,4},{4,8},{8,12},{12,16},{16,20},{20,24},{24,28},{28,32},{32,36}... | collective-permute-start | bytes 196616 | tf_op jit(solution)/shard_map/ppermute | solution.py:26
  3.3 8.3 %collective-permute-start.1 = (bf16[16,2048]{1,0:T(8,128)(2,1)S(1)}, bf16[16,2048]{1,0:T(8,128)(2,1)S(1)}, u32[]{:S(2)}, u32[]{:S(2)}) collective-permute-start(bf16[16,2048]{1,0:T(8,128)(2,1)S(1)} %convert_element_type.12), channel_id=1, source_target_pairs={{4,0},{8,4},{12,8},{16,12},{20,16},{24,20},{28,24},{32,28},{36,32}... | collective-permute-start | bytes 196616 | tf_op jit(solution)/shard_map/ppermute | solution.py:28
  4.6 7.7 %collective-permute-start.2 = (bf16[2048,32]{0,1:T(8,128)(2,1)}, bf16[2048,32]{0,1:T(8,128)(2,1)S(1)}, u32[]{:S(2)}, u32[]{:S(2)}) collective-permute-start(bf16[2048,32]{0,1:T(8,128)(2,1)} %param.4), channel_id=1, source_target_pairs={{0,4},{4,8},{8,12},{12,16},{16,20},{20,24},{24,28},{28,32},{32,36}... | collective-permute-start | bytes 393224 | tf_op jit(solution)/shard_map/ppermute | solution.py:26
  8.9 4.7 %collective-permute-start.3 = (bf16[2048,32]{0,1:T(8,128)(2,1)}, bf16[2048,32]{0,1:T(8,128)(2,1)S(1)}, u32[]{:S(2)}, u32[]{:S(2)}) collective-permute-start(bf16[2048,32]{0,1:T(8,128)(2,1)} %param.4), channel_id=1, source_target_pairs={{4,0},{8,4},{12,8},{16,12},{20,16},{24,20},{28,24},{32,28},{36,32}... | collective-permute-start | bytes 393224 | tf_op jit(solution)/shard_map/ppermute | solution.py:28
  13.6 2.3 %copy-start = (bf16[6144,32]{0,1:T(8,128)(2,1)}, bf16[6144,32]{0,1:T(8,128)(2,1)S(1)}, u32[]{:S(2)}) copy-start(bf16[6144,32]{0,1:T(8,128)(2,1)S(1)} %constant_dynamic-update-slice_fusion) | copy-start | bytes 1179652
  15.9 49.0 %copy-start.1 = (f32[16,2048]{1,0:T(8,128)S(1)}, f32[16,2048]{1,0:T(8,128)}, u32[]{:S(2)}) copy-start(f32[16,2048]{1,0:T(8,128)} %param.6) | copy-start | bytes 393220
  15.9 49.0 %copy-start.3 = (f32[2048]{0:T(1024)S(1)}, f32[2048]{0:T(1024)}, u32[]{:S(2)}) copy-start(f32[2048]{0:T(1024)} %param.5) | copy-start | bytes 24580
  65.9 12.0 %collective-permute-start.4 = (bf16[16,2048]{1,0:T(8,128)(2,1)S(1)}, bf16[16,2048]{1,0:T(8,128)(2,1)S(1)}, u32[]{:S(2)}, u32[]{:S(2)}) collective-permute-start(bf16[16,2048]{1,0:T(8,128)(2,1)S(1)} %convert_element_type.14), channel_id=1, source_target_pairs={{0,4},{4,8},{8,12},{12,16},{16,20},{20,24},{24,28},{28,32},{32,36}... | collective-permute-start | bytes 196616 | tf_op jit(solution)/shard_map/ppermute | solution.py:26
  76.0 4.2 %collective-permute-start.5 = (bf16[16,2048]{1,0:T(8,128)(2,1)S(1)}, bf16[16,2048]{1,0:T(8,128)(2,1)S(1)}, u32[]{:S(2)}, u32[]{:S(2)}) collective-permute-start(bf16[16,2048]{1,0:T(8,128)(2,1)S(1)} %convert_element_type.14), channel_id=1, source_target_pairs={{4,0},{8,4},{12,8},{16,12},{20,16},{24,20},{28,24},{32,28},{36,32}... | collective-permute-start | bytes 196616 | tf_op jit(solution)/shard_map/ppermute | solution.py:28
  113.1 34.8 %copy-start.2 = (f32[16,2048]{1,0:T(8,128)S(1)}, f32[16,2048]{1,0:T(8,128)}, u32[]{:S(2)}) copy-start(f32[16,2048]{1,0:T(8,128)} %get-tuple-element.8) | copy-start | bytes 393220
  115.0 3.2 %collective-permute-start.6 = (bf16[16,2048]{1,0:T(8,128)(2,1)S(1)}, bf16[16,2048]{1,0:T(8,128)(2,1)S(1)}, u32[]{:S(2)}, u32[]{:S(2)}) collective-permute-start(bf16[16,2048]{1,0:T(8,128)(2,1)S(1)} %get-tuple-element.20), channel_id=1, source_target_pairs={{0,4},{4,8},{8,12},{12,16},{16,20},{20,24},{24,28},{28,32},{32,36}... | collective-permute-start | bytes 196616 | tf_op jit(solution)/shard_map/ppermute | solution.py:26
  116.3 4.5 %collective-permute-start.7 = (bf16[16,2048]{1,0:T(8,128)(2,1)S(1)}, bf16[16,2048]{1,0:T(8,128)(2,1)S(1)}, u32[]{:S(2)}, u32[]{:S(2)}) collective-permute-start(bf16[16,2048]{1,0:T(8,128)(2,1)S(1)} %get-tuple-element.20), channel_id=1, source_target_pairs={{4,0},{8,4},{12,8},{16,12},{20,16},{24,20},{28,24},{32,28},{36,32}... | collective-permute-start | bytes 196616 | tf_op jit(solution)/shard_map/ppermute | solution.py:28

commit v9 on v8

--- a/solution.py
+++ b/solution.py
@@ -229,14 +229,11 @@
     @pl.when(a == 0)
     def _():
         greet()
+        start_first()
 
     blocks = v_ref.shape[1] // BLK - 2 * REACH
 
-    @pl.when(a == min(2, blocks - 1))
-    def _():
-        start_first()
-
-    @pl.when(a == min(blocks // 2, blocks - 1))
+    @pl.when(a == min(blocks // 2 - 2, blocks - 1))
     def _():
         start_second()
 
@@ -293,7 +290,23 @@
     block_count = local_rows // BLK
     rim_rows = REACH * BLK
     kernel_scale = 1.0 / (4 * BLK)
-    wide_points = with_halo(points, "pts", 0, rim_rows)
+    first_low = right_side.astype(jnp.bfloat16)
+    point_rows = points.size // 128
+    packed = jnp.concatenate([points.reshape(point_rows, 128), first_low.reshape(-1, 128)], axis=0)
+    count = lax.axis_size("pts")
+    from_left = lax.ppermute(packed, "pts", [(i, i + 1) for i in range(count - 1)])
+    from_right = lax.ppermute(packed, "pts", [(i + 1, i) for i in range(count - 1)])
+    wide_points = jnp.concatenate(
+        [from_left[:point_rows].reshape(points.shape), points, from_right[:point_rows].reshape(points.shape)], axis=0
+    )
+    first_wide = jnp.concatenate(
+        [
+            from_left[point_rows:].reshape(first_low.shape),
+            first_low,
+            from_right[point_rows:].reshape(first_low.shape),
+        ],
+        axis=1,
+    )
     kmat = build_k(pattern.reshape(-1), wide_points, block_count)
 
     rhs_count = lax.axis_size("rhs")
@@ -316,7 +329,7 @@
 
     solution = jnp.zeros_like(right_side)
     residual = right_side
-    res_image = apply_operator(residual)
+    res_image = noise_var[None, :] * residual + kernel_scale * apply_k(first_wide, kmat)
     direction = jnp.zeros_like(right_side)
     dir_image = jnp.zeros_like(right_side)
     dir_twice = jnp.zeros_like(right_side)

time: 152 us -> 151 us (level)
  Pallas kernels: 107 us -> 115 us
  starting transfers between devices: 22.5 us -> 15.8 us
  waiting for transfers between devices: 5.28 us -> 0.56 us
  local copies, waits for them, and re-layouts: 3.85 us -> 5.4 us
    ppermute x4 -> x2, starting transfers between devices: 17.4 us -> 8.87 us  [with_halo(): lax.ppermute(tail, axis, [(i, (i + 1) % count) for i in range(ends)])]
    pallas_call x2, Pallas kernels: 57.9 us -> 65 us  [apply_sum(): pl.pallas_call(functools.partial(apply_sum_kernel, inner, outer), out_sha...]
    ppermute x4 -> x2, waiting for transfers between devices: 5.27 us -> 0.01 us  [with_halo(): lax.ppermute(head, axis, [((i + 1) % count, i) for i in range(ends)])]
    ppermute x0 -> x2, starting transfers between devices: none -> 4.33 us  [the longest x1 3.04 us: per_device(): lax.ppermute(packed, 'pts', [(i, i + 1) for i in range(count - 1)])]
    ppermute x4 -> x2, starting transfers between devices: 5.17 us -> 2.58 us  [with_halo(): lax.ppermute(head, axis, [((i + 1) % count, i) for i in range(ends)])]
  transfers between devices with their start and end apart: 8 -> 6, of which waited for: 3 -> 2; matrix products, arithmetic and copies ran while one was open for 3% -> 2% of each run, Pallas kernels for 0% -> 0%
where the time goes in v9:
time: 151 us; the launch traced here: 149 us
  Pallas kernels  115 us (76%)
  starting transfers between devices  15.8 us (10%)
  other arithmetic  11.3 us (7%)
  local copies, waits for them, and re-layouts  5.4 us (4%)
    pallas_call x2, Pallas kernels, apply_sum(): pl.pallas_call(functools.partial(apply_sum_kernel, inner, outer), out_sha...  65 us
    pallas_call x1, Pallas kernels, build_k(): pl.pallas_call(build_kernel, out_shape=jax.ShapeDtypeStruct((blocks, BLK,...  35.3 us
    pallas_call x1, Pallas kernels, apply_k(): pl.pallas_call(apply_kernel, out_shape=jax.ShapeDtypeStruct((rows, blocks...  15.1 us
    ppermute x2, starting transfers between devices, with_halo(): lax.ppermute(tail, axis, [(i, (i + 1) % count) for i in range(ends)])  8.87 us
    ppermute x1, starting transfers between devices, per_device(): lax.ppermute(packed, 'pts', [(i, i + 1) for i in range(count - 1)])  3.04 us
  transfers between devices with their start and end apart: 6, of which 2 were waited for; matrix products, arithmetic and copies ran while one was open for 2% of the time, Pallas kernels for 0%

profile of v9, /device:TPU:16, one launch (start us, length us, event | category | flops | bytes accessed | tf_op | source)
XLA Modules:
  0.0 149.3 jit_solution(5526031288127185728)
XLA Ops:
  0.6 0.9 convert_element_type.12
  1.6 1.2 copy.8
  2.8 0.3 reshape.93
  3.1 1.3 collective-permute-start.1
  4.4 3.0 %collective-permute-start = (bf16[768,128]{1,0:T(8,128)(2,1)S(1)}, bf16[768,128]{1,0:T(8,128)(2,1)S(1)}, u32[]{:S(2)}, u32[]{:S(2)}) collective-permute-start(bf16[768,128]{1,0:T(8,128)(2,1)S(1)} %constant_dynamic-update-slice_fusion), channel_id=1, source_target_pairs={{0,4},{4,8},{8,12},{12,16},{16,20},{20,24},{24,28},{28,32},{32,36}... | collective-permute-start | bytes 589832 | tf_op jit(solution)/shard_map/ppermute | solution.py:297
  7.4 1.4 reshape.97.pat_ref
  8.8 0.0 collective-permute-done.1
  8.9 0.0 collective-permute-done
  9.0 0.2 reshape.98
  9.2 0.2 copy.9
  9.4 0.2 reshape.99
  9.7 0.2 copy.10
  9.8 1.6 %multiply_reduce_fusion = (f32[6144]{0:T(1024)}, bf16[6144,32]{0,1:T(8,128)(2,1)S(1)}) fusion(bf16[2048,32]{0,1:T(8,128)(2,1)S(1)} %copy.10, bf16[2048,32]{0,1:T(8,128)(2,1)} %param.4, bf16[2048,32]{0,1:T(8,128)(2,1)S(1)} %copy.9), kind=kLoop, calls=%fused_computation | loop fusion | flops 1763328 | bytes 811008 | tf_op jit(solution)/shard_map/reduce_sum | solution.py:100
  11.5 0.0 copy-start
  11.5 1.5 %copy.11.pw_ref = bf16[6144,32]{1,0:T(8,128)(2,1)} copy(bf16[6144,32]{0,1:T(8,128)(2,1)S(1)} %get-tuple-element.19) | data formatting | bytes 786432 | tf_op jit(solution)/shard_map/concatenate | solution.py:299
  13.0 0.7 pad_maximum_fusion.1.v_ref
  13.7 0.0 copy-done
  13.7 0.0 copy-start.1
  13.7 0.0 copy-start.3
  13.7 35.3 %shard_map.67.k_ref = bf16[16,128,4224]{2,1,0:T(8,128)(2,1)} custom-call(s32[528]{0:T(1024)} %reshape.97.pat_ref, bf16[6144,32]{1,0:T(8,128)(2,1)} %copy.11.pw_ref, bf16[32,6144]{1,0:T(8,128)(2,1)} %bitcast.30, f32[1,6144]{1,0:T(1,128)} %bitcast.31), custom_call_target="tpu_custom_call" | custom-call | tf_op jit(solution)/shard_map/pallas_call | solution.py:101
  49.1 15.1 %shard_map.68 = f32[16,2048]{1,0:T(8,128)} custom-call(bf16[16,6144]{1,0:T(8,128)(2,1)} %pad_maximum_fusion.1.v_ref, bf16[16,128,4224]{2,1,0:T(8,128)(2,1)} %shard_map.67.k_ref), custom_call_target="tpu_custom_call" | custom-call | tf_op jit(solution)/shard_map/pallas_call | solution.py:125
  64.1 0.0 copy-done.1
  64.1 0.0 copy-done.3
  64.1 1.0 multiply_reduce_fusion.4
  65.2 1.3 collective-permute-start.3
  66.5 5.8 %collective-permute-start.2 = (bf16[16,2048]{1,0:T(8,128)(2,1)S(1)}, bf16[16,2048]{1,0:T(8,128)(2,1)S(1)}, u32[]{:S(2)}, u32[]{:S(2)}) collective-permute-start(bf16[16,2048]{1,0:T(8,128)(2,1)S(1)} %convert_element_type.14), channel_id=1, source_target_pairs={{0,4},{4,8},{8,12},{12,16},{16,20},{20,24},{24,28},{28,32},{32,36}... | collective-permute-start | bytes 196616 | tf_op jit(solution)/shard_map/ppermute | solution.py:26
  72.4 0.6 select_maximum_fusion.1.part_ref
  73.0 0.0 collective-permute-done.3
  73.0 0.3 collective-permute-done.2
  73.2 0.7 pad_maximum_fusion.2.v_ref
  73.9 41.7 %shard_map.69 = (f32[16,2048]{1,0:T(8,128)}, f32[8,128]{1,0:T(8,128)}) custom-call(bf16[16,6144]{1,0:T(8,128)(2,1)} %pad_maximum_fusion.2.v_ref, bf16[16,128,4224]{2,1,0:T(8,128)(2,1)} %shard_map.67.k_ref, f32[8,128]{1,0:T(8,128)} %select_maximum_fusion.1.part_ref), custom_call_target="tpu_custom_call" | custom-call | tf_op jit(solution)/shard_map/pallas_call | solution.py:257
  115.6 0.0 copy-start.2
  115.6 0.8 bitcast_divide_fusion.1
  116.4 1.1 multiply_reduce_fusion.2
  117.5 1.3 collective-permute-start.5
  118.8 3.0 %collective-permute-start.4 = (bf16[16,2048]{1,0:T(8,128)(2,1)S(1)}, bf16[16,2048]{1,0:T(8,128)(2,1)S(1)}, u32[]{:S(2)}, u32[]{:S(2)}) collective-permute-start(bf16[16,2048]{1,0:T(8,128)(2,1)S(1)} %get-tuple-element.22), channel_id=1, source_target_pairs={{0,4},{4,8},{8,12},{12,16},{16,20},{20,24},{24,28},{28,32},{32,36}... | collective-permute-start | bytes 196616 | tf_op jit(solution)/shard_map/ppermute | solution.py:26
  121.9 0.6 select_maximum_fusion.part_ref
  122.5 0.0 collective-permute-done.5
  122.5 0.3 collective-permute-done.4
  122.7 0.7 pad_maximum_fusion.3.v_ref
  123.4 23.3 %shard_map.70 = (f32[16,2048]{1,0:T(8,128)}, f32[8,128]{1,0:T(8,128)}) custom-call(bf16[16,6144]{1,0:T(8,128)(2,1)} %pad_maximum_fusion.3.v_ref, bf16[16,128,4224]{2,1,0:T(8,128)(2,1)} %shard_map.67.k_ref, f32[8,128]{1,0:T(8,128)} %select_maximum_fusion.part_ref), custom_call_target="tpu_custom_call" | custom-call | tf_op jit(solution)/shard_map/pallas_call | solution.py:257
  146.7 0.8 fusion.1
  147.5 0.0 copy-done.2
  147.5 1.8 %multiply_subtract_fusion = (f32[16,2048]{1,0:T(8,128)}, f32[16,2048]{1,0:T(8,128)}, f32[16,2048]{1,0:T(8,128)}) fusion(f32[16,2048]{1,0:T(8,128)} %get-tuple-element.10, f32[16,2048]{1,0:T(8,128)S(1)} %copy-done.2, f32[16,2048]{1,0:T(8,128)S(1)} %get-tuple-element.17, f32[16]{0:T(128)S(1)} %get-tuple-element.16, f32[16]{0:T(128)S(1)} %get-tuple-element.15, ...), kind=kLoop, calls=%fused_computation.5 | loop fusion | flops 753664 | bytes 925888 | tf_op jit(solution)/shard_map/sub | solution.py:358
  (10 shorter events, 0.2 us)
Async XLA Ops:
  3.1 5.7 %collective-permute-start.1 = (bf16[768,128]{1,0:T(8,128)(2,1)S(1)}, bf16[768,128]{1,0:T(8,128)(2,1)S(1)}, u32[]{:S(2)}, u32[]{:S(2)}) collective-permute-start(bf16[768,128]{1,0:T(8,128)(2,1)S(1)} %constant_dynamic-update-slice_fusion), channel_id=1, source_target_pairs={{4,0},{8,4},{12,8},{16,12},{20,16},{24,20},{28,24},{32,28},{36,32}... | collective-permute-start | bytes 589832 | tf_op jit(solution)/shard_map/ppermute | solution.py:298
  4.4 4.5 %collective-permute-start = (bf16[768,128]{1,0:T(8,128)(2,1)S(1)}, bf16[768,128]{1,0:T(8,128)(2,1)S(1)}, u32[]{:S(2)}, u32[]{:S(2)}) collective-permute-start(bf16[768,128]{1,0:T(8,128)(2,1)S(1)} %constant_dynamic-update-slice_fusion), channel_id=1, source_target_pairs={{0,4},{4,8},{8,12},{12,16},{16,20},{20,24},{24,28},{28,32},{32,36}... | collective-permute-start | bytes 589832 | tf_op jit(solution)/shard_map/ppermute | solution.py:297
  11.5 2.2 %copy-start = (bf16[6144,32]{0,1:T(8,128)(2,1)}, bf16[6144,32]{0,1:T(8,128)(2,1)S(1)}, u32[]{:S(2)}) copy-start(bf16[6144,32]{0,1:T(8,128)(2,1)S(1)} %get-tuple-element.19) | copy-start | bytes 1179652
  13.7 50.4 %copy-start.1 = (f32[16,2048]{1,0:T(8,128)S(1)}, f32[16,2048]{1,0:T(8,128)}, u32[]{:S(2)}) copy-start(f32[16,2048]{1,0:T(8,128)} %param.6) | copy-start | bytes 393220
  13.7 50.4 %copy-start.3 = (f32[2048]{0:T(1024)S(1)}, f32[2048]{0:T(1024)}, u32[]{:S(2)}) copy-start(f32[2048]{0:T(1024)} %param.5) | copy-start | bytes 24580
  65.2 7.7 %collective-permute-start.3 = (bf16[16,2048]{1,0:T(8,128)(2,1)S(1)}, bf16[16,2048]{1,0:T(8,128)(2,1)S(1)}, u32[]{:S(2)}, u32[]{:S(2)}) collective-permute-start(bf16[16,2048]{1,0:T(8,128)(2,1)S(1)} %convert_element_type.14), channel_id=1, source_target_pairs={{4,0},{8,4},{12,8},{16,12},{20,16},{24,20},{28,24},{32,28},{36,32}... | collective-permute-start | bytes 196616 | tf_op jit(solution)/shard_map/ppermute | solution.py:28
  66.5 6.7 %collective-permute-start.2 = (bf16[16,2048]{1,0:T(8,128)(2,1)S(1)}, bf16[16,2048]{1,0:T(8,128)(2,1)S(1)}, u32[]{:S(2)}, u32[]{:S(2)}) collective-permute-start(bf16[16,2048]{1,0:T(8,128)(2,1)S(1)} %convert_element_type.14), channel_id=1, source_target_pairs={{0,4},{4,8},{8,12},{12,16},{16,20},{20,24},{24,28},{28,32},{32,36}... | collective-permute-start | bytes 196616 | tf_op jit(solution)/shard_map/ppermute | solution.py:26
  115.6 31.9 %copy-start.2 = (f32[16,2048]{1,0:T(8,128)S(1)}, f32[16,2048]{1,0:T(8,128)}, u32[]{:S(2)}) copy-start(f32[16,2048]{1,0:T(8,128)} %get-tuple-element.8) | copy-start | bytes 393220
  117.5 4.9 %collective-permute-start.5 = (bf16[16,2048]{1,0:T(8,128)(2,1)S(1)}, bf16[16,2048]{1,0:T(8,128)(2,1)S(1)}, u32[]{:S(2)}, u32[]{:S(2)}) collective-permute-start(bf16[16,2048]{1,0:T(8,128)(2,1)S(1)} %get-tuple-element.22), channel_id=1, source_target_pairs={{4,0},{8,4},{12,8},{16,12},{20,16},{24,20},{28,24},{32,28},{36,32}... | collective-permute-start | bytes 196616 | tf_op jit(solution)/shard_map/ppermute | solution.py:28
  118.8 3.9 %collective-permute-start.4 = (bf16[16,2048]{1,0:T(8,128)(2,1)S(1)}, bf16[16,2048]{1,0:T(8,128)(2,1)S(1)}, u32[]{:S(2)}, u32[]{:S(2)}) collective-permute-start(bf16[16,2048]{1,0:T(8,128)(2,1)S(1)} %get-tuple-element.22), channel_id=1, source_target_pairs={{0,4},{4,8},{8,12},{12,16},{16,20},{20,24},{24,28},{28,32},{32,36}... | collective-permute-start | bytes 196616 | tf_op jit(solution)/shard_map/ppermute | solution.py:26

commit v10 on v9

--- a/solution.py
+++ b/solution.py
@@ -13,6 +13,7 @@
 ITERS = 2
 WIDE = 33
 WEXP = 18
+SLAB = 32
 MESH = pl.DeviceIdType.MESH
 
 
@@ -42,13 +43,13 @@
     return (b16 * b2) * (WEXP * radius + 1.0)
 
 
-def build_kernel(pat_ref, pw_ref, pwt_ref, sqr_ref, k_ref, mirror, cross_ref):
+def build_kernel(pat_ref, pw_ref, pwt_ref, sqr_ref, k_ref, mirror, cross_ref, sq_left_ref):
     a = pl.program_id(0)
     blocks = pl.num_programs(0)
     start = pl.multiple_of((a + REACH) * BLK, BLK)
     left = pw_ref[pl.ds(start, BLK), :]
     left_f = left.astype(jnp.float32)
-    sq_left = jnp.sum(left_f * left_f, axis=1, keepdims=True)
+    sq_left_ref[...] = jnp.sum(left_f * left_f, axis=1, keepdims=True)
     left_m2 = left * jnp.asarray(-2.0, jnp.bfloat16)
     window = pwt_ref[:, pl.ds(pl.multiple_of(a * BLK, BLK), WIDE * BLK)]
     cross_ref[...] = jnp.dot(left_m2, window, preferred_element_type=jnp.float32)
@@ -68,12 +69,14 @@
         @pl.when(jnp.logical_and(live, jnp.logical_not(lower)))
         def _():
             sq_right = sqr_ref[:, pl.ds(col, BLK)]
-            value = profile_tile(sq_left, sq_right, cross_ref[:, dst])
-            k_ref[0, :, dst] = value.astype(jnp.bfloat16)
+            for h in range(BLK // SLAB):
+                rows = pl.ds(h * SLAB, SLAB)
+                value = profile_tile(sq_left_ref[rows, :], sq_right, cross_ref[rows, dst])
+                k_ref[0, rows, dst] = value.astype(jnp.bfloat16)
 
             @pl.when(upper)
             def _():
-                mirror[other, a] = value.T.astype(jnp.bfloat16)
+                mirror[other, a] = k_ref[0, :, dst].astype(jnp.float32).T.astype(jnp.bfloat16)
 
         @pl.when(jnp.logical_not(live))
         def _():
@@ -113,6 +116,7 @@
             scratch_shapes=[
                 pltpu.VMEM((blocks, blocks, BLK, BLK), jnp.bfloat16),
                 pltpu.VMEM((BLK, WIDE * BLK), jnp.float32),
+                pltpu.VMEM((BLK, 1), jnp.float32),
             ],
         ),
         compiler_params=pltpu.CompilerParams(dimension_semantics=("arbitrary",)),

time: 151 us -> 164 us (1.086)
  Pallas kernels: 115 us -> 122 us
  starting transfers between devices: 15.8 us -> 22.4 us
    pallas_call x1, Pallas kernels: 35.3 us -> 43.9 us  [build_k(): pl.pallas_call(build_kernel, out_shape=jax.ShapeDtypeStruct((blocks, BLK,...]
    ppermute x2, starting transfers between devices: 8.87 us -> 15.5 us  [with_halo(): lax.ppermute(tail, axis, [(i, (i + 1) % count) for i in range(ends)])]
    pallas_call x2, Pallas kernels: 65 us -> 63.2 us  [apply_sum(): pl.pallas_call(functools.partial(apply_sum_kernel, inner, outer), out_sha...]
where the time goes in v10:
time: 164 us; the launch traced here: 163 us
  Pallas kernels  122 us (74%)
  starting transfers between devices  22.4 us (14%)
  other arithmetic  11.3 us (7%)
  local copies, waits for them, and re-layouts  5.4 us (3%)
    pallas_call x2, Pallas kernels, apply_sum(): pl.pallas_call(functools.partial(apply_sum_kernel, inner, outer), out_sha...  63.2 us
    pallas_call x1, Pallas kernels, build_k(): pl.pallas_call(build_kernel, out_shape=jax.ShapeDtypeStruct((blocks, BLK,...  43.9 us
    ppermute x2, starting transfers between devices, with_halo(): lax.ppermute(tail, axis, [(i, (i + 1) % count) for i in range(ends)])  15.5 us
    pallas_call x1, Pallas kernels, apply_k(): pl.pallas_call(apply_kernel, out_shape=jax.ShapeDtypeStruct((rows, blocks...  15.1 us
  transfers between devices with their start and end apart: 6, of which 2 were waited for; matrix products, arithmetic and copies ran while one was open for 2% of the time, Pallas kernels for 0%

profile of v10, /device:TPU:16, one launch (start us, length us, event | category | flops | bytes accessed | tf_op | source)
XLA Modules:
  0.0 162.7 jit_solution(3324765132477782786)
XLA Ops:
  0.6 0.9 convert_element_type.12
  1.6 1.2 copy.8
  2.8 0.3 reshape.93
  3.1 1.3 collective-permute-start.1
  4.4 3.0 %collective-permute-start = (bf16[768,128]{1,0:T(8,128)(2,1)S(1)}, bf16[768,128]{1,0:T(8,128)(2,1)S(1)}, u32[]{:S(2)}, u32[]{:S(2)}) collective-permute-start(bf16[768,128]{1,0:T(8,128)(2,1)S(1)} %constant_dynamic-update-slice_fusion), channel_id=1, source_target_pairs={{0,4},{4,8},{8,12},{12,16},{16,20},{20,24},{24,28},{28,32},{32,36}... | collective-permute-start | bytes 589832 | tf_op jit(solution)/shard_map/ppermute | solution.py:301
  7.4 1.4 reshape.97.pat_ref
  8.8 0.0 collective-permute-done.1
  8.9 0.0 collective-permute-done
  9.0 0.2 reshape.98
  9.2 0.2 copy.9
  9.4 0.2 reshape.99
  9.7 0.2 copy.10
  9.8 1.6 %multiply_reduce_fusion = (f32[6144]{0:T(1024)}, bf16[6144,32]{0,1:T(8,128)(2,1)S(1)}) fusion(bf16[2048,32]{0,1:T(8,128)(2,1)S(1)} %copy.10, bf16[2048,32]{0,1:T(8,128)(2,1)} %param.4, bf16[2048,32]{0,1:T(8,128)(2,1)S(1)} %copy.9), kind=kLoop, calls=%fused_computation | loop fusion | flops 1763328 | bytes 811008 | tf_op jit(solution)/shard_map/reduce_sum | solution.py:103
  11.5 0.0 copy-start
  11.5 1.5 copy.11.pw_ref
  13.0 0.7 pad_maximum_fusion.1.v_ref
  13.7 0.0 copy-done
  13.7 0.0 copy-start.1
  13.7 0.0 copy-start.3
  13.7 43.9 %shard_map.67.k_ref = bf16[16,128,4224]{2,1,0:T(8,128)(2,1)} custom-call(s32[528]{0:T(1024)} %reshape.97.pat_ref, bf16[6144,32]{1,0:T(8,128)(2,1)} %copy.11.pw_ref, bf16[32,6144]{1,0:T(8,128)(2,1)} %bitcast.30, f32[1,6144]{1,0:T(1,128)} %bitcast.31), custom_call_target="tpu_custom_call" | custom-call | tf_op jit(solution)/shard_map/pallas_call | solution.py:104
  57.6 15.1 %shard_map.68 = f32[16,2048]{1,0:T(8,128)} custom-call(bf16[16,6144]{1,0:T(8,128)(2,1)} %pad_maximum_fusion.1.v_ref, bf16[16,128,4224]{2,1,0:T(8,128)(2,1)} %shard_map.67.k_ref), custom_call_target="tpu_custom_call" | custom-call | tf_op jit(solution)/shard_map/pallas_call | solution.py:129
  72.7 0.0 copy-done.1
  72.7 0.0 copy-done.3
  72.7 1.0 multiply_reduce_fusion.4
  73.8 1.3 collective-permute-start.3
  75.1 12.5 %collective-permute-start.2 = (bf16[16,2048]{1,0:T(8,128)(2,1)S(1)}, bf16[16,2048]{1,0:T(8,128)(2,1)S(1)}, u32[]{:S(2)}, u32[]{:S(2)}) collective-permute-start(bf16[16,2048]{1,0:T(8,128)(2,1)S(1)} %convert_element_type.14), channel_id=1, source_target_pairs={{0,4},{4,8},{8,12},{12,16},{16,20},{20,24},{24,28},{28,32},{32,36}... | collective-permute-start | bytes 196616 | tf_op jit(solution)/shard_map/ppermute | solution.py:27
  87.6 0.6 select_maximum_fusion.1.part_ref
  88.2 0.0 collective-permute-done.3
  88.2 0.3 collective-permute-done.2
  88.5 0.7 pad_maximum_fusion.2.v_ref
  89.2 39.0 %shard_map.69 = (f32[16,2048]{1,0:T(8,128)}, f32[8,128]{1,0:T(8,128)}) custom-call(bf16[16,6144]{1,0:T(8,128)(2,1)} %pad_maximum_fusion.2.v_ref, bf16[16,128,4224]{2,1,0:T(8,128)(2,1)} %shard_map.67.k_ref, f32[8,128]{1,0:T(8,128)} %select_maximum_fusion.1.part_ref), custom_call_target="tpu_custom_call" | custom-call | tf_op jit(solution)/shard_map/pallas_call | solution.py:261
  128.1 0.0 copy-start.2
  128.1 0.8 bitcast_divide_fusion.1
  128.9 1.1 multiply_reduce_fusion.2
  130.0 1.3 collective-permute-start.5
  131.3 3.0 %collective-permute-start.4 = (bf16[16,2048]{1,0:T(8,128)(2,1)S(1)}, bf16[16,2048]{1,0:T(8,128)(2,1)S(1)}, u32[]{:S(2)}, u32[]{:S(2)}) collective-permute-start(bf16[16,2048]{1,0:T(8,128)(2,1)S(1)} %get-tuple-element.22), channel_id=1, source_target_pairs={{0,4},{4,8},{8,12},{12,16},{16,20},{20,24},{24,28},{28,32},{32,36}... | collective-permute-start | bytes 196616 | tf_op jit(solution)/shard_map/ppermute | solution.py:27
  134.4 0.6 select_maximum_fusion.part_ref
  135.0 0.0 collective-permute-done.5
  135.0 0.3 collective-permute-done.4
  135.2 0.7 pad_maximum_fusion.3.v_ref
  135.9 24.2 %shard_map.70 = (f32[16,2048]{1,0:T(8,128)}, f32[8,128]{1,0:T(8,128)}) custom-call(bf16[16,6144]{1,0:T(8,128)(2,1)} %pad_maximum_fusion.3.v_ref, bf16[16,128,4224]{2,1,0:T(8,128)(2,1)} %shard_map.67.k_ref, f32[8,128]{1,0:T(8,128)} %select_maximum_fusion.part_ref), custom_call_target="tpu_custom_call" | custom-call | tf_op jit(solution)/shard_map/pallas_call | solution.py:261
  160.2 0.8 fusion.1
  160.9 0.0 copy-done.2
  161.0 1.8 %multiply_subtract_fusion = (f32[16,2048]{1,0:T(8,128)}, f32[16,2048]{1,0:T(8,128)}, f32[16,2048]{1,0:T(8,128)}) fusion(f32[16,2048]{1,0:T(8,128)} %get-tuple-element.10, f32[16,2048]{1,0:T(8,128)S(1)} %copy-done.2, f32[16,2048]{1,0:T(8,128)S(1)} %get-tuple-element.17, f32[16]{0:T(128)S(1)} %get-tuple-element.16, f32[16]{0:T(128)S(1)} %get-tuple-element.15, ...), kind=kLoop, calls=%fused_computation.5 | loop fusion | flops 753664 | bytes 925888 | tf_op jit(solution)/shard_map/sub | solution.py:362
  (10 shorter events, 0.2 us)
Async XLA Ops:
  3.1 5.7 %collective-permute-start.1 = (bf16[768,128]{1,0:T(8,128)(2,1)S(1)}, bf16[768,128]{1,0:T(8,128)(2,1)S(1)}, u32[]{:S(2)}, u32[]{:S(2)}) collective-permute-start(bf16[768,128]{1,0:T(8,128)(2,1)S(1)} %constant_dynamic-update-slice_fusion), channel_id=1, source_target_pairs={{4,0},{8,4},{12,8},{16,12},{20,16},{24,20},{28,24},{32,28},{36,32}... | collective-permute-start | bytes 589832 | tf_op jit(solution)/shard_map/ppermute | solution.py:302
  4.4 4.5 %collective-permute-start = (bf16[768,128]{1,0:T(8,128)(2,1)S(1)}, bf16[768,128]{1,0:T(8,128)(2,1)S(1)}, u32[]{:S(2)}, u32[]{:S(2)}) collective-permute-start(bf16[768,128]{1,0:T(8,128)(2,1)S(1)} %constant_dynamic-update-slice_fusion), channel_id=1, source_target_pairs={{0,4},{4,8},{8,12},{12,16},{16,20},{20,24},{24,28},{28,32},{32,36}... | collective-permute-start | bytes 589832 | tf_op jit(solution)/shard_map/ppermute | solution.py:301
  11.5 2.2 %copy-start = (bf16[6144,32]{0,1:T(8,128)(2,1)}, bf16[6144,32]{0,1:T(8,128)(2,1)S(1)}, u32[]{:S(2)}) copy-start(bf16[6144,32]{0,1:T(8,128)(2,1)S(1)} %get-tuple-element.19) | copy-start | bytes 1179652
  13.7 59.0 %copy-start.1 = (f32[16,2048]{1,0:T(8,128)S(1)}, f32[16,2048]{1,0:T(8,128)}, u32[]{:S(2)}) copy-start(f32[16,2048]{1,0:T(8,128)} %param.6) | copy-start | bytes 393220
  13.7 59.0 %copy-start.3 = (f32[2048]{0:T(1024)S(1)}, f32[2048]{0:T(1024)}, u32[]{:S(2)}) copy-start(f32[2048]{0:T(1024)} %param.5) | copy-start | bytes 24580
  73.8 14.4 %collective-permute-start.3 = (bf16[16,2048]{1,0:T(8,128)(2,1)S(1)}, bf16[16,2048]{1,0:T(8,128)(2,1)S(1)}, u32[]{:S(2)}, u32[]{:S(2)}) collective-permute-start(bf16[16,2048]{1,0:T(8,128)(2,1)S(1)} %convert_element_type.14), channel_id=1, source_target_pairs={{4,0},{8,4},{12,8},{16,12},{20,16},{24,20},{28,24},{32,28},{36,32}... | collective-permute-start | bytes 196616 | tf_op jit(solution)/shard_map/ppermute | solution.py:29
  75.1 13.4 %collective-permute-start.2 = (bf16[16,2048]{1,0:T(8,128)(2,1)S(1)}, bf16[16,2048]{1,0:T(8,128)(2,1)S(1)}, u32[]{:S(2)}, u32[]{:S(2)}) collective-permute-start(bf16[16,2048]{1,0:T(8,128)(2,1)S(1)} %convert_element_type.14), channel_id=1, source_target_pairs={{0,4},{4,8},{8,12},{12,16},{16,20},{20,24},{24,28},{28,32},{32,36}... | collective-permute-start | bytes 196616 | tf_op jit(solution)/shard_map/ppermute | solution.py:27
  128.1 32.8 %copy-start.2 = (f32[16,2048]{1,0:T(8,128)S(1)}, f32[16,2048]{1,0:T(8,128)}, u32[]{:S(2)}) copy-start(f32[16,2048]{1,0:T(8,128)} %get-tuple-element.8) | copy-start | bytes 393220
  130.0 4.9 %collective-permute-start.5 = (bf16[16,2048]{1,0:T(8,128)(2,1)S(1)}, bf16[16,2048]{1,0:T(8,128)(2,1)S(1)}, u32[]{:S(2)}, u32[]{:S(2)}) collective-permute-start(bf16[16,2048]{1,0:T(8,128)(2,1)S(1)} %get-tuple-element.22), channel_id=1, source_target_pairs={{4,0},{8,4},{12,8},{16,12},{20,16},{24,20},{28,24},{32,28},{36,32}... | collective-permute-start | bytes 196616 | tf_op jit(solution)/shard_map/ppermute | solution.py:29
  131.3 3.9 %collective-permute-start.4 = (bf16[16,2048]{1,0:T(8,128)(2,1)S(1)}, bf16[16,2048]{1,0:T(8,128)(2,1)S(1)}, u32[]{:S(2)}, u32[]{:S(2)}) collective-permute-start(bf16[16,2048]{1,0:T(8,128)(2,1)S(1)} %get-tuple-element.22), channel_id=1, source_target_pairs={{0,4},{4,8},{8,12},{12,16},{16,20},{20,24},{24,28},{28,32},{32,36}... | collective-permute-start | bytes 196616 | tf_op jit(solution)/shard_map/ppermute | solution.py:27

commit v11 on v9

--- a/solution.py
+++ b/solution.py
@@ -181,7 +181,6 @@
     own2 = pltpu.make_async_copy(stage1, stage2.at[zc], local_sem.at[1])
 
     def start_first():
-        pl.semaphore_wait(pltpu.get_barrier_semaphore(), (inner - 1) + (outer - 1))
         own1.start()
 
         def send_first(k, carry):
@@ -221,15 +220,116 @@
     return greet, start_first, start_second, finish
 
 
-def apply_sum_kernel(inner, outer, v_ref, k_ref, part_ref, out_ref, sum_ref, *scratch):
+def apply_sum_kernel(inner, outer, vloc_ref, k_ref, part_ref, out_ref, sum_ref, v_ref, halo_send, halo_recv, halo_local, *scratch):
     a = pl.program_id(0)
     last = pl.num_programs(0) - 1
     greet, start_first, start_second, finish = reduction_steps(inner, outer, part_ref, *scratch)
+    me = lax.axis_index("pts")
+    row = lax.axis_index("rhs")
+    count = inner * outer
+    rc = me % inner
+    width = vloc_ref.shape[1]
+    has_left = me > 0
+    has_right = me < count - 1
+    extra = jnp.logical_or(
+        jnp.logical_and(rc == 0, has_left), jnp.logical_and(rc == inner - 1, has_right)
+    )
+
+    def to_right():
+        return pltpu.make_async_remote_copy(
+            src_ref=vloc_ref,
+            dst_ref=v_ref.at[:, pl.ds(0, width)],
+            send_sem=halo_send.at[0],
+            recv_sem=halo_recv.at[0],
+            device_id=(me + 1, row),
+            device_id_type=MESH,
+        )
+
+    def to_left():
+        return pltpu.make_async_remote_copy(
+            src_ref=vloc_ref,
+            dst_ref=v_ref.at[:, pl.ds(2 * width, width)],
+            send_sem=halo_send.at[1],
+            recv_sem=halo_recv.at[1],
+            device_id=(me - 1, row),
+            device_id_type=MESH,
+        )
+
+    def from_left():
+        return pltpu.make_async_remote_copy(
+            src_ref=vloc_ref,
+            dst_ref=v_ref.at[:, pl.ds(0, width)],
+            send_sem=halo_send.at[0],
+            recv_sem=halo_recv.at[0],
+            device_id=(me - 1, row),
+            device_id_type=MESH,
+        )
+
+    def from_right():
+        return pltpu.make_async_remote_copy(
+            src_ref=vloc_ref,
+            dst_ref=v_ref.at[:, pl.ds(2 * width, width)],
+            send_sem=halo_send.at[1],
+            recv_sem=halo_recv.at[1],
+            device_id=(me + 1, row),
+            device_id_type=MESH,
+        )
+
+    own = pltpu.make_async_copy(vloc_ref, v_ref.at[:, pl.ds(width, width)], halo_local.at[0])
 
     @pl.when(a == 0)
     def _():
         greet()
+        barrier = pltpu.get_barrier_semaphore()
+
+        @pl.when(jnp.logical_and(extra, rc == 0))
+        def _():
+            pl.semaphore_signal(barrier, inc=1, device_id=(me - 1, row), device_id_type=MESH)
+
+        @pl.when(jnp.logical_and(extra, rc == inner - 1))
+        def _():
+            pl.semaphore_signal(barrier, inc=1, device_id=(me + 1, row), device_id_type=MESH)
+
+        peers = (inner - 1) + (outer - 1)
+
+        @pl.when(extra)
+        def _():
+            pl.semaphore_wait(barrier, peers + 1)
+
+        @pl.when(jnp.logical_not(extra))
+        def _():
+            pl.semaphore_wait(barrier, peers)
+
         start_first()
+        own.start()
+
+        @pl.when(has_right)
+        def _():
+            to_right().start()
+
+        @pl.when(has_left)
+        def _():
+            to_left().start()
+
+        @pl.when(jnp.logical_not(has_left))
+        def _():
+            v_ref[:, pl.ds(0, width)] = jnp.zeros((v_ref.shape[0], width), v_ref.dtype)
+
+        @pl.when(jnp.logical_not(has_right))
+        def _():
+            v_ref[:, pl.ds(2 * width, width)] = jnp.zeros((v_ref.shape[0], width), v_ref.dtype)
+
+        own.wait()
+
+        @pl.when(has_right)
+        def _():
+            to_right().wait_send()
+            from_right().wait_recv()
+
+        @pl.when(has_left)
+        def _():
+            to_left().wait_send()
+            from_left().wait_recv()
 
     blocks = v_ref.shape[1] // BLK - 2 * REACH
 
@@ -248,8 +348,9 @@
         sum_ref[...] = finish()
 
 
-def apply_sum(wide_vec, kmat, tile):
-    rows, wide_cols = wide_vec.shape
+def apply_sum(local_vec, kmat, tile):
+    rows, width = local_vec.shape
+    wide_cols = width + 2 * REACH * BLK
     blocks = kmat.shape[0]
     count = lax.axis_size("pts")
     inner = 8 if count % 8 == 0 else count
@@ -262,7 +363,7 @@
         ),
         grid=(blocks,),
         in_specs=[
-            pl.BlockSpec((rows, wide_cols), lambda a: (0, 0)),
+            pl.BlockSpec((rows, width), lambda a: (0, 0)),
             pl.BlockSpec((1, BLK, WIDE * BLK), lambda a: (a, 0, 0)),
             pl.BlockSpec(tile.shape, lambda a: (0, 0)),
         ],
@@ -271,6 +372,10 @@
             pl.BlockSpec(tile.shape, lambda a: (0, 0)),
         ),
         scratch_shapes=[
+            pltpu.VMEM((rows, wide_cols), local_vec.dtype),
+            pltpu.SemaphoreType.DMA((2,)),
+            pltpu.SemaphoreType.DMA((2,)),
+            pltpu.SemaphoreType.DMA((1,)),
             pltpu.VMEM((inner,) + tile.shape, jnp.float32),
             pltpu.VMEM((outer, inner) + tile.shape, jnp.float32),
             pltpu.SemaphoreType.DMA((2,)),
@@ -282,7 +387,7 @@
         compiler_params=pltpu.CompilerParams(
             dimension_semantics=("arbitrary",), collective_id=0, has_side_effects=True
         ),
-    )(wide_vec, kmat, tile)
+    )(local_vec, kmat, tile)
 
 
 def per_device(points, noise_var, right_side, pattern):
@@ -322,8 +427,7 @@
         tile = jnp.zeros((8, 128), jnp.float32)
         tile = lax.dynamic_update_slice(tile, parts, (0, 0))
         vec_low = vector.astype(jnp.bfloat16)
-        wide_vec = with_halo(vec_low, "pts", 1, rim_rows)
-        image_part, summed = apply_sum(wide_vec, kmat, tile)
+        image_part, summed = apply_sum(vec_low, kmat, tile)
         image = noise_var[None, :] * vector + kernel_scale * image_part
         return image, summed[: parts.shape[0], : parts.shape[1]]
 

time: 151 us -> 137 us (0.907)
  starting transfers between devices: 15.8 us -> 4.33 us
  Pallas kernels: 115 us -> 113 us
    ppermute x4 -> x0, starting transfers between devices: 11.4 us -> none  [the longest x2 8.87 us: with_halo(): lax.ppermute(tail, axis, [(i, (i + 1) % count) for i in range(ends)])]
    pallas_call x1, Pallas kernels: 35.3 us -> 33.5 us  [build_k(): pl.pallas_call(build_kernel, out_shape=jax.ShapeDtypeStruct((blocks, BLK,...]
  transfers between devices with their start and end apart: 6 -> 2, of which waited for: 2 -> 0; matrix products, arithmetic and copies ran while one was open for 2% -> 1% of each run, Pallas kernels for 0% -> 0%
where the time goes in v11:
time: 137 us; the launch traced here: 135 us
  Pallas kernels  113 us (82%)
  other arithmetic  11.2 us (8%)
  local copies, waits for them, and re-layouts  5.41 us (4%)
  starting transfers between devices  4.33 us (3%)
    pallas_call x2, Pallas kernels, apply_sum(): pl.pallas_call(functools.partial(apply_sum_kernel, inner, outer), out_sha...  64.8 us
    pallas_call x1, Pallas kernels, build_k(): pl.pallas_call(build_kernel, out_shape=jax.ShapeDtypeStruct((blocks, BLK,...  33.5 us
    pallas_call x1, Pallas kernels, apply_k(): pl.pallas_call(apply_kernel, out_shape=jax.ShapeDtypeStruct((rows, blocks...  15.1 us
    ppermute x1, starting transfers between devices, per_device(): lax.ppermute(packed, 'pts', [(i, i + 1) for i in range(count - 1)])  3.04 us
    reduce_sum x2, other arithmetic, per_device(): jnp.sum(residual * residual, axis=1)  2.8 us
  transfers between devices with their start and end apart: 2, of which 0 were waited for; matrix products, arithmetic and copies ran while one was open for 1% of the time, Pallas kernels for 0%

profile of v11, /device:TPU:16, one launch (start us, length us, event | category | flops | bytes accessed | tf_op | source)
XLA Modules:
  0.0 135.1 jit_solution(7328851072481921569)
XLA Ops:
  0.6 0.9 convert_element_type.12
  1.6 1.2 copy.8
  2.8 0.3 reshape.93
  3.1 1.3 collective-permute-start.1
  4.4 3.0 %collective-permute-start = (bf16[768,128]{1,0:T(8,128)(2,1)S(1)}, bf16[768,128]{1,0:T(8,128)(2,1)S(1)}, u32[]{:S(2)}, u32[]{:S(2)}) collective-permute-start(bf16[768,128]{1,0:T(8,128)(2,1)S(1)} %constant_dynamic-update-slice_fusion), channel_id=1, source_target_pairs={{0,4},{4,8},{8,12},{12,16},{16,20},{20,24},{24,28},{28,32},{32,36}... | collective-permute-start | bytes 589832 | tf_op jit(solution)/shard_map/ppermute | solution.py:402
  7.4 1.4 %reshape.97.pat_ref = s32[528]{0:T(1024)} reshape(s32[16,33]{1,0:T(8,128)} %param.7) | data formatting | bytes 4224 | tf_op jit(solution)/shard_map/reshape | solution.py:415
  8.8 0.0 collective-permute-done.1
  8.9 0.0 collective-permute-done
  9.0 0.2 reshape.98
  9.2 0.2 copy.9
  9.4 0.2 reshape.99
  9.7 0.2 copy.10
  9.8 1.6 %multiply_reduce_fusion = (f32[6144]{0:T(1024)}, bf16[6144,32]{0,1:T(8,128)(2,1)S(1)}) fusion(bf16[2048,32]{0,1:T(8,128)(2,1)S(1)} %copy.10, bf16[2048,32]{0,1:T(8,128)(2,1)} %param.4, bf16[2048,32]{0,1:T(8,128)(2,1)S(1)} %copy.9), kind=kLoop, calls=%fused_computation | loop fusion | flops 1763328 | bytes 811008 | tf_op jit(solution)/shard_map/reduce_sum | solution.py:100
  11.5 0.0 copy-start
  11.5 1.6 %copy.11.pw_ref = bf16[6144,32]{1,0:T(8,128)(2,1)} copy(bf16[6144,32]{0,1:T(8,128)(2,1)S(1)} %get-tuple-element.19) | data formatting | bytes 786432 | tf_op jit(solution)/shard_map/concatenate | solution.py:404
  13.0 0.7 pad_maximum_fusion.1.v_ref
  13.7 0.0 copy-done
  13.7 0.0 copy-start.1
  13.7 0.0 copy-start.3
  13.7 33.5 %shard_map.67.k_ref = bf16[16,128,4224]{2,1,0:T(8,128)(2,1)} custom-call(s32[528]{0:T(1024)} %reshape.97.pat_ref, bf16[6144,32]{1,0:T(8,128)(2,1)} %copy.11.pw_ref, bf16[32,6144]{1,0:T(8,128)(2,1)} %bitcast.30, f32[1,6144]{1,0:T(1,128)} %bitcast.31), custom_call_target="tpu_custom_call" | custom-call | tf_op jit(solution)/shard_map/pallas_call | solution.py:101
  47.3 15.1 %shard_map.68 = f32[16,2048]{1,0:T(8,128)} custom-call(bf16[16,6144]{1,0:T(8,128)(2,1)} %pad_maximum_fusion.1.v_ref, bf16[16,128,4224]{2,1,0:T(8,128)(2,1)} %shard_map.67.k_ref), custom_call_target="tpu_custom_call" | custom-call | tf_op jit(solution)/shard_map/pallas_call | solution.py:125
  62.3 0.0 copy-done.1
  62.3 0.0 copy-done.3
  62.3 1.0 multiply_reduce_fusion.4
  63.4 0.6 convert_element_type.14.vloc_ref
  64.0 0.6 select_maximum_fusion.1.part_ref
  64.6 41.9 %shard_map.69 = (f32[16,2048]{1,0:T(8,128)}, f32[8,128]{1,0:T(8,128)}) custom-call(bf16[16,2048]{1,0:T(8,128)(2,1)} %convert_element_type.14.vloc_ref, bf16[16,128,4224]{2,1,0:T(8,128)(2,1)} %shard_map.67.k_ref, f32[8,128]{1,0:T(8,128)} %select_maximum_fusion.1.part_ref), custom_call_target="tpu_custom_call" | custom-call | tf_op jit(solution)/shard_map/pallas_call | solution.py:358
  106.6 0.0 copy-start.2
  106.6 0.8 bitcast_divide_fusion.1
  107.3 1.8 %multiply_reduce_fusion.2 = (f32[16]{0:T(128)S(1)}, f32[16]{0:T(128)S(1)}, bf16[16,2048]{1,0:T(8,128)(2,1)}) fusion(f32[16,2048]{1,0:T(8,128)S(1)} %copy-done.1, f32[16,2048]{1,0:T(8,128)S(1)} %get-tuple-element.17, f32[16]{0:T(128)S(1)} %bitcast_divide_fusion.1, f32[16,2048]{1,0:T(8,128)} %get-tuple-element.8, f32[2048]{0:T(1024)S(1)} %copy-done.3), kind=kLoop, calls=%fused_computation.7 | loop fusion | flops 393184 | bytes 467136 | tf_op jit(solution)/shard_map/reduce_sum | solution.py:445
  109.1 0.6 select_maximum_fusion.part_ref
  109.7 22.9 %shard_map.70 = (f32[16,2048]{1,0:T(8,128)}, f32[8,128]{1,0:T(8,128)}) custom-call(bf16[16,2048]{1,0:T(8,128)(2,1)} %get-tuple-element.22.vloc_ref, bf16[16,128,4224]{2,1,0:T(8,128)(2,1)} %shard_map.67.k_ref, f32[8,128]{1,0:T(8,128)} %select_maximum_fusion.part_ref), custom_call_target="tpu_custom_call" | custom-call | tf_op jit(solution)/shard_map/pallas_call | solution.py:358
  132.6 0.8 fusion.1
  133.4 0.0 copy-done.2
  133.4 1.8 %multiply_subtract_fusion = (f32[16,2048]{1,0:T(8,128)}, f32[16,2048]{1,0:T(8,128)}, f32[16,2048]{1,0:T(8,128)}) fusion(f32[16,2048]{1,0:T(8,128)} %get-tuple-element.10, f32[16,2048]{1,0:T(8,128)S(1)} %copy-done.2, f32[16,2048]{1,0:T(8,128)S(1)} %get-tuple-element.17, f32[16]{0:T(128)S(1)} %get-tuple-element.16, f32[16]{0:T(128)S(1)} %get-tuple-element.15, ...), kind=kLoop, calls=%fused_computation.3 | loop fusion | flops 753664 | bytes 925888 | tf_op jit(solution)/shard_map/sub | solution.py:462
  (9 shorter events, 0.2 us)
Async XLA Ops:
  3.1 5.7 %collective-permute-start.1 = (bf16[768,128]{1,0:T(8,128)(2,1)S(1)}, bf16[768,128]{1,0:T(8,128)(2,1)S(1)}, u32[]{:S(2)}, u32[]{:S(2)}) collective-permute-start(bf16[768,128]{1,0:T(8,128)(2,1)S(1)} %constant_dynamic-update-slice_fusion), channel_id=1, source_target_pairs={{4,0},{8,4},{12,8},{16,12},{20,16},{24,20},{28,24},{32,28},{36,32}... | collective-permute-start | bytes 589832 | tf_op jit(solution)/shard_map/ppermute | solution.py:403
  4.4 4.5 %collective-permute-start = (bf16[768,128]{1,0:T(8,128)(2,1)S(1)}, bf16[768,128]{1,0:T(8,128)(2,1)S(1)}, u32[]{:S(2)}, u32[]{:S(2)}) collective-permute-start(bf16[768,128]{1,0:T(8,128)(2,1)S(1)} %constant_dynamic-update-slice_fusion), channel_id=1, source_target_pairs={{0,4},{4,8},{8,12},{12,16},{16,20},{20,24},{24,28},{28,32},{32,36}... | collective-permute-start | bytes 589832 | tf_op jit(solution)/shard_map/ppermute | solution.py:402
  11.5 2.2 %copy-start = (bf16[6144,32]{0,1:T(8,128)(2,1)}, bf16[6144,32]{0,1:T(8,128)(2,1)S(1)}, u32[]{:S(2)}) copy-start(bf16[6144,32]{0,1:T(8,128)(2,1)S(1)} %get-tuple-element.19) | copy-start | bytes 1179652
  13.7 48.6 %copy-start.1 = (f32[16,2048]{1,0:T(8,128)S(1)}, f32[16,2048]{1,0:T(8,128)}, u32[]{:S(2)}) copy-start(f32[16,2048]{1,0:T(8,128)} %param.6) | copy-start | bytes 393220
  13.7 48.6 %copy-start.3 = (f32[2048]{0:T(1024)S(1)}, f32[2048]{0:T(1024)}, u32[]{:S(2)}) copy-start(f32[2048]{0:T(1024)} %param.5) | copy-start | bytes 24580
  106.6 26.8 %copy-start.2 = (f32[16,2048]{1,0:T(8,128)S(1)}, f32[16,2048]{1,0:T(8,128)}, u32[]{:S(2)}) copy-start(f32[16,2048]{1,0:T(8,128)} %get-tuple-element.8) | copy-start | bytes 393220

commit v12 on v11

--- a/solution.py
+++ b/solution.py
@@ -42,21 +42,23 @@
     return (b16 * b2) * (WEXP * radius + 1.0)
 
 
-def build_kernel(pat_ref, pw_ref, pwt_ref, sqr_ref, k_ref, mirror, cross_ref):
+def build_kernel(pat_ref, pw_ref, pwt_ref, k_ref, mirror, cross_ref, sqr_ref):
     a = pl.program_id(0)
     blocks = pl.num_programs(0)
-    start = pl.multiple_of((a + REACH) * BLK, BLK)
+    start = pl.multiple_of(a * BLK, BLK)
     left = pw_ref[pl.ds(start, BLK), :]
     left_f = left.astype(jnp.float32)
     sq_left = jnp.sum(left_f * left_f, axis=1, keepdims=True)
     left_m2 = left * jnp.asarray(-2.0, jnp.bfloat16)
     window = pwt_ref[:, pl.ds(pl.multiple_of(a * BLK, BLK), WIDE * BLK)]
     cross_ref[...] = jnp.dot(left_m2, window, preferred_element_type=jnp.float32)
+    window_f = window.astype(jnp.float32)
+    sqr_ref[...] = jnp.sum(window_f * window_f, axis=0, keepdims=True)
 
     def body(o, carry):
         col = pl.multiple_of((a + o) * BLK, BLK)
         dst = pl.ds(pl.multiple_of(o * BLK, BLK), BLK)
-        live = pat_ref[a * WIDE + o] != 0
+        live = pat_ref[a, o] != 0
         other = a + o - REACH
         lower = jnp.logical_and(other >= 0, other < a)
         upper = jnp.logical_and(other > a, other < blocks)
@@ -67,7 +69,7 @@
 
         @pl.when(jnp.logical_and(live, jnp.logical_not(lower)))
         def _():
-            sq_right = sqr_ref[:, pl.ds(col, BLK)]
+            sq_right = sqr_ref[:, dst]
             value = profile_tile(sq_left, sq_right, cross_ref[:, dst])
             k_ref[0, :, dst] = value.astype(jnp.bfloat16)
 
@@ -93,11 +95,9 @@
     )
 
 
-def build_k(pattern_flat, wide_points, blocks):
-    wide_rows = wide_points.shape[0]
-    wide_points_t = wide_points.T
-    wide_f = wide_points_t.astype(jnp.float32)
-    sq_row = jnp.sum(wide_f * wide_f, axis=0, keepdims=True)
+def build_k(pattern, points, wide_points_t, blocks):
+    rows = points.shape[0]
+    wide_cols = wide_points_t.shape[1]
     return pl.pallas_call(
         build_kernel,
         out_shape=jax.ShapeDtypeStruct((blocks, BLK, WIDE * BLK), jnp.bfloat16),
@@ -105,18 +105,18 @@
             num_scalar_prefetch=1,
             grid=(blocks,),
             in_specs=[
-                pl.BlockSpec((wide_rows, F), lambda a, p: (0, 0)),
-                pl.BlockSpec((F, wide_rows), lambda a, p: (0, 0)),
-                pl.BlockSpec((1, wide_rows), lambda a, p: (0, 0)),
+                pl.BlockSpec((rows, F), lambda a, p: (0, 0)),
+                pl.BlockSpec((F, wide_cols), lambda a, p: (0, 0)),
             ],
             out_specs=pl.BlockSpec((1, BLK, WIDE * BLK), lambda a, p: (a, 0, 0)),
             scratch_shapes=[
                 pltpu.VMEM((blocks, blocks, BLK, BLK), jnp.bfloat16),
                 pltpu.VMEM((BLK, WIDE * BLK), jnp.float32),
+                pltpu.VMEM((1, WIDE * BLK), jnp.float32),
             ],
         ),
         compiler_params=pltpu.CompilerParams(dimension_semantics=("arbitrary",)),
-    )(pattern_flat, wide_points, wide_points_t, sq_row)
+    )(pattern, points, wide_points_t)
 
 
 def apply_k(wide_vec, kmat):
@@ -396,23 +396,14 @@
     rim_rows = REACH * BLK
     kernel_scale = 1.0 / (4 * BLK)
     first_low = right_side.astype(jnp.bfloat16)
-    point_rows = points.size // 128
-    packed = jnp.concatenate([points.reshape(point_rows, 128), first_low.reshape(-1, 128)], axis=0)
+    points_t = points.T
+    packed = jnp.concatenate([points_t, first_low], axis=0)
     count = lax.axis_size("pts")
     from_left = lax.ppermute(packed, "pts", [(i, i + 1) for i in range(count - 1)])
     from_right = lax.ppermute(packed, "pts", [(i + 1, i) for i in range(count - 1)])
-    wide_points = jnp.concatenate(
-        [from_left[:point_rows].reshape(points.shape), points, from_right[:point_rows].reshape(points.shape)], axis=0
-    )
-    first_wide = jnp.concatenate(
-        [
-            from_left[point_rows:].reshape(first_low.shape),
-            first_low,
-            from_right[point_rows:].reshape(first_low.shape),
-        ],
-        axis=1,
-    )
-    kmat = build_k(pattern.reshape(-1), wide_points, block_count)
+    wide_points_t = jnp.concatenate([from_left[:F], points_t, from_right[:F]], axis=1)
+    first_wide = jnp.concatenate([from_left[F:], first_low, from_right[F:]], axis=1)
+    kmat = build_k(pattern, points, wide_points_t, block_count)
 
     rhs_count = lax.axis_size("rhs")
     rhs_index = lax.axis_index("rhs")

time: 137 us -> 131 us (0.956)
  local copies, waits for them, and re-layouts: 5.41 us -> 1.97 us
  Pallas kernels: 113 us -> 110 us
    pallas_call x2, Pallas kernels: 64.8 us -> 58.9 us  [apply_sum(): pl.pallas_call(functools.partial(apply_sum_kernel, inner, outer), out_sha...]
    pallas_call x1, Pallas kernels: 33.5 us -> 36.4 us  [build_k(): pl.pallas_call(build_kernel, out_shape=jax.ShapeDtypeStruct((blocks, BLK,...]
    reshape x9 -> x0, local copies, waits for them, and re-layouts: 2.61 us -> none  [the longest x1 1.37 us: per_device(): kmat = build_k(pattern.reshape(-1), wide_points, block_count)]
    concatenate x1 -> x3, other arithmetic: 0.68 us -> 3.29 us  [the longest x1 1.68 us: per_device(): jnp.concatenate([from_left[:F], points_t, from_right[:F]], axis=1)]
    reduce_sum x1 -> x0, other arithmetic: 1.64 us -> none  [build_k(): sq_row = jnp.sum(wide_f * wide_f, axis=0, keepdims=True)]
    concatenate x2 -> x0, local copies, waits for them, and re-layouts: 1.57 us -> none  [the longest x1 1.55 us: per_device(): jnp.concatenate([from_left[:point_rows].reshape(points.shape), points, fr...]
where the time goes in v12:
time: 131 us; the launch traced here: 130 us
  Pallas kernels  110 us (84%)
  other arithmetic  12.1 us (9%)
  starting transfers between devices  4.33 us (3%)
  local copies, waits for them, and re-layouts  1.97 us (2%)
    pallas_call x2, Pallas kernels, apply_sum(): pl.pallas_call(functools.partial(apply_sum_kernel, inner, outer), out_sha...  58.9 us
    pallas_call x1, Pallas kernels, build_k(): pl.pallas_call(build_kernel, out_shape=jax.ShapeDtypeStruct((blocks, BLK,...  36.4 us
    pallas_call x1, Pallas kernels, apply_k(): pl.pallas_call(apply_kernel, out_shape=jax.ShapeDtypeStruct((rows, blocks...  15.1 us
    ppermute x1, starting transfers between devices, per_device(): lax.ppermute(packed, 'pts', [(i, i + 1) for i in range(count - 1)])  3.04 us
    reduce_sum x2, other arithmetic, per_device(): jnp.sum(residual * residual, axis=1)  2.8 us
  transfers between devices with their start and end apart: 2, of which 0 were waited for; matrix products, arithmetic and copies ran while one was open for 1% of the time, Pallas kernels for 0%

profile of v12, /device:TPU:16, one launch (start us, length us, event | category | flops | bytes accessed | tf_op | source)
XLA Modules:
  0.0 129.6 jit_solution(946253576719845271)
XLA Ops:
  0.6 0.9 convert_element_type.9
  1.5 0.9 pad_maximum_fusion.1
  2.5 1.3 collective-permute-start.1
  3.8 3.0 %collective-permute-start = (bf16[48,2048]{1,0:T(8,128)(2,1)S(1)}, bf16[48,2048]{1,0:T(8,128)(2,1)S(1)}, u32[]{:S(2)}, u32[]{:S(2)}) collective-permute-start(bf16[48,2048]{1,0:T(8,128)(2,1)S(1)} %pad_maximum_fusion.1), channel_id=1, source_target_pairs={{0,4},{4,8},{8,12},{12,16},{16,20},{20,24},{24,28},{28,32},{32,36}... | collective-permute-start | bytes 589832 | tf_op jit(solution)/shard_map/ppermute | solution.py:402
  6.8 1.9 %copy.7.pw_ref = bf16[2048,32]{1,0:T(8,128)(2,1)} copy(bf16[2048,32]{0,1:T(8,128)(2,1)} %param.4) | data formatting | bytes 262144 | tf_op args[0]
  8.7 0.0 collective-permute-done.1
  8.8 0.0 collective-permute-done
  8.8 0.7 pad_maximum_fusion.2.v_ref
  9.5 1.7 %pad_maximum_fusion.pwt_ref = bf16[32,6144]{1,0:T(8,128)(2,1)} fusion(bf16[32,2048]{1,0:T(8,128)(2,1)S(1)} %slice.41, bf16[32,2048]{1,0:T(8,128)(2,1)} %bitcast.29, bf16[32,2048]{1,0:T(8,128)(2,1)S(1)} %slice.40), kind=kLoop, calls=%fused_computation | loop fusion | flops 1179648 | bytes 786432 | tf_op jit(solution)/shard_map/concatenate | solution.py:404
  11.2 0.0 copy-start
  11.2 0.0 copy-start.2
  11.2 36.4 %shard_map.67.k_ref = bf16[16,128,4224]{2,1,0:T(8,128)(2,1)} custom-call(s32[16,33]{1,0:T(8,128)} %pat_ref.1, bf16[2048,32]{1,0:T(8,128)(2,1)} %copy.7.pw_ref, bf16[32,6144]{1,0:T(8,128)(2,1)} %pad_maximum_fusion.pwt_ref), custom_call_target="tpu_custom_call" | custom-call | tf_op jit(solution)/shard_map/pallas_call | solution.py:101
  47.6 15.1 %shard_map.68 = f32[16,2048]{1,0:T(8,128)} custom-call(bf16[16,6144]{1,0:T(8,128)(2,1)} %pad_maximum_fusion.2.v_ref, bf16[16,128,4224]{2,1,0:T(8,128)(2,1)} %shard_map.67.k_ref), custom_call_target="tpu_custom_call" | custom-call | tf_op jit(solution)/shard_map/pallas_call | solution.py:125
  62.7 0.0 copy-done
  62.7 0.0 copy-done.2
  62.7 1.0 multiply_reduce_fusion.3
  63.8 0.6 convert_element_type.10.vloc_ref
  64.4 0.6 select_maximum_fusion.1.part_ref
  65.0 36.0 %shard_map.69 = (f32[16,2048]{1,0:T(8,128)}, f32[8,128]{1,0:T(8,128)}) custom-call(bf16[16,2048]{1,0:T(8,128)(2,1)} %convert_element_type.10.vloc_ref, bf16[16,128,4224]{2,1,0:T(8,128)(2,1)} %shard_map.67.k_ref, f32[8,128]{1,0:T(8,128)} %select_maximum_fusion.1.part_ref), custom_call_target="tpu_custom_call" | custom-call | tf_op jit(solution)/shard_map/pallas_call | solution.py:358
  101.0 0.0 copy-start.1
  101.1 0.8 bitcast_divide_fusion.1
  101.8 1.8 %multiply_reduce_fusion.1 = (f32[16]{0:T(128)S(1)}, f32[16]{0:T(128)S(1)}, bf16[16,2048]{1,0:T(8,128)(2,1)}) fusion(f32[16,2048]{1,0:T(8,128)S(1)} %copy-done, f32[16,2048]{1,0:T(8,128)S(1)} %get-tuple-element.17, f32[16]{0:T(128)S(1)} %bitcast_divide_fusion.1, f32[16,2048]{1,0:T(8,128)} %get-tuple-element.8, f32[2048]{0:T(1024)S(1)} %copy-done.2), kind=kLoop, calls=%fused_computation.7 | loop fusion | flops 393184 | bytes 467136 | tf_op jit(solution)/shard_map/reduce_sum | solution.py:436
  103.6 0.6 select_maximum_fusion.part_ref
  104.2 22.9 %shard_map.70 = (f32[16,2048]{1,0:T(8,128)}, f32[8,128]{1,0:T(8,128)}) custom-call(bf16[16,2048]{1,0:T(8,128)(2,1)} %get-tuple-element.20.vloc_ref, bf16[16,128,4224]{2,1,0:T(8,128)(2,1)} %shard_map.67.k_ref, f32[8,128]{1,0:T(8,128)} %select_maximum_fusion.part_ref), custom_call_target="tpu_custom_call" | custom-call | tf_op jit(solution)/shard_map/pallas_call | solution.py:358
  127.0 0.8 fusion.1
  127.8 0.0 copy-done.1
  127.8 1.8 %multiply_subtract_fusion = (f32[16,2048]{1,0:T(8,128)}, f32[16,2048]{1,0:T(8,128)}, f32[16,2048]{1,0:T(8,128)}) fusion(f32[16,2048]{1,0:T(8,128)} %get-tuple-element.10, f32[16,2048]{1,0:T(8,128)S(1)} %copy-done.1, f32[16,2048]{1,0:T(8,128)S(1)} %get-tuple-element.17, f32[16]{0:T(128)S(1)} %get-tuple-element.16, f32[16]{0:T(128)S(1)} %get-tuple-element.15, ...), kind=kLoop, calls=%fused_computation.3 | loop fusion | flops 753664 | bytes 925888 | tf_op jit(solution)/shard_map/sub | solution.py:453
  (4 shorter events, 0.0 us)
Async XLA Ops:
  2.5 6.3 %collective-permute-start.1 = (bf16[48,2048]{1,0:T(8,128)(2,1)S(1)}, bf16[48,2048]{1,0:T(8,128)(2,1)S(1)}, u32[]{:S(2)}, u32[]{:S(2)}) collective-permute-start(bf16[48,2048]{1,0:T(8,128)(2,1)S(1)} %pad_maximum_fusion.1), channel_id=1, source_target_pairs={{4,0},{8,4},{12,8},{16,12},{20,16},{24,20},{28,24},{32,28},{36,32}... | collective-permute-start | bytes 589832 | tf_op jit(solution)/shard_map/ppermute | solution.py:403
  3.8 5.0 %collective-permute-start = (bf16[48,2048]{1,0:T(8,128)(2,1)S(1)}, bf16[48,2048]{1,0:T(8,128)(2,1)S(1)}, u32[]{:S(2)}, u32[]{:S(2)}) collective-permute-start(bf16[48,2048]{1,0:T(8,128)(2,1)S(1)} %pad_maximum_fusion.1), channel_id=1, source_target_pairs={{0,4},{4,8},{8,12},{12,16},{16,20},{20,24},{24,28},{28,32},{32,36}... | collective-permute-start | bytes 589832 | tf_op jit(solution)/shard_map/ppermute | solution.py:402
  11.2 51.5 %copy-start = (f32[16,2048]{1,0:T(8,128)S(1)}, f32[16,2048]{1,0:T(8,128)}, u32[]{:S(2)}) copy-start(f32[16,2048]{1,0:T(8,128)} %param.6) | copy-start | bytes 393220
  11.2 51.5 %copy-start.2 = (f32[2048]{0:T(1024)S(1)}, f32[2048]{0:T(1024)}, u32[]{:S(2)}) copy-start(f32[2048]{0:T(1024)} %param.5) | copy-start | bytes 24580
  101.0 26.8 %copy-start.1 = (f32[16,2048]{1,0:T(8,128)S(1)}, f32[16,2048]{1,0:T(8,128)}, u32[]{:S(2)}) copy-start(f32[16,2048]{1,0:T(8,128)} %get-tuple-element.8) | copy-start | bytes 393220

commit v13 on v12

--- a/solution.py
+++ b/solution.py
@@ -42,7 +42,7 @@
     return (b16 * b2) * (WEXP * radius + 1.0)
 
 
-def build_kernel(pat_ref, pw_ref, pwt_ref, k_ref, mirror, cross_ref, sqr_ref):
+def build_kernel(pat_ref, pw_ref, pwt_ref, v_ref, k_ref, out_ref, mirror, cross_ref, sqr_ref):
     a = pl.program_id(0)
     blocks = pl.num_programs(0)
     start = pl.multiple_of(a * BLK, BLK)
@@ -84,6 +84,10 @@
         return carry
 
     lax.fori_loop(0, WIDE, body, 0)
+    v_cat = v_ref[:, pl.ds(start, WIDE * BLK)]
+    out_ref[...] = lax.dot_general(
+        v_cat, k_ref[0], (((1,), (1,)), ((), ())), preferred_element_type=jnp.float32
+    )
 
 
 def apply_kernel(v_ref, k_ref, out_ref):
@@ -95,20 +99,28 @@
     )
 
 
-def build_k(pattern, points, wide_points_t, blocks):
+def build_k(pattern, points, wide_points_t, first_wide, blocks):
     rows = points.shape[0]
     wide_cols = wide_points_t.shape[1]
+    vec_rows = first_wide.shape[0]
     return pl.pallas_call(
         build_kernel,
-        out_shape=jax.ShapeDtypeStruct((blocks, BLK, WIDE * BLK), jnp.bfloat16),
+        out_shape=(
+            jax.ShapeDtypeStruct((blocks, BLK, WIDE * BLK), jnp.bfloat16),
+            jax.ShapeDtypeStruct((vec_rows, blocks * BLK), jnp.float32),
+        ),
         grid_spec=pltpu.PrefetchScalarGridSpec(
             num_scalar_prefetch=1,
             grid=(blocks,),
             in_specs=[
                 pl.BlockSpec((rows, F), lambda a, p: (0, 0)),
                 pl.BlockSpec((F, wide_cols), lambda a, p: (0, 0)),
+                pl.BlockSpec((vec_rows, wide_cols), lambda a, p: (0, 0)),
             ],
-            out_specs=pl.BlockSpec((1, BLK, WIDE * BLK), lambda a, p: (a, 0, 0)),
+            out_specs=(
+                pl.BlockSpec((1, BLK, WIDE * BLK), lambda a, p: (a, 0, 0)),
+                pl.BlockSpec((vec_rows, BLK), lambda a, p: (0, a)),
+            ),
             scratch_shapes=[
                 pltpu.VMEM((blocks, blocks, BLK, BLK), jnp.bfloat16),
                 pltpu.VMEM((BLK, WIDE * BLK), jnp.float32),
@@ -116,7 +128,7 @@
             ],
         ),
         compiler_params=pltpu.CompilerParams(dimension_semantics=("arbitrary",)),
-    )(pattern, points, wide_points_t)
+    )(pattern, points, wide_points_t, first_wide)
 
 
 def apply_k(wide_vec, kmat):
@@ -403,7 +415,7 @@
     from_right = lax.ppermute(packed, "pts", [(i + 1, i) for i in range(count - 1)])
     wide_points_t = jnp.concatenate([from_left[:F], points_t, from_right[:F]], axis=1)
     first_wide = jnp.concatenate([from_left[F:], first_low, from_right[F:]], axis=1)
-    kmat = build_k(pattern, points, wide_points_t, block_count)
+    kmat, first_image = build_k(pattern, points, wide_points_t, first_wide, block_count)
 
     rhs_count = lax.axis_size("rhs")
     rhs_index = lax.axis_index("rhs")
@@ -424,7 +436,7 @@
 
     solution = jnp.zeros_like(right_side)
     residual = right_side
-    res_image = noise_var[None, :] * residual + kernel_scale * apply_k(first_wide, kmat)
+    res_image = noise_var[None, :] * residual + kernel_scale * first_image
     direction = jnp.zeros_like(right_side)
     dir_image = jnp.zeros_like(right_side)
     dir_twice = jnp.zeros_like(right_side)

time: 131 us -> 131 us (level)
    pallas_call x2, Pallas kernels: 58.9 us -> 57.1 us  [apply_sum(): pl.pallas_call(functools.partial(apply_sum_kernel, inner, outer), out_sha...]
    pallas_call x2 -> x1, Pallas kernels: 51.5 us -> 51.9 us  [build_k(): pl.pallas_call(build_kernel, out_shape=(jax.ShapeDtypeStruct((blocks, BLK...]
  transfers between devices with their start and end apart: 2 -> 2, of which waited for: 0 -> 0; matrix products, arithmetic and copies ran while one was open for 1% -> 2% of each run, Pallas kernels for 0% -> 0%
where the time goes in v13:
time: 131 us; the launch traced here: 128 us
  Pallas kernels  109 us (83%)
  other arithmetic  12.3 us (9%)
  starting transfers between devices  4.33 us (3%)
  local copies, waits for them, and re-layouts  1.97 us (2%)
    pallas_call x2, Pallas kernels, apply_sum(): pl.pallas_call(functools.partial(apply_sum_kernel, inner, outer), out_sha...  57.1 us
    pallas_call x1, Pallas kernels, build_k(): pl.pallas_call(build_kernel, out_shape=(jax.ShapeDtypeStruct((blocks, BLK...  51.9 us
    ppermute x1, starting transfers between devices, per_device(): lax.ppermute(packed, 'pts', [(i, i + 1) for i in range(count - 1)])  3.04 us
    reduce_sum x2, other arithmetic, per_device(): jnp.sum(residual * residual, axis=1)  2.86 us
  transfers between devices with their start and end apart: 2, of which 0 were waited for; matrix products, arithmetic and copies ran while one was open for 2% of the time, Pallas kernels for 0%

profile of v13, /device:TPU:16, one launch (start us, length us, event | category | flops | bytes accessed | tf_op | source)
XLA Modules:
  0.0 128.4 jit_solution(12582946799439214701)
XLA Ops:
  0.6 0.0 copy-start
  0.6 0.0 copy-start.2
  0.7 1.0 convert_element_type.9
  1.6 0.9 pad_maximum_fusion.1
  2.5 1.3 %collective-permute-start.1 = (bf16[48,2048]{1,0:T(8,128)(2,1)S(1)}, bf16[48,2048]{1,0:T(8,128)(2,1)S(1)}, u32[]{:S(2)}, u32[]{:S(2)}) collective-permute-start(bf16[48,2048]{1,0:T(8,128)(2,1)S(1)} %pad_maximum_fusion.1), channel_id=1, source_target_pairs={{4,0},{8,4},{12,8},{16,12},{20,16},{24,20},{28,24},{32,28},{36,32}... | collective-permute-start | bytes 589832 | tf_op jit(solution)/shard_map/ppermute | solution.py:415
  3.8 3.0 %collective-permute-start = (bf16[48,2048]{1,0:T(8,128)(2,1)S(1)}, bf16[48,2048]{1,0:T(8,128)(2,1)S(1)}, u32[]{:S(2)}, u32[]{:S(2)}) collective-permute-start(bf16[48,2048]{1,0:T(8,128)(2,1)S(1)} %pad_maximum_fusion.1), channel_id=1, source_target_pairs={{0,4},{4,8},{8,12},{12,16},{16,20},{20,24},{24,28},{28,32},{32,36}... | collective-permute-start | bytes 589832 | tf_op jit(solution)/shard_map/ppermute | solution.py:414
  6.9 1.9 %copy.7.pw_ref = bf16[2048,32]{1,0:T(8,128)(2,1)} copy(bf16[2048,32]{0,1:T(8,128)(2,1)} %param.4) | data formatting | bytes 262144 | tf_op args[0]
  8.8 0.0 collective-permute-done.1
  8.8 0.0 collective-permute-done
  8.8 0.7 pad_maximum_fusion.2.v_ref
  9.6 1.7 %pad_maximum_fusion.pwt_ref = bf16[32,6144]{1,0:T(8,128)(2,1)} fusion(bf16[32,2048]{1,0:T(8,128)(2,1)S(1)} %slice.39, bf16[32,2048]{1,0:T(8,128)(2,1)} %bitcast.29, bf16[32,2048]{1,0:T(8,128)(2,1)S(1)} %slice.38), kind=kLoop, calls=%fused_computation | loop fusion | flops 1179648 | bytes 786432 | tf_op jit(solution)/shard_map/concatenate | solution.py:416
  11.3 51.9 %shard_map.67 = (bf16[16,128,4224]{2,1,0:T(8,128)(2,1)}, f32[16,2048]{1,0:T(8,128)}) custom-call(s32[16,33]{1,0:T(8,128)} %pat_ref.1, bf16[2048,32]{1,0:T(8,128)(2,1)} %copy.7.pw_ref, bf16[32,6144]{1,0:T(8,128)(2,1)} %pad_maximum_fusion.pwt_ref, bf16[16,6144]{1,0:T(8,128)(2,1)} %pad_maximum_fusion.2.v_ref), custom_call_target="tpu_custom_call" | custom-call | tf_op jit(solution)/shard_map/pallas_call | solution.py:106
  63.2 1.1 multiply_reduce_fusion.3
  64.3 0.6 convert_element_type.10.vloc_ref
  64.9 0.6 select_maximum_fusion.1.part_ref
  65.5 33.9 %shard_map.68 = (f32[16,2048]{1,0:T(8,128)}, f32[8,128]{1,0:T(8,128)}) custom-call(bf16[16,2048]{1,0:T(8,128)(2,1)} %convert_element_type.10.vloc_ref, bf16[16,128,4224]{2,1,0:T(8,128)(2,1)} %get-tuple-element.10.k_ref, f32[8,128]{1,0:T(8,128)} %select_maximum_fusion.1.part_ref), custom_call_target="tpu_custom_call" | custom-call | tf_op jit(solution)/shard_map/pallas_call | solution.py:370
  99.5 0.0 copy-start.1
  99.5 0.8 bitcast_divide_fusion.1
  100.2 0.0 copy-done
  100.2 0.0 copy-done.2
  100.2 1.8 %multiply_reduce_fusion.1 = (f32[16]{0:T(128)S(1)}, f32[16]{0:T(128)S(1)}, bf16[16,2048]{1,0:T(8,128)(2,1)}) fusion(f32[16,2048]{1,0:T(8,128)S(1)} %copy-done, f32[16,2048]{1,0:T(8,128)S(1)} %get-tuple-element.21, f32[16]{0:T(128)S(1)} %bitcast_divide_fusion.1, f32[16,2048]{1,0:T(8,128)} %get-tuple-element.12, f32[2048]{0:T(1024)S(1)} %copy-done.2), kind=kLoop, calls=%fused_computation.7 | loop fusion | flops 393184 | bytes 467136 | tf_op jit(solution)/shard_map/reduce_sum | solution.py:448
  102.0 0.6 select_maximum_fusion.part_ref
  102.6 23.2 %shard_map.69 = (f32[16,2048]{1,0:T(8,128)}, f32[8,128]{1,0:T(8,128)}) custom-call(bf16[16,2048]{1,0:T(8,128)(2,1)} %get-tuple-element.24.vloc_ref, bf16[16,128,4224]{2,1,0:T(8,128)(2,1)} %get-tuple-element.10.k_ref, f32[8,128]{1,0:T(8,128)} %select_maximum_fusion.part_ref), custom_call_target="tpu_custom_call" | custom-call | tf_op jit(solution)/shard_map/pallas_call | solution.py:370
  125.8 0.8 fusion.1
  126.6 0.0 copy-done.1
  126.6 1.8 %multiply_subtract_fusion = (f32[16,2048]{1,0:T(8,128)}, f32[16,2048]{1,0:T(8,128)}, f32[16,2048]{1,0:T(8,128)}) fusion(f32[16,2048]{1,0:T(8,128)} %get-tuple-element.14, f32[16,2048]{1,0:T(8,128)S(1)} %copy-done.1, f32[16,2048]{1,0:T(8,128)S(1)} %get-tuple-element.21, f32[16]{0:T(128)S(1)} %get-tuple-element.20, f32[16]{0:T(128)S(1)} %get-tuple-element.19, ...), kind=kLoop, calls=%fused_computation.3 | loop fusion | flops 753664 | bytes 925888 | tf_op jit(solution)/shard_map/sub | solution.py:465
  (4 shorter events, 0.0 us)
Async XLA Ops:
  0.6 99.6 %copy-start = (f32[16,2048]{1,0:T(8,128)S(1)}, f32[16,2048]{1,0:T(8,128)}, u32[]{:S(2)}) copy-start(f32[16,2048]{1,0:T(8,128)} %param.6) | copy-start | bytes 393220
  0.6 99.6 %copy-start.2 = (f32[2048]{0:T(1024)S(1)}, f32[2048]{0:T(1024)}, u32[]{:S(2)}) copy-start(f32[2048]{0:T(1024)} %param.5) | copy-start | bytes 24580
  2.5 6.3 %collective-permute-start.1 = (bf16[48,2048]{1,0:T(8,128)(2,1)S(1)}, bf16[48,2048]{1,0:T(8,128)(2,1)S(1)}, u32[]{:S(2)}, u32[]{:S(2)}) collective-permute-start(bf16[48,2048]{1,0:T(8,128)(2,1)S(1)} %pad_maximum_fusion.1), channel_id=1, source_target_pairs={{4,0},{8,4},{12,8},{16,12},{20,16},{24,20},{28,24},{32,28},{36,32}... | collective-permute-start | bytes 589832 | tf_op jit(solution)/shard_map/ppermute | solution.py:415
  3.8 5.0 %collective-permute-start = (bf16[48,2048]{1,0:T(8,128)(2,1)S(1)}, bf16[48,2048]{1,0:T(8,128)(2,1)S(1)}, u32[]{:S(2)}, u32[]{:S(2)}) collective-permute-start(bf16[48,2048]{1,0:T(8,128)(2,1)S(1)} %pad_maximum_fusion.1), channel_id=1, source_target_pairs={{0,4},{4,8},{8,12},{12,16},{16,20},{20,24},{24,28},{28,32},{32,36}... | collective-permute-start | bytes 589832 | tf_op jit(solution)/shard_map/ppermute | solution.py:414
  99.5 27.1 %copy-start.1 = (f32[16,2048]{1,0:T(8,128)S(1)}, f32[16,2048]{1,0:T(8,128)}, u32[]{:S(2)}) copy-start(f32[16,2048]{1,0:T(8,128)} %get-tuple-element.12) | copy-start | bytes 393220

commit v14 on v12

--- a/solution.py
+++ b/solution.py
@@ -333,7 +333,7 @@
 
     blocks = v_ref.shape[1] // BLK - 2 * REACH
 
-    @pl.when(a == min(blocks // 2 - 2, blocks - 1))
+    @pl.when(a == min(blocks // 2, blocks - 1))
     def _():
         start_second()
 

time: 131 us -> 137 us (1.046)
  Pallas kernels: 110 us -> 116 us
    pallas_call x2, Pallas kernels: 58.9 us -> 72 us  [apply_sum(): pl.pallas_call(functools.partial(apply_sum_kernel, inner, outer), out_sha...]
    pallas_call x1, Pallas kernels: 36.4 us -> 29.3 us  [build_k(): pl.pallas_call(build_kernel, out_shape=jax.ShapeDtypeStruct((blocks, BLK,...]
where the time goes in v14:
time: 137 us; the launch traced here: 136 us
  Pallas kernels  116 us (85%)
  other arithmetic  12.1 us (9%)
  starting transfers between devices  4.33 us (3%)
  local copies, waits for them, and re-layouts  1.97 us (1%)
    pallas_call x2, Pallas kernels, apply_sum(): pl.pallas_call(functools.partial(apply_sum_kernel, inner, outer), out_sha...  72 us
    pallas_call x1, Pallas kernels, build_k(): pl.pallas_call(build_kernel, out_shape=jax.ShapeDtypeStruct((blocks, BLK,...  29.3 us
    pallas_call x1, Pallas kernels, apply_k(): pl.pallas_call(apply_kernel, out_shape=jax.ShapeDtypeStruct((rows, blocks...  15.1 us
    ppermute x1, starting transfers between devices, per_device(): lax.ppermute(packed, 'pts', [(i, i + 1) for i in range(count - 1)])  3.04 us
    reduce_sum x2, other arithmetic, per_device(): jnp.sum(residual * residual, axis=1)  2.8 us
  transfers between devices with their start and end apart: 2, of which 0 were waited for; matrix products, arithmetic and copies ran while one was open for 1% of the time, Pallas kernels for 0%

profile of v14, /device:TPU:16, one launch (start us, length us, event | category | flops | bytes accessed | tf_op | source)
XLA Modules:
  0.0 135.5 jit_solution(8191774534684175312)
XLA Ops:
  0.6 0.9 convert_element_type.9
  1.5 0.9 pad_maximum_fusion.1
  2.5 1.3 collective-permute-start.1
  3.8 3.0 %collective-permute-start = (bf16[48,2048]{1,0:T(8,128)(2,1)S(1)}, bf16[48,2048]{1,0:T(8,128)(2,1)S(1)}, u32[]{:S(2)}, u32[]{:S(2)}) collective-permute-start(bf16[48,2048]{1,0:T(8,128)(2,1)S(1)} %pad_maximum_fusion.1), channel_id=1, source_target_pairs={{0,4},{4,8},{8,12},{12,16},{16,20},{20,24},{24,28},{28,32},{32,36}... | collective-permute-start | bytes 589832 | tf_op jit(solution)/shard_map/ppermute | solution.py:402
  6.8 1.9 %copy.7.pw_ref = bf16[2048,32]{1,0:T(8,128)(2,1)} copy(bf16[2048,32]{0,1:T(8,128)(2,1)} %param.4) | data formatting | bytes 262144 | tf_op args[0]
  8.7 0.0 collective-permute-done.1
  8.8 0.0 collective-permute-done
  8.8 0.7 pad_maximum_fusion.2.v_ref
  9.5 1.7 %pad_maximum_fusion.pwt_ref = bf16[32,6144]{1,0:T(8,128)(2,1)} fusion(bf16[32,2048]{1,0:T(8,128)(2,1)S(1)} %slice.41, bf16[32,2048]{1,0:T(8,128)(2,1)} %bitcast.29, bf16[32,2048]{1,0:T(8,128)(2,1)S(1)} %slice.40), kind=kLoop, calls=%fused_computation | loop fusion | flops 1179648 | bytes 786432 | tf_op jit(solution)/shard_map/concatenate | solution.py:404
  11.2 0.0 copy-start
  11.2 0.0 copy-start.2
  11.2 29.3 %shard_map.67.k_ref = bf16[16,128,4224]{2,1,0:T(8,128)(2,1)} custom-call(s32[16,33]{1,0:T(8,128)} %pat_ref.1, bf16[2048,32]{1,0:T(8,128)(2,1)} %copy.7.pw_ref, bf16[32,6144]{1,0:T(8,128)(2,1)} %pad_maximum_fusion.pwt_ref), custom_call_target="tpu_custom_call" | custom-call | tf_op jit(solution)/shard_map/pallas_call | solution.py:101
  40.4 15.1 %shard_map.68 = f32[16,2048]{1,0:T(8,128)} custom-call(bf16[16,6144]{1,0:T(8,128)(2,1)} %pad_maximum_fusion.2.v_ref, bf16[16,128,4224]{2,1,0:T(8,128)(2,1)} %shard_map.67.k_ref), custom_call_target="tpu_custom_call" | custom-call | tf_op jit(solution)/shard_map/pallas_call | solution.py:125
  55.5 0.0 copy-done
  55.5 0.0 copy-done.2
  55.5 1.0 multiply_reduce_fusion.3
  56.6 0.6 convert_element_type.10.vloc_ref
  57.2 0.6 select_maximum_fusion.1.part_ref
  57.8 47.2 %shard_map.69 = (f32[16,2048]{1,0:T(8,128)}, f32[8,128]{1,0:T(8,128)}) custom-call(bf16[16,2048]{1,0:T(8,128)(2,1)} %convert_element_type.10.vloc_ref, bf16[16,128,4224]{2,1,0:T(8,128)(2,1)} %shard_map.67.k_ref, f32[8,128]{1,0:T(8,128)} %select_maximum_fusion.1.part_ref), custom_call_target="tpu_custom_call" | custom-call | tf_op jit(solution)/shard_map/pallas_call | solution.py:358
  105.1 0.0 copy-start.1
  105.1 0.8 bitcast_divide_fusion.1
  105.9 1.8 %multiply_reduce_fusion.1 = (f32[16]{0:T(128)S(1)}, f32[16]{0:T(128)S(1)}, bf16[16,2048]{1,0:T(8,128)(2,1)}) fusion(f32[16,2048]{1,0:T(8,128)S(1)} %copy-done, f32[16,2048]{1,0:T(8,128)S(1)} %get-tuple-element.17, f32[16]{0:T(128)S(1)} %bitcast_divide_fusion.1, f32[16,2048]{1,0:T(8,128)} %get-tuple-element.8, f32[2048]{0:T(1024)S(1)} %copy-done.2), kind=kLoop, calls=%fused_computation.7 | loop fusion | flops 393184 | bytes 467136 | tf_op jit(solution)/shard_map/reduce_sum | solution.py:436
  107.6 0.6 select_maximum_fusion.part_ref
  108.2 24.7 %shard_map.70 = (f32[16,2048]{1,0:T(8,128)}, f32[8,128]{1,0:T(8,128)}) custom-call(bf16[16,2048]{1,0:T(8,128)(2,1)} %get-tuple-element.20.vloc_ref, bf16[16,128,4224]{2,1,0:T(8,128)(2,1)} %shard_map.67.k_ref, f32[8,128]{1,0:T(8,128)} %select_maximum_fusion.part_ref), custom_call_target="tpu_custom_call" | custom-call | tf_op jit(solution)/shard_map/pallas_call | solution.py:358
  133.0 0.8 fusion.1
  133.7 0.0 copy-done.1
  133.7 1.8 %multiply_subtract_fusion = (f32[16,2048]{1,0:T(8,128)}, f32[16,2048]{1,0:T(8,128)}, f32[16,2048]{1,0:T(8,128)}) fusion(f32[16,2048]{1,0:T(8,128)} %get-tuple-element.10, f32[16,2048]{1,0:T(8,128)S(1)} %copy-done.1, f32[16,2048]{1,0:T(8,128)S(1)} %get-tuple-element.17, f32[16]{0:T(128)S(1)} %get-tuple-element.16, f32[16]{0:T(128)S(1)} %get-tuple-element.15, ...), kind=kLoop, calls=%fused_computation.3 | loop fusion | flops 753664 | bytes 925888 | tf_op jit(solution)/shard_map/sub | solution.py:453
  (4 shorter events, 0.0 us)
Async XLA Ops:
  2.5 6.3 %collective-permute-start.1 = (bf16[48,2048]{1,0:T(8,128)(2,1)S(1)}, bf16[48,2048]{1,0:T(8,128)(2,1)S(1)}, u32[]{:S(2)}, u32[]{:S(2)}) collective-permute-start(bf16[48,2048]{1,0:T(8,128)(2,1)S(1)} %pad_maximum_fusion.1), channel_id=1, source_target_pairs={{4,0},{8,4},{12,8},{16,12},{20,16},{24,20},{28,24},{32,28},{36,32}... | collective-permute-start | bytes 589832 | tf_op jit(solution)/shard_map/ppermute | solution.py:403
  3.8 5.0 %collective-permute-start = (bf16[48,2048]{1,0:T(8,128)(2,1)S(1)}, bf16[48,2048]{1,0:T(8,128)(2,1)S(1)}, u32[]{:S(2)}, u32[]{:S(2)}) collective-permute-start(bf16[48,2048]{1,0:T(8,128)(2,1)S(1)} %pad_maximum_fusion.1), channel_id=1, source_target_pairs={{0,4},{4,8},{8,12},{12,16},{16,20},{20,24},{24,28},{28,32},{32,36}... | collective-permute-start | bytes 589832 | tf_op jit(solution)/shard_map/ppermute | solution.py:402
  11.2 44.4 %copy-start = (f32[16,2048]{1,0:T(8,128)S(1)}, f32[16,2048]{1,0:T(8,128)}, u32[]{:S(2)}) copy-start(f32[16,2048]{1,0:T(8,128)} %param.6) | copy-start | bytes 393220
  11.2 44.4 %copy-start.2 = (f32[2048]{0:T(1024)S(1)}, f32[2048]{0:T(1024)}, u32[]{:S(2)}) copy-start(f32[2048]{0:T(1024)} %param.5) | copy-start | bytes 24580
  105.1 28.6 %copy-start.1 = (f32[16,2048]{1,0:T(8,128)S(1)}, f32[16,2048]{1,0:T(8,128)}, u32[]{:S(2)}) copy-start(f32[16,2048]{1,0:T(8,128)} %get-tuple-element.8) | copy-start | bytes 393220

commit v15 on v14

--- a/solution.py
+++ b/solution.py
@@ -333,7 +333,7 @@
 
     blocks = v_ref.shape[1] // BLK - 2 * REACH
 
-    @pl.when(a == min(blocks // 2, blocks - 1))
+    @pl.when(a == min(blocks // 4, blocks - 1))
     def _():
         start_second()
 

time: 137 us -> 136 us (level)
  the two profiles are of different devices: /device:TPU:16 before, /device:TPU:23 now
where the time goes in v15:
time: 136 us; the launch traced here: 134 us
  Pallas kernels  111 us (82%)
  other arithmetic  12.1 us (9%)
  starting transfers between devices  7.67 us (6%)
  local copies, waits for them, and re-layouts  1.97 us (1%)
    pallas_call x2, Pallas kernels, apply_sum(): pl.pallas_call(functools.partial(apply_sum_kernel, inner, outer), out_sha...  61.3 us
    pallas_call x1, Pallas kernels, build_k(): pl.pallas_call(build_kernel, out_shape=jax.ShapeDtypeStruct((blocks, BLK,...  34.6 us
    pallas_call x1, Pallas kernels, apply_k(): pl.pallas_call(apply_kernel, out_shape=jax.ShapeDtypeStruct((rows, blocks...  15.1 us
    ppermute x1, starting transfers between devices, per_device(): lax.ppermute(packed, 'pts', [(i, i + 1) for i in range(count - 1)])  5.09 us
    reduce_sum x2, other arithmetic, per_device(): jnp.sum(residual * residual, axis=1)  2.8 us
  transfers between devices with their start and end apart: 2, of which 1 were waited for; matrix products, arithmetic and copies ran while one was open for 1% of the time, Pallas kernels for 0%

profile of v15, /device:TPU:23, one launch (start us, length us, event | category | flops | bytes accessed | tf_op | source)
XLA Modules:
  0.0 134.1 jit_solution(16993285353384634863)
XLA Ops:
  0.6 0.9 convert_element_type.9
  1.5 0.9 pad_maximum_fusion.1
  2.5 2.6 %collective-permute-start.1 = (bf16[48,2048]{1,0:T(8,128)(2,1)S(1)}, bf16[48,2048]{1,0:T(8,128)(2,1)S(1)}, u32[]{:S(2)}, u32[]{:S(2)}) collective-permute-start(bf16[48,2048]{1,0:T(8,128)(2,1)S(1)} %pad_maximum_fusion.1), channel_id=1, source_target_pairs={{4,0},{8,4},{12,8},{16,12},{20,16},{24,20},{28,24},{32,28},{36,32}... | collective-permute-start | bytes 589832 | tf_op jit(solution)/shard_map/ppermute | solution.py:403
  5.1 5.1 %collective-permute-start = (bf16[48,2048]{1,0:T(8,128)(2,1)S(1)}, bf16[48,2048]{1,0:T(8,128)(2,1)S(1)}, u32[]{:S(2)}, u32[]{:S(2)}) collective-permute-start(bf16[48,2048]{1,0:T(8,128)(2,1)S(1)} %pad_maximum_fusion.1), channel_id=1, source_target_pairs={{0,4},{4,8},{8,12},{12,16},{16,20},{20,24},{24,28},{28,32},{32,36}... | collective-permute-start | bytes 589832 | tf_op jit(solution)/shard_map/ppermute | solution.py:402
  10.2 1.9 %copy.7.pw_ref = bf16[2048,32]{1,0:T(8,128)(2,1)} copy(bf16[2048,32]{0,1:T(8,128)(2,1)} %param.4) | data formatting | bytes 262144 | tf_op args[0]
  12.1 0.0 collective-permute-done.1
  12.1 0.7 collective-permute-done
  12.8 0.7 pad_maximum_fusion.2.v_ref
  13.5 1.7 %pad_maximum_fusion.pwt_ref = bf16[32,6144]{1,0:T(8,128)(2,1)} fusion(bf16[32,2048]{1,0:T(8,128)(2,1)S(1)} %slice.41, bf16[32,2048]{1,0:T(8,128)(2,1)} %bitcast.29, bf16[32,2048]{1,0:T(8,128)(2,1)S(1)} %slice.40), kind=kLoop, calls=%fused_computation | loop fusion | flops 1179648 | bytes 786432 | tf_op jit(solution)/shard_map/concatenate | solution.py:404
  15.2 0.0 copy-start
  15.2 0.0 copy-start.2
  15.2 34.6 %shard_map.67.k_ref = bf16[16,128,4224]{2,1,0:T(8,128)(2,1)} custom-call(s32[16,33]{1,0:T(8,128)} %pat_ref.1, bf16[2048,32]{1,0:T(8,128)(2,1)} %copy.7.pw_ref, bf16[32,6144]{1,0:T(8,128)(2,1)} %pad_maximum_fusion.pwt_ref), custom_call_target="tpu_custom_call" | custom-call | tf_op jit(solution)/shard_map/pallas_call | solution.py:101
  49.8 15.1 %shard_map.68 = f32[16,2048]{1,0:T(8,128)} custom-call(bf16[16,6144]{1,0:T(8,128)(2,1)} %pad_maximum_fusion.2.v_ref, bf16[16,128,4224]{2,1,0:T(8,128)(2,1)} %shard_map.67.k_ref), custom_call_target="tpu_custom_call" | custom-call | tf_op jit(solution)/shard_map/pallas_call | solution.py:125
  64.9 0.0 copy-done
  64.9 0.0 copy-done.2
  64.9 1.0 multiply_reduce_fusion.3
  65.9 0.6 convert_element_type.10.vloc_ref
  66.6 0.6 select_maximum_fusion.1.part_ref
  67.2 38.7 %shard_map.69 = (f32[16,2048]{1,0:T(8,128)}, f32[8,128]{1,0:T(8,128)}) custom-call(bf16[16,2048]{1,0:T(8,128)(2,1)} %convert_element_type.10.vloc_ref, bf16[16,128,4224]{2,1,0:T(8,128)(2,1)} %shard_map.67.k_ref, f32[8,128]{1,0:T(8,128)} %select_maximum_fusion.1.part_ref), custom_call_target="tpu_custom_call" | custom-call | tf_op jit(solution)/shard_map/pallas_call | solution.py:358
  105.8 0.0 copy-start.1
  105.9 0.8 bitcast_divide_fusion.1
  106.6 1.8 %multiply_reduce_fusion.1 = (f32[16]{0:T(128)S(1)}, f32[16]{0:T(128)S(1)}, bf16[16,2048]{1,0:T(8,128)(2,1)}) fusion(f32[16,2048]{1,0:T(8,128)S(1)} %copy-done, f32[16,2048]{1,0:T(8,128)S(1)} %get-tuple-element.17, f32[16]{0:T(128)S(1)} %bitcast_divide_fusion.1, f32[16,2048]{1,0:T(8,128)} %get-tuple-element.8, f32[2048]{0:T(1024)S(1)} %copy-done.2), kind=kLoop, calls=%fused_computation.7 | loop fusion | flops 393184 | bytes 467136 | tf_op jit(solution)/shard_map/reduce_sum | solution.py:436
  108.4 0.6 select_maximum_fusion.part_ref
  109.0 22.6 %shard_map.70 = (f32[16,2048]{1,0:T(8,128)}, f32[8,128]{1,0:T(8,128)}) custom-call(bf16[16,2048]{1,0:T(8,128)(2,1)} %get-tuple-element.20.vloc_ref, bf16[16,128,4224]{2,1,0:T(8,128)(2,1)} %shard_map.67.k_ref, f32[8,128]{1,0:T(8,128)} %select_maximum_fusion.part_ref), custom_call_target="tpu_custom_call" | custom-call | tf_op jit(solution)/shard_map/pallas_call | solution.py:358
  131.6 0.8 fusion.1
  132.4 0.0 copy-done.1
  132.4 1.8 %multiply_subtract_fusion = (f32[16,2048]{1,0:T(8,128)}, f32[16,2048]{1,0:T(8,128)}, f32[16,2048]{1,0:T(8,128)}) fusion(f32[16,2048]{1,0:T(8,128)} %get-tuple-element.10, f32[16,2048]{1,0:T(8,128)S(1)} %copy-done.1, f32[16,2048]{1,0:T(8,128)S(1)} %get-tuple-element.17, f32[16]{0:T(128)S(1)} %get-tuple-element.16, f32[16]{0:T(128)S(1)} %get-tuple-element.15, ...), kind=kLoop, calls=%fused_computation.3 | loop fusion | flops 753664 | bytes 925888 | tf_op jit(solution)/shard_map/sub | solution.py:453
  (4 shorter events, 0.0 us)
Async XLA Ops:
  2.5 9.6 %collective-permute-start.1 = (bf16[48,2048]{1,0:T(8,128)(2,1)S(1)}, bf16[48,2048]{1,0:T(8,128)(2,1)S(1)}, u32[]{:S(2)}, u32[]{:S(2)}) collective-permute-start(bf16[48,2048]{1,0:T(8,128)(2,1)S(1)} %pad_maximum_fusion.1), channel_id=1, source_target_pairs={{4,0},{8,4},{12,8},{16,12},{20,16},{24,20},{28,24},{32,28},{36,32}... | collective-permute-start | bytes 589832 | tf_op jit(solution)/shard_map/ppermute | solution.py:403
  5.1 7.7 %collective-permute-start = (bf16[48,2048]{1,0:T(8,128)(2,1)S(1)}, bf16[48,2048]{1,0:T(8,128)(2,1)S(1)}, u32[]{:S(2)}, u32[]{:S(2)}) collective-permute-start(bf16[48,2048]{1,0:T(8,128)(2,1)S(1)} %pad_maximum_fusion.1), channel_id=1, source_target_pairs={{0,4},{4,8},{8,12},{12,16},{16,20},{20,24},{24,28},{28,32},{32,36}... | collective-permute-start | bytes 589832 | tf_op jit(solution)/shard_map/ppermute | solution.py:402
  15.2 49.7 %copy-start = (f32[16,2048]{1,0:T(8,128)S(1)}, f32[16,2048]{1,0:T(8,128)}, u32[]{:S(2)}) copy-start(f32[16,2048]{1,0:T(8,128)} %param.6) | copy-start | bytes 393220
  15.2 49.7 %copy-start.2 = (f32[2048]{0:T(1024)S(1)}, f32[2048]{0:T(1024)}, u32[]{:S(2)}) copy-start(f32[2048]{0:T(1024)} %param.5) | copy-start | bytes 24580
  105.8 26.5 %copy-start.1 = (f32[16,2048]{1,0:T(8,128)S(1)}, f32[16,2048]{1,0:T(8,128)}, u32[]{:S(2)}) copy-start(f32[16,2048]{1,0:T(8,128)} %get-tuple-element.8) | copy-start | bytes 393220

commit v16 on v12

--- a/solution.py
+++ b/solution.py
@@ -160,7 +160,7 @@
     def first(slot, other):
         return pltpu.make_async_remote_copy(
             src_ref=part_ref,
-            dst_ref=stage1.at[slot],
+            dst_ref=stage1.at[pl.ds(slot, 1)],
             send_sem=send1.at[other],
             recv_sem=recv1.at[slot],
             device_id=(zc * inner + other, row),
@@ -177,7 +177,7 @@
             device_id_type=MESH,
         )
 
-    own1 = pltpu.make_async_copy(part_ref, stage1.at[rc], local_sem.at[0])
+    own1 = pltpu.make_async_copy(part_ref, stage1.at[pl.ds(rc, 1)], local_sem.at[0])
     own2 = pltpu.make_async_copy(stage1, stage2.at[zc], local_sem.at[1])
 
     def start_first():
@@ -215,7 +215,7 @@
 
         lax.fori_loop(1, outer, finish_second, 0)
         own2.wait()
-        return jnp.sum(jnp.sum(stage2[...], axis=0), axis=0)
+        return jnp.sum(jnp.sum(stage2[...], axis=0), axis=0, keepdims=True)
 
     return greet, start_first, start_second, finish
 
@@ -376,8 +376,8 @@
             pltpu.SemaphoreType.DMA((2,)),
             pltpu.SemaphoreType.DMA((2,)),
             pltpu.SemaphoreType.DMA((1,)),
-            pltpu.VMEM((inner,) + tile.shape, jnp.float32),
-            pltpu.VMEM((outer, inner) + tile.shape, jnp.float32),
+            pltpu.VMEM((inner, tile.shape[1]), jnp.float32),
+            pltpu.VMEM((outer, inner, tile.shape[1]), jnp.float32),
             pltpu.SemaphoreType.DMA((2,)),
             pltpu.SemaphoreType.DMA((inner,)),
             pltpu.SemaphoreType.DMA((inner,)),
@@ -415,12 +415,13 @@
         return noise_var[None, :] * vector + kernel_scale * image_part
 
     def apply_and_total(vector, parts):
-        tile = jnp.zeros((8, 128), jnp.float32)
-        tile = lax.dynamic_update_slice(tile, parts, (0, 0))
+        flat = parts.reshape(1, -1)
+        tile = jnp.zeros((1, 128), jnp.float32)
+        tile = lax.dynamic_update_slice(tile, flat, (0, 0))
         vec_low = vector.astype(jnp.bfloat16)
         image_part, summed = apply_sum(vec_low, kmat, tile)
         image = noise_var[None, :] * vector + kernel_scale * image_part
-        return image, summed[: parts.shape[0], : parts.shape[1]]
+        return image, summed[0, : flat.shape[1]].reshape(parts.shape)
 
     solution = jnp.zeros_like(right_side)
     residual = right_side

time: 131 us -> 130 us (level)
  the two profiles are of different devices: /device:TPU:16 before, /device:TPU:1 now
where the time goes in v16:
time: 130 us; the launch traced here: 129 us
  Pallas kernels  106 us (82%)
  other arithmetic  11.1 us (9%)
  starting transfers between devices  7.07 us (5%)
  local copies, waits for them, and re-layouts  3.17 us (2%)
    pallas_call x2, Pallas kernels, apply_sum(): pl.pallas_call(functools.partial(apply_sum_kernel, inner, outer), out_sha...  60.2 us
    pallas_call x1, Pallas kernels, build_k(): pl.pallas_call(build_kernel, out_shape=jax.ShapeDtypeStruct((blocks, BLK,...  30.6 us
    pallas_call x1, Pallas kernels, apply_k(): pl.pallas_call(apply_kernel, out_shape=jax.ShapeDtypeStruct((rows, blocks...  15.1 us
    ppermute x1, starting transfers between devices, per_device(): lax.ppermute(packed, 'pts', [(i + 1, i) for i in range(count - 1)])  5.15 us
    reduce_sum x2, other arithmetic, per_device(): jnp.sum(residual * residual, axis=1)  2.8 us
  transfers between devices with their start and end apart: 2, of which 1 were waited for; matrix products, arithmetic and copies ran while one was open for 1% of the time, Pallas kernels for 0%

profile of v16, /device:TPU:1, one launch (start us, length us, event | category | flops | bytes accessed | tf_op | source)
XLA Modules:
  0.0 128.7 jit_solution(3238333235103668238)
XLA Ops:
  0.6 0.9 convert_element_type.9
  1.5 0.9 pad_maximum_fusion.1
  2.5 5.1 %collective-permute-start.1 = (bf16[48,2048]{1,0:T(8,128)(2,1)S(1)}, bf16[48,2048]{1,0:T(8,128)(2,1)S(1)}, u32[]{:S(2)}, u32[]{:S(2)}) collective-permute-start(bf16[48,2048]{1,0:T(8,128)(2,1)S(1)} %pad_maximum_fusion.1), channel_id=1, source_target_pairs={{4,0},{8,4},{12,8},{16,12},{20,16},{24,20},{28,24},{32,28},{36,32}... | collective-permute-start | bytes 589832 | tf_op jit(solution)/shard_map/ppermute | solution.py:403
  7.6 1.9 %collective-permute-start = (bf16[48,2048]{1,0:T(8,128)(2,1)S(1)}, bf16[48,2048]{1,0:T(8,128)(2,1)S(1)}, u32[]{:S(2)}, u32[]{:S(2)}) collective-permute-start(bf16[48,2048]{1,0:T(8,128)(2,1)S(1)} %pad_maximum_fusion.1), channel_id=1, source_target_pairs={{0,4},{4,8},{8,12},{12,16},{16,20},{20,24},{24,28},{28,32},{32,36}... | collective-permute-start | bytes 589832 | tf_op jit(solution)/shard_map/ppermute | solution.py:402
  9.5 1.9 %copy.7.pw_ref = bf16[2048,32]{1,0:T(8,128)(2,1)} copy(bf16[2048,32]{0,1:T(8,128)(2,1)} %param.4) | data formatting | bytes 262144 | tf_op args[0]
  11.5 0.0 collective-permute-done.1
  11.5 0.7 collective-permute-done
  12.1 0.7 pad_maximum_fusion.2.v_ref
  12.9 1.7 %pad_maximum_fusion.pwt_ref = bf16[32,6144]{1,0:T(8,128)(2,1)} fusion(bf16[32,2048]{1,0:T(8,128)(2,1)S(1)} %slice.45, bf16[32,2048]{1,0:T(8,128)(2,1)} %bitcast.29, bf16[32,2048]{1,0:T(8,128)(2,1)S(1)} %slice.44), kind=kLoop, calls=%fused_computation | loop fusion | flops 1179648 | bytes 786432 | tf_op jit(solution)/shard_map/concatenate | solution.py:404
  14.6 0.0 copy-start
  14.6 0.0 copy-start.2
  14.6 30.6 %shard_map.67.k_ref = bf16[16,128,4224]{2,1,0:T(8,128)(2,1)} custom-call(s32[16,33]{1,0:T(8,128)} %pat_ref.1, bf16[2048,32]{1,0:T(8,128)(2,1)} %copy.7.pw_ref, bf16[32,6144]{1,0:T(8,128)(2,1)} %pad_maximum_fusion.pwt_ref), custom_call_target="tpu_custom_call" | custom-call | tf_op jit(solution)/shard_map/pallas_call | solution.py:101
  45.2 15.1 %shard_map.68 = f32[16,2048]{1,0:T(8,128)} custom-call(bf16[16,6144]{1,0:T(8,128)(2,1)} %pad_maximum_fusion.2.v_ref, bf16[16,128,4224]{2,1,0:T(8,128)(2,1)} %shard_map.67.k_ref), custom_call_target="tpu_custom_call" | custom-call | tf_op jit(solution)/shard_map/pallas_call | solution.py:125
  60.3 0.0 copy-done
  60.3 0.0 copy-done.2
  60.3 1.0 multiply_reduce_fusion.3
  61.3 0.1 reshape.86
  61.4 0.6 convert_element_type.10.vloc_ref
  62.1 0.5 dynamic_update_slice.6.part_ref
  62.6 36.7 %shard_map.69 = (f32[16,2048]{1,0:T(8,128)}, f32[1,128]{1,0:T(1,128)}) custom-call(bf16[16,2048]{1,0:T(8,128)(2,1)} %convert_element_type.10.vloc_ref, bf16[16,128,4224]{2,1,0:T(8,128)(2,1)} %shard_map.67.k_ref, f32[1,128]{1,0:T(1,128)} %dynamic_update_slice.6.part_ref), custom_call_target="tpu_custom_call" | custom-call | tf_op jit(solution)/shard_map/pallas_call | solution.py:358
  99.3 0.0 copy-start.3
  99.3 0.0 copy-start.1
  99.3 0.9 bitcast_divide_fusion.1
  100.1 1.8 %multiply_reduce_fusion.1 = (f32[16]{0:T(128)S(1)}, f32[16]{0:T(128)S(1)}, bf16[16,2048]{1,0:T(8,128)(2,1)}) fusion(f32[16,2048]{1,0:T(8,128)S(1)} %copy-done, f32[16,2048]{1,0:T(8,128)S(1)} %get-tuple-element.17, f32[16]{0:T(128)S(1)} %bitcast_divide_fusion.1, f32[16,2048]{1,0:T(8,128)} %get-tuple-element.8, f32[2048]{0:T(1024)S(1)} %copy-done.2), kind=kLoop, calls=%fused_computation.7 | loop fusion | flops 393184 | bytes 467136 | tf_op jit(solution)/shard_map/reduce_sum | solution.py:437
  101.9 0.1 reshape.87
  102.0 0.5 dynamic_update_slice.7.part_ref
  102.5 23.5 %shard_map.70 = (f32[16,2048]{1,0:T(8,128)}, f32[1,128]{1,0:T(1,128)}) custom-call(bf16[16,2048]{1,0:T(8,128)(2,1)} %get-tuple-element.20.vloc_ref, bf16[16,128,4224]{2,1,0:T(8,128)(2,1)} %shard_map.67.k_ref, f32[1,128]{1,0:T(1,128)} %dynamic_update_slice.7.part_ref), custom_call_target="tpu_custom_call" | custom-call | tf_op jit(solution)/shard_map/pallas_call | solution.py:358
  126.1 0.0 copy-done.3
  126.1 0.8 fusion
  126.9 0.0 copy-done.1
  126.9 1.8 %multiply_subtract_fusion = (f32[16,2048]{1,0:T(8,128)}, f32[16,2048]{1,0:T(8,128)}, f32[16,2048]{1,0:T(8,128)}) fusion(f32[16,2048]{1,0:T(8,128)} %get-tuple-element.10, f32[16,2048]{1,0:T(8,128)S(1)} %copy-done.1, f32[16,2048]{1,0:T(8,128)S(1)} %get-tuple-element.17, f32[16]{0:T(128)S(1)} %get-tuple-element.16, f32[16]{0:T(128)S(1)} %get-tuple-element.15, ...), kind=kLoop, calls=%fused_computation.3 | loop fusion | flops 753664 | bytes 925888 | tf_op jit(solution)/shard_map/sub | solution.py:454
  (6 shorter events, 0.1 us)
Async XLA Ops:
  2.5 9.0 %collective-permute-start.1 = (bf16[48,2048]{1,0:T(8,128)(2,1)S(1)}, bf16[48,2048]{1,0:T(8,128)(2,1)S(1)}, u32[]{:S(2)}, u32[]{:S(2)}) collective-permute-start(bf16[48,2048]{1,0:T(8,128)(2,1)S(1)} %pad_maximum_fusion.1), channel_id=1, source_target_pairs={{4,0},{8,4},{12,8},{16,12},{20,16},{24,20},{28,24},{32,28},{36,32}... | collective-permute-start | bytes 589832 | tf_op jit(solution)/shard_map/ppermute | solution.py:403
  7.6 4.5 %collective-permute-start = (bf16[48,2048]{1,0:T(8,128)(2,1)S(1)}, bf16[48,2048]{1,0:T(8,128)(2,1)S(1)}, u32[]{:S(2)}, u32[]{:S(2)}) collective-permute-start(bf16[48,2048]{1,0:T(8,128)(2,1)S(1)} %pad_maximum_fusion.1), channel_id=1, source_target_pairs={{0,4},{4,8},{8,12},{12,16},{16,20},{20,24},{24,28},{28,32},{32,36}... | collective-permute-start | bytes 589832 | tf_op jit(solution)/shard_map/ppermute | solution.py:402
  14.6 45.7 %copy-start = (f32[16,2048]{1,0:T(8,128)S(1)}, f32[16,2048]{1,0:T(8,128)}, u32[]{:S(2)}) copy-start(f32[16,2048]{1,0:T(8,128)} %param.6) | copy-start | bytes 393220
  14.6 45.7 %copy-start.2 = (f32[2048]{0:T(1024)S(1)}, f32[2048]{0:T(1024)}, u32[]{:S(2)}) copy-start(f32[2048]{0:T(1024)} %param.5) | copy-start | bytes 24580
  99.3 26.8 %copy-start.3 = (f32[1,128]{1,0:T(1,128)S(1)}, f32[1,128]{1,0:T(1,128)}, u32[]{:S(2)}) copy-start(f32[1,128]{1,0:T(1,128)} %get-tuple-element.7) | copy-start | bytes 1540
  99.3 27.6 %copy-start.1 = (f32[16,2048]{1,0:T(8,128)S(1)}, f32[16,2048]{1,0:T(8,128)}, u32[]{:S(2)}) copy-start(f32[16,2048]{1,0:T(8,128)} %get-tuple-element.8) | copy-start | bytes 393220

commit v17 on v12

--- a/solution.py
+++ b/solution.py
@@ -70,12 +70,12 @@
         @pl.when(jnp.logical_and(live, jnp.logical_not(lower)))
         def _():
             sq_right = sqr_ref[:, dst]
-            value = profile_tile(sq_left, sq_right, cross_ref[:, dst])
-            k_ref[0, :, dst] = value.astype(jnp.bfloat16)
+            value = profile_tile(sq_left, sq_right, cross_ref[:, dst]).astype(jnp.bfloat16)
+            k_ref[0, :, dst] = value
 
             @pl.when(upper)
             def _():
-                mirror[other, a] = value.T.astype(jnp.bfloat16)
+                mirror[other, a] = value.T
 
         @pl.when(jnp.logical_not(live))
         def _():

time: 131 us -> 133 us (1.015)
  Pallas kernels: 110 us -> 112 us
    pallas_call x2, Pallas kernels: 58.9 us -> 62.1 us  [apply_sum(): pl.pallas_call(functools.partial(apply_sum_kernel, inner, outer), out_sha...]
    pallas_call x1, Pallas kernels: 36.4 us -> 34.4 us  [build_k(): pl.pallas_call(build_kernel, out_shape=jax.ShapeDtypeStruct((blocks, BLK,...]
where the time goes in v17:
time: 133 us; the launch traced here: 131 us
  Pallas kernels  112 us (84%)
  other arithmetic  12.1 us (9%)
  starting transfers between devices  4.33 us (3%)
  local copies, waits for them, and re-layouts  1.97 us (1%)
    pallas_call x2, Pallas kernels, apply_sum(): pl.pallas_call(functools.partial(apply_sum_kernel, inner, outer), out_sha...  62.1 us
    pallas_call x1, Pallas kernels, build_k(): pl.pallas_call(build_kernel, out_shape=jax.ShapeDtypeStruct((blocks, BLK,...  34.4 us
    pallas_call x1, Pallas kernels, apply_k(): pl.pallas_call(apply_kernel, out_shape=jax.ShapeDtypeStruct((rows, blocks...  15.1 us
    ppermute x1, starting transfers between devices, per_device(): lax.ppermute(packed, 'pts', [(i, i + 1) for i in range(count - 1)])  3.04 us
    reduce_sum x2, other arithmetic, per_device(): jnp.sum(residual * residual, axis=1)  2.8 us
  transfers between devices with their start and end apart: 2, of which 0 were waited for; matrix products, arithmetic and copies ran while one was open for 1% of the time, Pallas kernels for 0%

profile of v17, /device:TPU:16, one launch (start us, length us, event | category | flops | bytes accessed | tf_op | source)
XLA Modules:
  0.0 130.7 jit_solution(9560519457438598861)
XLA Ops:
  0.6 0.9 convert_element_type.9
  1.5 0.9 pad_maximum_fusion.1
  2.5 1.3 collective-permute-start.1
  3.8 3.0 %collective-permute-start = (bf16[48,2048]{1,0:T(8,128)(2,1)S(1)}, bf16[48,2048]{1,0:T(8,128)(2,1)S(1)}, u32[]{:S(2)}, u32[]{:S(2)}) collective-permute-start(bf16[48,2048]{1,0:T(8,128)(2,1)S(1)} %pad_maximum_fusion.1), channel_id=1, source_target_pairs={{0,4},{4,8},{8,12},{12,16},{16,20},{20,24},{24,28},{28,32},{32,36}... | collective-permute-start | bytes 589832 | tf_op jit(solution)/shard_map/ppermute | solution.py:402
  6.8 1.9 %copy.7.pw_ref = bf16[2048,32]{1,0:T(8,128)(2,1)} copy(bf16[2048,32]{0,1:T(8,128)(2,1)} %param.4) | data formatting | bytes 262144 | tf_op args[0]
  8.7 0.0 collective-permute-done.1
  8.8 0.0 collective-permute-done
  8.8 0.7 pad_maximum_fusion.2.v_ref
  9.5 1.7 %pad_maximum_fusion.pwt_ref = bf16[32,6144]{1,0:T(8,128)(2,1)} fusion(bf16[32,2048]{1,0:T(8,128)(2,1)S(1)} %slice.41, bf16[32,2048]{1,0:T(8,128)(2,1)} %bitcast.29, bf16[32,2048]{1,0:T(8,128)(2,1)S(1)} %slice.40), kind=kLoop, calls=%fused_computation | loop fusion | flops 1179648 | bytes 786432 | tf_op jit(solution)/shard_map/concatenate | solution.py:404
  11.2 0.0 copy-start
  11.2 0.0 copy-start.2
  11.2 34.4 %shard_map.67.k_ref = bf16[16,128,4224]{2,1,0:T(8,128)(2,1)} custom-call(s32[16,33]{1,0:T(8,128)} %pat_ref.1, bf16[2048,32]{1,0:T(8,128)(2,1)} %copy.7.pw_ref, bf16[32,6144]{1,0:T(8,128)(2,1)} %pad_maximum_fusion.pwt_ref), custom_call_target="tpu_custom_call" | custom-call | tf_op jit(solution)/shard_map/pallas_call | solution.py:101
  45.5 15.1 %shard_map.68 = f32[16,2048]{1,0:T(8,128)} custom-call(bf16[16,6144]{1,0:T(8,128)(2,1)} %pad_maximum_fusion.2.v_ref, bf16[16,128,4224]{2,1,0:T(8,128)(2,1)} %shard_map.67.k_ref), custom_call_target="tpu_custom_call" | custom-call | tf_op jit(solution)/shard_map/pallas_call | solution.py:125
  60.6 0.0 copy-done
  60.6 0.0 copy-done.2
  60.6 1.0 multiply_reduce_fusion.3
  61.7 0.6 convert_element_type.10.vloc_ref
  62.3 0.6 select_maximum_fusion.1.part_ref
  62.9 38.9 %shard_map.69 = (f32[16,2048]{1,0:T(8,128)}, f32[8,128]{1,0:T(8,128)}) custom-call(bf16[16,2048]{1,0:T(8,128)(2,1)} %convert_element_type.10.vloc_ref, bf16[16,128,4224]{2,1,0:T(8,128)(2,1)} %shard_map.67.k_ref, f32[8,128]{1,0:T(8,128)} %select_maximum_fusion.1.part_ref), custom_call_target="tpu_custom_call" | custom-call | tf_op jit(solution)/shard_map/pallas_call | solution.py:358
  101.9 0.0 copy-start.1
  101.9 0.8 bitcast_divide_fusion.1
  102.6 1.8 %multiply_reduce_fusion.1 = (f32[16]{0:T(128)S(1)}, f32[16]{0:T(128)S(1)}, bf16[16,2048]{1,0:T(8,128)(2,1)}) fusion(f32[16,2048]{1,0:T(8,128)S(1)} %copy-done, f32[16,2048]{1,0:T(8,128)S(1)} %get-tuple-element.17, f32[16]{0:T(128)S(1)} %bitcast_divide_fusion.1, f32[16,2048]{1,0:T(8,128)} %get-tuple-element.8, f32[2048]{0:T(1024)S(1)} %copy-done.2), kind=kLoop, calls=%fused_computation.7 | loop fusion | flops 393184 | bytes 467136 | tf_op jit(solution)/shard_map/reduce_sum | solution.py:436
  104.4 0.6 select_maximum_fusion.part_ref
  105.0 23.1 %shard_map.70 = (f32[16,2048]{1,0:T(8,128)}, f32[8,128]{1,0:T(8,128)}) custom-call(bf16[16,2048]{1,0:T(8,128)(2,1)} %get-tuple-element.20.vloc_ref, bf16[16,128,4224]{2,1,0:T(8,128)(2,1)} %shard_map.67.k_ref, f32[8,128]{1,0:T(8,128)} %select_maximum_fusion.part_ref), custom_call_target="tpu_custom_call" | custom-call | tf_op jit(solution)/shard_map/pallas_call | solution.py:358
  128.1 0.8 fusion.1
  128.9 0.0 copy-done.1
  128.9 1.8 %multiply_subtract_fusion = (f32[16,2048]{1,0:T(8,128)}, f32[16,2048]{1,0:T(8,128)}, f32[16,2048]{1,0:T(8,128)}) fusion(f32[16,2048]{1,0:T(8,128)} %get-tuple-element.10, f32[16,2048]{1,0:T(8,128)S(1)} %copy-done.1, f32[16,2048]{1,0:T(8,128)S(1)} %get-tuple-element.17, f32[16]{0:T(128)S(1)} %get-tuple-element.16, f32[16]{0:T(128)S(1)} %get-tuple-element.15, ...), kind=kLoop, calls=%fused_computation.3 | loop fusion | flops 753664 | bytes 925888 | tf_op jit(solution)/shard_map/sub | solution.py:453
  (4 shorter events, 0.0 us)
Async XLA Ops:
  2.5 6.3 %collective-permute-start.1 = (bf16[48,2048]{1,0:T(8,128)(2,1)S(1)}, bf16[48,2048]{1,0:T(8,128)(2,1)S(1)}, u32[]{:S(2)}, u32[]{:S(2)}) collective-permute-start(bf16[48,2048]{1,0:T(8,128)(2,1)S(1)} %pad_maximum_fusion.1), channel_id=1, source_target_pairs={{4,0},{8,4},{12,8},{16,12},{20,16},{24,20},{28,24},{32,28},{36,32}... | collective-permute-start | bytes 589832 | tf_op jit(solution)/shard_map/ppermute | solution.py:403
  3.8 5.0 %collective-permute-start = (bf16[48,2048]{1,0:T(8,128)(2,1)S(1)}, bf16[48,2048]{1,0:T(8,128)(2,1)S(1)}, u32[]{:S(2)}, u32[]{:S(2)}) collective-permute-start(bf16[48,2048]{1,0:T(8,128)(2,1)S(1)} %pad_maximum_fusion.1), channel_id=1, source_target_pairs={{0,4},{4,8},{8,12},{12,16},{16,20},{20,24},{24,28},{28,32},{32,36}... | collective-permute-start | bytes 589832 | tf_op jit(solution)/shard_map/ppermute | solution.py:402
  11.2 49.5 %copy-start = (f32[16,2048]{1,0:T(8,128)S(1)}, f32[16,2048]{1,0:T(8,128)}, u32[]{:S(2)}) copy-start(f32[16,2048]{1,0:T(8,128)} %param.6) | copy-start | bytes 393220
  11.2 49.5 %copy-start.2 = (f32[2048]{0:T(1024)S(1)}, f32[2048]{0:T(1024)}, u32[]{:S(2)}) copy-start(f32[2048]{0:T(1024)} %param.5) | copy-start | bytes 24580
  101.9 27.0 %copy-start.1 = (f32[16,2048]{1,0:T(8,128)S(1)}, f32[16,2048]{1,0:T(8,128)}, u32[]{:S(2)}) copy-start(f32[16,2048]{1,0:T(8,128)} %get-tuple-element.8) | copy-start | bytes 393220

commit v18 on v12

--- a/solution.py
+++ b/solution.py
@@ -154,8 +154,8 @@
             pl.semaphore_signal(barrier, inc=1, device_id=(peer, row), device_id_type=MESH)
             return carry
 
-        lax.fori_loop(1, inner, greet_inner, 0)
-        lax.fori_loop(1, outer, greet_outer, 0)
+        [greet_inner(k, 0) for k in range(1, inner)]
+        [greet_outer(k, 0) for k in range(1, outer)]
 
     def first(slot, other):
         return pltpu.make_async_remote_copy(
@@ -187,7 +187,7 @@
             first(rc, lax.rem(rc + k, inner)).start()
             return carry
 
-        lax.fori_loop(1, inner, send_first, 0)
+        [send_first(k, 0) for k in range(1, inner)]
 
     def start_second():
         def finish_first(k, carry):
@@ -196,7 +196,7 @@
             first(other, other).wait_recv()
             return carry
 
-        lax.fori_loop(1, inner, finish_first, 0)
+        [finish_first(k, 0) for k in range(1, inner)]
         own1.wait()
         own2.start()
 
@@ -204,7 +204,7 @@
             second(zc, lax.rem(zc + k, outer)).start()
             return carry
 
-        lax.fori_loop(1, outer, send_second, 0)
+        [send_second(k, 0) for k in range(1, outer)]
 
     def finish():
         def finish_second(k, carry):
@@ -213,7 +213,7 @@
             second(other, other).wait_recv()
             return carry
 
-        lax.fori_loop(1, outer, finish_second, 0)
+        [finish_second(k, 0) for k in range(1, outer)]
         own2.wait()
         return jnp.sum(jnp.sum(stage2[...], axis=0), axis=0)
 

time: 131 us -> 133 us (1.015)
  Pallas kernels: 110 us -> 112 us
    pallas_call x1, Pallas kernels: 36.4 us -> 39.5 us  [build_k(): pl.pallas_call(build_kernel, out_shape=jax.ShapeDtypeStruct((blocks, BLK,...]
where the time goes in v18:
time: 133 us; the launch traced here: 131 us
  Pallas kernels  112 us (84%)
  other arithmetic  12.1 us (9%)
  starting transfers between devices  4.33 us (3%)
  local copies, waits for them, and re-layouts  1.97 us (1%)
    pallas_call x2, Pallas kernels, apply_sum(): pl.pallas_call(functools.partial(apply_sum_kernel, inner, outer), out_sha...  57.6 us
    pallas_call x1, Pallas kernels, build_k(): pl.pallas_call(build_kernel, out_shape=jax.ShapeDtypeStruct((blocks, BLK,...  39.5 us
    pallas_call x1, Pallas kernels, apply_k(): pl.pallas_call(apply_kernel, out_shape=jax.ShapeDtypeStruct((rows, blocks...  15.1 us
    ppermute x1, starting transfers between devices, per_device(): lax.ppermute(packed, 'pts', [(i, i + 1) for i in range(count - 1)])  3.04 us
    reduce_sum x2, other arithmetic, per_device(): jnp.sum(residual * residual, axis=1)  2.8 us
  transfers between devices with their start and end apart: 2, of which 0 were waited for; matrix products, arithmetic and copies ran while one was open for 1% of the time, Pallas kernels for 0%

profile of v18, /device:TPU:16, one launch (start us, length us, event | category | flops | bytes accessed | tf_op | source)
XLA Modules:
  0.0 131.4 jit_solution(5402853076562089279)
XLA Ops:
  0.6 0.9 convert_element_type.9
  1.5 0.9 pad_maximum_fusion.1
  2.5 1.3 collective-permute-start.1
  3.8 3.0 %collective-permute-start = (bf16[48,2048]{1,0:T(8,128)(2,1)S(1)}, bf16[48,2048]{1,0:T(8,128)(2,1)S(1)}, u32[]{:S(2)}, u32[]{:S(2)}) collective-permute-start(bf16[48,2048]{1,0:T(8,128)(2,1)S(1)} %pad_maximum_fusion.1), channel_id=1, source_target_pairs={{0,4},{4,8},{8,12},{12,16},{16,20},{20,24},{24,28},{28,32},{32,36}... | collective-permute-start | bytes 589832 | tf_op jit(solution)/shard_map/ppermute | solution.py:402
  6.8 1.9 %copy.7.pw_ref = bf16[2048,32]{1,0:T(8,128)(2,1)} copy(bf16[2048,32]{0,1:T(8,128)(2,1)} %param.4) | data formatting | bytes 262144 | tf_op args[0]
  8.7 0.0 collective-permute-done.1
  8.8 0.0 collective-permute-done
  8.8 0.7 pad_maximum_fusion.2.v_ref
  9.5 1.7 %pad_maximum_fusion.pwt_ref = bf16[32,6144]{1,0:T(8,128)(2,1)} fusion(bf16[32,2048]{1,0:T(8,128)(2,1)S(1)} %slice.41, bf16[32,2048]{1,0:T(8,128)(2,1)} %bitcast.29, bf16[32,2048]{1,0:T(8,128)(2,1)S(1)} %slice.40), kind=kLoop, calls=%fused_computation | loop fusion | flops 1179648 | bytes 786432 | tf_op jit(solution)/shard_map/concatenate | solution.py:404
  11.2 0.0 copy-start
  11.2 0.0 copy-start.2
  11.2 39.5 %shard_map.67.k_ref = bf16[16,128,4224]{2,1,0:T(8,128)(2,1)} custom-call(s32[16,33]{1,0:T(8,128)} %pat_ref.1, bf16[2048,32]{1,0:T(8,128)(2,1)} %copy.7.pw_ref, bf16[32,6144]{1,0:T(8,128)(2,1)} %pad_maximum_fusion.pwt_ref), custom_call_target="tpu_custom_call" | custom-call | tf_op jit(solution)/shard_map/pallas_call | solution.py:101
  50.7 15.1 %shard_map.68 = f32[16,2048]{1,0:T(8,128)} custom-call(bf16[16,6144]{1,0:T(8,128)(2,1)} %pad_maximum_fusion.2.v_ref, bf16[16,128,4224]{2,1,0:T(8,128)(2,1)} %shard_map.67.k_ref), custom_call_target="tpu_custom_call" | custom-call | tf_op jit(solution)/shard_map/pallas_call | solution.py:125
  65.8 0.0 copy-done
  65.8 0.0 copy-done.2
  65.8 1.0 multiply_reduce_fusion.3
  66.9 0.6 convert_element_type.10.vloc_ref
  67.5 0.6 select_maximum_fusion.1.part_ref
  68.1 34.8 %shard_map.69 = (f32[16,2048]{1,0:T(8,128)}, f32[8,128]{1,0:T(8,128)}) custom-call(bf16[16,2048]{1,0:T(8,128)(2,1)} %convert_element_type.10.vloc_ref, bf16[16,128,4224]{2,1,0:T(8,128)(2,1)} %shard_map.67.k_ref, f32[8,128]{1,0:T(8,128)} %select_maximum_fusion.1.part_ref), custom_call_target="tpu_custom_call" | custom-call | tf_op jit(solution)/shard_map/pallas_call | solution.py:358
  102.9 0.0 copy-start.1
  102.9 0.8 bitcast_divide_fusion.1
  103.6 1.8 %multiply_reduce_fusion.1 = (f32[16]{0:T(128)S(1)}, f32[16]{0:T(128)S(1)}, bf16[16,2048]{1,0:T(8,128)(2,1)}) fusion(f32[16,2048]{1,0:T(8,128)S(1)} %copy-done, f32[16,2048]{1,0:T(8,128)S(1)} %get-tuple-element.17, f32[16]{0:T(128)S(1)} %bitcast_divide_fusion.1, f32[16,2048]{1,0:T(8,128)} %get-tuple-element.8, f32[2048]{0:T(1024)S(1)} %copy-done.2), kind=kLoop, calls=%fused_computation.7 | loop fusion | flops 393184 | bytes 467136 | tf_op jit(solution)/shard_map/reduce_sum | solution.py:436
  105.4 0.6 select_maximum_fusion.part_ref
  106.0 22.9 %shard_map.70 = (f32[16,2048]{1,0:T(8,128)}, f32[8,128]{1,0:T(8,128)}) custom-call(bf16[16,2048]{1,0:T(8,128)(2,1)} %get-tuple-element.20.vloc_ref, bf16[16,128,4224]{2,1,0:T(8,128)(2,1)} %shard_map.67.k_ref, f32[8,128]{1,0:T(8,128)} %select_maximum_fusion.part_ref), custom_call_target="tpu_custom_call" | custom-call | tf_op jit(solution)/shard_map/pallas_call | solution.py:358
  128.9 0.8 fusion.1
  129.7 0.0 copy-done.1
  129.7 1.8 %multiply_subtract_fusion = (f32[16,2048]{1,0:T(8,128)}, f32[16,2048]{1,0:T(8,128)}, f32[16,2048]{1,0:T(8,128)}) fusion(f32[16,2048]{1,0:T(8,128)} %get-tuple-element.10, f32[16,2048]{1,0:T(8,128)S(1)} %copy-done.1, f32[16,2048]{1,0:T(8,128)S(1)} %get-tuple-element.17, f32[16]{0:T(128)S(1)} %get-tuple-element.16, f32[16]{0:T(128)S(1)} %get-tuple-element.15, ...), kind=kLoop, calls=%fused_computation.3 | loop fusion | flops 753664 | bytes 925888 | tf_op jit(solution)/shard_map/sub | solution.py:453
  (4 shorter events, 0.0 us)
Async XLA Ops:
  2.5 6.3 %collective-permute-start.1 = (bf16[48,2048]{1,0:T(8,128)(2,1)S(1)}, bf16[48,2048]{1,0:T(8,128)(2,1)S(1)}, u32[]{:S(2)}, u32[]{:S(2)}) collective-permute-start(bf16[48,2048]{1,0:T(8,128)(2,1)S(1)} %pad_maximum_fusion.1), channel_id=1, source_target_pairs={{4,0},{8,4},{12,8},{16,12},{20,16},{24,20},{28,24},{32,28},{36,32}... | collective-permute-start | bytes 589832 | tf_op jit(solution)/shard_map/ppermute | solution.py:403
  3.8 5.0 %collective-permute-start = (bf16[48,2048]{1,0:T(8,128)(2,1)S(1)}, bf16[48,2048]{1,0:T(8,128)(2,1)S(1)}, u32[]{:S(2)}, u32[]{:S(2)}) collective-permute-start(bf16[48,2048]{1,0:T(8,128)(2,1)S(1)} %pad_maximum_fusion.1), channel_id=1, source_target_pairs={{0,4},{4,8},{8,12},{12,16},{16,20},{20,24},{24,28},{28,32},{32,36}... | collective-permute-start | bytes 589832 | tf_op jit(solution)/shard_map/ppermute | solution.py:402
  11.2 54.6 %copy-start = (f32[16,2048]{1,0:T(8,128)S(1)}, f32[16,2048]{1,0:T(8,128)}, u32[]{:S(2)}) copy-start(f32[16,2048]{1,0:T(8,128)} %param.6) | copy-start | bytes 393220
  11.2 54.6 %copy-start.2 = (f32[2048]{0:T(1024)S(1)}, f32[2048]{0:T(1024)}, u32[]{:S(2)}) copy-start(f32[2048]{0:T(1024)} %param.5) | copy-start | bytes 24580
  102.9 26.8 %copy-start.1 = (f32[16,2048]{1,0:T(8,128)S(1)}, f32[16,2048]{1,0:T(8,128)}, u32[]{:S(2)}) copy-start(f32[16,2048]{1,0:T(8,128)} %get-tuple-element.8) | copy-start | bytes 393220

commit v19 on v12

--- a/solution.py
+++ b/solution.py
@@ -52,8 +52,11 @@
     left_m2 = left * jnp.asarray(-2.0, jnp.bfloat16)
     window = pwt_ref[:, pl.ds(pl.multiple_of(a * BLK, BLK), WIDE * BLK)]
     cross_ref[...] = jnp.dot(left_m2, window, preferred_element_type=jnp.float32)
-    window_f = window.astype(jnp.float32)
-    sqr_ref[...] = jnp.sum(window_f * window_f, axis=0, keepdims=True)
+
+    @pl.when(a == 0)
+    def _():
+        wide_f = pwt_ref[...].astype(jnp.float32)
+        sqr_ref[...] = jnp.sum(wide_f * wide_f, axis=0, keepdims=True)
 
     def body(o, carry):
         col = pl.multiple_of((a + o) * BLK, BLK)
@@ -69,7 +72,7 @@
 
         @pl.when(jnp.logical_and(live, jnp.logical_not(lower)))
         def _():
-            sq_right = sqr_ref[:, dst]
+            sq_right = sqr_ref[:, pl.ds(col, BLK)]
             value = profile_tile(sq_left, sq_right, cross_ref[:, dst])
             k_ref[0, :, dst] = value.astype(jnp.bfloat16)
 
@@ -112,7 +115,7 @@
             scratch_shapes=[
                 pltpu.VMEM((blocks, blocks, BLK, BLK), jnp.bfloat16),
                 pltpu.VMEM((BLK, WIDE * BLK), jnp.float32),
-                pltpu.VMEM((1, WIDE * BLK), jnp.float32),
+                pltpu.VMEM((1, wide_cols), jnp.float32),
             ],
         ),
         compiler_params=pltpu.CompilerParams(dimension_semantics=("arbitrary",)),

time: 131 us -> 132 us (level)
  Pallas kernels: 110 us -> 112 us
    pallas_call x2, Pallas kernels: 58.9 us -> 67.3 us  [apply_sum(): pl.pallas_call(functools.partial(apply_sum_kernel, inner, outer), out_sha...]
    pallas_call x1, Pallas kernels: 36.4 us -> 29.7 us  [build_k(): pl.pallas_call(build_kernel, out_shape=jax.ShapeDtypeStruct((blocks, BLK,...]
where the time goes in v19:
time: 132 us; the launch traced here: 131 us
  Pallas kernels  112 us (85%)
  other arithmetic  12.1 us (9%)
  starting transfers between devices  4.33 us (3%)
  local copies, waits for them, and re-layouts  1.97 us (1%)
    pallas_call x2, Pallas kernels, apply_sum(): pl.pallas_call(functools.partial(apply_sum_kernel, inner, outer), out_sha...  67.3 us
    pallas_call x1, Pallas kernels, build_k(): pl.pallas_call(build_kernel, out_shape=jax.ShapeDtypeStruct((blocks, BLK,...  29.7 us
    pallas_call x1, Pallas kernels, apply_k(): pl.pallas_call(apply_kernel, out_shape=jax.ShapeDtypeStruct((rows, blocks...  15.1 us
    ppermute x1, starting transfers between devices, per_device(): lax.ppermute(packed, 'pts', [(i, i + 1) for i in range(count - 1)])  3.04 us
    reduce_sum x2, other arithmetic, per_device(): jnp.sum(residual * residual, axis=1)  2.8 us
  transfers between devices with their start and end apart: 2, of which 0 were waited for; matrix products, arithmetic and copies ran while one was open for 1% of the time, Pallas kernels for 0%

profile of v19, /device:TPU:16, one launch (start us, length us, event | category | flops | bytes accessed | tf_op | source)
XLA Modules:
  0.0 131.3 jit_solution(2851765493121153532)
XLA Ops:
  0.6 0.9 convert_element_type.9
  1.5 0.9 pad_maximum_fusion.1
  2.5 1.3 collective-permute-start.1
  3.8 3.0 %collective-permute-start = (bf16[48,2048]{1,0:T(8,128)(2,1)S(1)}, bf16[48,2048]{1,0:T(8,128)(2,1)S(1)}, u32[]{:S(2)}, u32[]{:S(2)}) collective-permute-start(bf16[48,2048]{1,0:T(8,128)(2,1)S(1)} %pad_maximum_fusion.1), channel_id=1, source_target_pairs={{0,4},{4,8},{8,12},{12,16},{16,20},{20,24},{24,28},{28,32},{32,36}... | collective-permute-start | bytes 589832 | tf_op jit(solution)/shard_map/ppermute | solution.py:405
  6.8 1.9 %copy.7.pw_ref = bf16[2048,32]{1,0:T(8,128)(2,1)} copy(bf16[2048,32]{0,1:T(8,128)(2,1)} %param.4) | data formatting | bytes 262144 | tf_op args[0]
  8.7 0.0 collective-permute-done.1
  8.8 0.0 collective-permute-done
  8.8 0.7 pad_maximum_fusion.2.v_ref
  9.5 1.7 %pad_maximum_fusion.pwt_ref = bf16[32,6144]{1,0:T(8,128)(2,1)} fusion(bf16[32,2048]{1,0:T(8,128)(2,1)S(1)} %slice.41, bf16[32,2048]{1,0:T(8,128)(2,1)} %bitcast.29, bf16[32,2048]{1,0:T(8,128)(2,1)S(1)} %slice.40), kind=kLoop, calls=%fused_computation | loop fusion | flops 1179648 | bytes 786432 | tf_op jit(solution)/shard_map/concatenate | solution.py:407
  11.2 0.0 copy-start
  11.2 0.0 copy-start.2
  11.2 29.7 %shard_map.67.k_ref = bf16[16,128,4224]{2,1,0:T(8,128)(2,1)} custom-call(s32[16,33]{1,0:T(8,128)} %pat_ref.1, bf16[2048,32]{1,0:T(8,128)(2,1)} %copy.7.pw_ref, bf16[32,6144]{1,0:T(8,128)(2,1)} %pad_maximum_fusion.pwt_ref), custom_call_target="tpu_custom_call" | custom-call | tf_op jit(solution)/shard_map/pallas_call | solution.py:104
  40.9 15.1 %shard_map.68 = f32[16,2048]{1,0:T(8,128)} custom-call(bf16[16,6144]{1,0:T(8,128)(2,1)} %pad_maximum_fusion.2.v_ref, bf16[16,128,4224]{2,1,0:T(8,128)(2,1)} %shard_map.67.k_ref), custom_call_target="tpu_custom_call" | custom-call | tf_op jit(solution)/shard_map/pallas_call | solution.py:128
  56.0 0.0 copy-done
  56.0 0.0 copy-done.2
  56.0 1.0 multiply_reduce_fusion.3
  57.1 0.6 convert_element_type.10.vloc_ref
  57.7 0.6 select_maximum_fusion.1.part_ref
  58.3 44.4 %shard_map.69 = (f32[16,2048]{1,0:T(8,128)}, f32[8,128]{1,0:T(8,128)}) custom-call(bf16[16,2048]{1,0:T(8,128)(2,1)} %convert_element_type.10.vloc_ref, bf16[16,128,4224]{2,1,0:T(8,128)(2,1)} %shard_map.67.k_ref, f32[8,128]{1,0:T(8,128)} %select_maximum_fusion.1.part_ref), custom_call_target="tpu_custom_call" | custom-call | tf_op jit(solution)/shard_map/pallas_call | solution.py:361
  102.7 0.0 copy-start.1
  102.8 0.8 bitcast_divide_fusion.1
  103.5 1.8 %multiply_reduce_fusion.1 = (f32[16]{0:T(128)S(1)}, f32[16]{0:T(128)S(1)}, bf16[16,2048]{1,0:T(8,128)(2,1)}) fusion(f32[16,2048]{1,0:T(8,128)S(1)} %copy-done, f32[16,2048]{1,0:T(8,128)S(1)} %get-tuple-element.17, f32[16]{0:T(128)S(1)} %bitcast_divide_fusion.1, f32[16,2048]{1,0:T(8,128)} %get-tuple-element.8, f32[2048]{0:T(1024)S(1)} %copy-done.2), kind=kLoop, calls=%fused_computation.7 | loop fusion | flops 393184 | bytes 467136 | tf_op jit(solution)/shard_map/reduce_sum | solution.py:439
  105.3 0.6 select_maximum_fusion.part_ref
  105.9 22.8 %shard_map.70 = (f32[16,2048]{1,0:T(8,128)}, f32[8,128]{1,0:T(8,128)}) custom-call(bf16[16,2048]{1,0:T(8,128)(2,1)} %get-tuple-element.20.vloc_ref, bf16[16,128,4224]{2,1,0:T(8,128)(2,1)} %shard_map.67.k_ref, f32[8,128]{1,0:T(8,128)} %select_maximum_fusion.part_ref), custom_call_target="tpu_custom_call" | custom-call | tf_op jit(solution)/shard_map/pallas_call | solution.py:361
  128.7 0.8 fusion.1
  129.5 0.0 copy-done.1
  129.5 1.8 %multiply_subtract_fusion = (f32[16,2048]{1,0:T(8,128)}, f32[16,2048]{1,0:T(8,128)}, f32[16,2048]{1,0:T(8,128)}) fusion(f32[16,2048]{1,0:T(8,128)} %get-tuple-element.10, f32[16,2048]{1,0:T(8,128)S(1)} %copy-done.1, f32[16,2048]{1,0:T(8,128)S(1)} %get-tuple-element.17, f32[16]{0:T(128)S(1)} %get-tuple-element.16, f32[16]{0:T(128)S(1)} %get-tuple-element.15, ...), kind=kLoop, calls=%fused_computation.3 | loop fusion | flops 753664 | bytes 925888 | tf_op jit(solution)/shard_map/sub | solution.py:456
  (4 shorter events, 0.0 us)
Async XLA Ops:
  2.5 6.3 %collective-permute-start.1 = (bf16[48,2048]{1,0:T(8,128)(2,1)S(1)}, bf16[48,2048]{1,0:T(8,128)(2,1)S(1)}, u32[]{:S(2)}, u32[]{:S(2)}) collective-permute-start(bf16[48,2048]{1,0:T(8,128)(2,1)S(1)} %pad_maximum_fusion.1), channel_id=1, source_target_pairs={{4,0},{8,4},{12,8},{16,12},{20,16},{24,20},{28,24},{32,28},{36,32}... | collective-permute-start | bytes 589832 | tf_op jit(solution)/shard_map/ppermute | solution.py:406
  3.8 5.0 %collective-permute-start = (bf16[48,2048]{1,0:T(8,128)(2,1)S(1)}, bf16[48,2048]{1,0:T(8,128)(2,1)S(1)}, u32[]{:S(2)}, u32[]{:S(2)}) collective-permute-start(bf16[48,2048]{1,0:T(8,128)(2,1)S(1)} %pad_maximum_fusion.1), channel_id=1, source_target_pairs={{0,4},{4,8},{8,12},{12,16},{16,20},{20,24},{24,28},{28,32},{32,36}... | collective-permute-start | bytes 589832 | tf_op jit(solution)/shard_map/ppermute | solution.py:405
  11.2 44.8 %copy-start = (f32[16,2048]{1,0:T(8,128)S(1)}, f32[16,2048]{1,0:T(8,128)}, u32[]{:S(2)}) copy-start(f32[16,2048]{1,0:T(8,128)} %param.6) | copy-start | bytes 393220
  11.2 44.8 %copy-start.2 = (f32[2048]{0:T(1024)S(1)}, f32[2048]{0:T(1024)}, u32[]{:S(2)}) copy-start(f32[2048]{0:T(1024)} %param.5) | copy-start | bytes 24580
  102.7 26.7 %copy-start.1 = (f32[16,2048]{1,0:T(8,128)S(1)}, f32[16,2048]{1,0:T(8,128)}, u32[]{:S(2)}) copy-start(f32[16,2048]{1,0:T(8,128)} %get-tuple-element.8) | copy-start | bytes 393220
